TPU v7x, 512 devices: a whole 4x8x8 slice. The times are simulated.
512 devices in a mesh: group: 16 (over x, y_lo, core), shard: 32 (over y_hi, z).
Axes of the slice: x: 4, y: 8 (y_hi: 4, y_lo: 2; y = y_hi * 2 + y_lo), z: 8, core: 2. Of those that a mesh axis runs over, the one named last changes fastest.
Arguments:
- hidden: bfloat16 [8192, 8192], P('group', 'shard'), may hold values from -6 to 6
- w_x: bfloat16 [8192, 8192], P('group', 'shard'), may hold values from -0.0625 to 0.0625
- w_small: bfloat16 [8192, 2176], P('shard'), may hold values from -0.0625 to 0.0625
- conv_x: float32 [4, 8192], P(None, 'shard'), may hold values from -3 to 3
- conv_x_bias: float32 [8192], P('shard'), may hold values from -2 to 2
- conv_bc: float32 [4, 2048], replicated, may hold values from -1.5 to 1.5
- conv_bc_bias: float32 [2048], replicated, may hold values from -1 to 1
- rate: float32 [128], P('shard'), may hold values from 0.002 to 0.06
- dt_bias: float32 [128], P('shard'), may hold values from -2 to 0.5
- dskip: float32 [128], P('shard'), may hold values from 0.5 to 1.5
- old_state: float32 [64, 128, 64, 256], P('group', 'shard'), may hold values from -2 to 2
- x_tail: float32 [64, 3, 8192], P('group', None, 'shard'), may hold values from -6 to 6
- bc_tail: float32 [64, 3, 2048], P('group'), may hold values from -6 to 6
- req_count: int32 [16], replicated, may hold values from 1 to 4, as said below
- req_source: int32 [16, 4], replicated, may hold values from 0 to 63, as said below
- req_start: int32 [16, 4], replicated, may hold values from 0 to 512, as said below
Outputs:
- y_out: bfloat16 [8192, 8192], P('group', 'shard')
- new_state: float32 [64, 128, 64, 256], P('group', 'shard')
Inputs may be any that keep to these rules, and one draw needn't show every extreme that they name: `req_count`: some group serves 4 requests. `req_source`: every place is named by exactly one entry; the places named by one group lie in distinct groups, so one group takes at most one request from any one group's places. `req_start`: each group's row starts with 0 and rises strictly over its first req_count entries; later entries equal 512.
All inputs are finite; a program needn't handle non-finite values.
Results may differ from a plain program's by a relative error of at most 0.006.
Values may be sent and summed in bfloat16 or wider, within the bound.
No kernel may reach another device: no remote copies, remote signals or barrier semaphores. Data moves between devices by JAX's collectives and lax.ppermute only.
A program may use at most 128 MiB of HBM per device.

v0:
```python
import jax
import jax.numpy as jnp
from jax import lax
from jax.sharding import PartitionSpec as P

P_SIZE = 64
DSTATE = 256
KCONV = 4
HEAD_DEV = 4
NGRP = 4
REQ_GRP = 4


highest_mode = lax.Precision.HIGHEST


def token_requests(starts, length):
    positions = jnp.arange(length, dtype=jnp.int32)
    return jnp.sum((starts[None, :] <= positions[:, None]).astype(jnp.int32), axis=1) - 1


def causal_conv(signal, tail_vals, starts, req_tok, kernel, shift_bias):
    length = signal.shape[0]
    positions = jnp.arange(length, dtype=jnp.int32)
    own_start = jnp.take(starts, req_tok)
    tok_tail = jnp.take(tail_vals, req_tok, axis=0)
    values = signal.astype(jnp.float32)
    summed = kernel[KCONV - 1] * values
    tail_index = jnp.arange(KCONV - 1, dtype=jnp.int32)
    for lag_steps in range(1, KCONV):
        shifted = jnp.concatenate(
            [jnp.zeros((lag_steps, values.shape[1]), jnp.float32), values[:-lag_steps]], axis=0
        )
        before = own_start - (positions - lag_steps)
        select = (tail_index[None, :] == (KCONV - 1 - before)[:, None]).astype(jnp.float32)
        from_tail = jnp.sum(tok_tail * select[:, :, None], axis=1)
        summed = summed + kernel[KCONV - 1 - lag_steps] * jnp.where(
            (before > 0)[:, None], from_tail, shifted
        )
    return jax.nn.silu(summed + shift_bias)


def ssd_head(
    x_head,
    dt_head,
    rate_head,
    skip_head,
    h_head,
    scores,
    c_wide,
    b_wide,
    req_tok,
    starts,
    req_total,
):
    length = x_head.shape[0]
    positions = jnp.arange(length, dtype=jnp.int32)
    log_decay = -rate_head * dt_head
    cumul = jnp.cumsum(log_decay)
    cum_before = cumul - log_decay
    inside = (req_tok[:, None] == req_tok[None, :]) & (positions[:, None] >= positions[None, :])
    decay_mat = jnp.where(
        inside, jnp.exp(jnp.where(inside, cumul[:, None] - cumul[None, :], 0.0)), 0.0
    )
    mixing = (scores * decay_mat * dt_head[None, :]).astype(jnp.bfloat16)
    local_out = jnp.dot(mixing, x_head, preferred_element_type=jnp.float32)
    slot_ids = jnp.arange(REQ_GRP, dtype=jnp.int32)
    member = req_tok[None, :] == slot_ids[:, None]
    carried = jnp.einsum("tn,kpn->ktp", c_wide, h_head, precision=highest_mode)
    carry_tok = jnp.sum(jnp.where(member[:, :, None], carried, 0.0), axis=0)
    own_start = jnp.take(starts, req_tok)
    init_decay = jnp.exp(cumul - jnp.take(cum_before, own_start))
    x_wide = x_head.astype(jnp.float32)
    y_head = local_out + init_decay[:, None] * carry_tok + skip_head * x_wide
    next_start = jnp.concatenate([starts[1:], jnp.full((1,), length, jnp.int32)])
    last_index = jnp.minimum(next_start, length) - 1
    first_index = jnp.minimum(starts, length - 1)
    cum_end = jnp.take(cumul, last_index)
    weights = (
        jnp.where(member, jnp.exp(jnp.where(member, cum_end[:, None] - cumul[None, :], 0.0)), 0.0)
        * dt_head[None, :]
    )
    weighted = weights[:, :, None] * x_wide[None, :, :]
    gained = jnp.einsum("ktp,tn->kpn", weighted, b_wide, precision=highest_mode)
    total_decay = jnp.exp(cum_end - jnp.take(cum_before, first_index))
    new_head = total_decay[:, None, None] * h_head + gained
    return (y_head, jnp.where((slot_ids < req_total)[:, None, None], new_head, 0.0))


def project_rows(hidden, panel):
    return jnp.dot(
        lax.all_gather(hidden, "shard", axis=1, tiled=True),
        panel,
        preferred_element_type=jnp.float32,
    ).astype(jnp.bfloat16)


def fetch_states(old_state, x_tail, bc_tail, sources):
    every_slot = (
        lax.all_gather(old_state, "group", axis=0, tiled=True),
        lax.all_gather(x_tail, "group", axis=0, tiled=True),
        lax.all_gather(bc_tail, "group", axis=0, tiled=True),
    )
    return tuple((jnp.take(gathered, sources, axis=0) for gathered in every_slot))


def small_columns(hidden, w_small, bc_group, shard_index):
    bc_width = 2 * NGRP * DSTATE
    b_low = bc_group * DSTATE
    c_low = NGRP * DSTATE + bc_group * DSTATE
    partial_proj = jnp.dot(hidden, w_small, preferred_element_type=jnp.float32)
    small_proj = lax.psum(partial_proj, "shard")
    b_cols = lax.dynamic_slice_in_dim(small_proj, b_low, DSTATE, 1)
    c_cols = lax.dynamic_slice_in_dim(small_proj, c_low, DSTATE, 1)
    dt_cols = lax.dynamic_slice_in_dim(small_proj, bc_width + shard_index * HEAD_DEV, HEAD_DEV, 1)
    return (b_cols, c_cols, dt_cols)


def body(
    hidden,
    w_x,
    w_small,
    conv_x,
    conv_x_bias,
    conv_bc,
    conv_bc_bias,
    rate,
    dt_bias,
    dskip,
    old_state,
    x_tail,
    bc_tail,
    req_count,
    req_source,
    req_start,
):
    tokens_here = hidden.shape[0]
    heads_total = HEAD_DEV * lax.axis_size("shard")
    heads_grp = heads_total // NGRP
    group_index = lax.axis_index("group")
    shard_index = lax.axis_index("shard")
    bc_group = shard_index * HEAD_DEV // heads_grp
    sources = lax.dynamic_index_in_dim(req_source, group_index, 0, keepdims=False)
    starts = lax.dynamic_index_in_dim(req_start, group_index, 0, keepdims=False)
    req_total = lax.dynamic_index_in_dim(req_count, group_index, 0, keepdims=False)
    panel = lax.all_gather(w_x, "group", axis=0, tiled=True)
    x_pre = project_rows(hidden, panel)
    served = fetch_states(old_state, x_tail, bc_tail, sources)
    h_served, x_served, bc_served = served
    b_cols, c_cols, dt_cols = small_columns(hidden, w_small, bc_group, shard_index)
    b_low = bc_group * DSTATE
    c_low = NGRP * DSTATE + bc_group * DSTATE
    req_tok = token_requests(starts, tokens_here)
    x_conv = causal_conv(x_pre, x_served, starts, req_tok, conv_x, conv_x_bias).astype(jnp.bfloat16)
    b_conv = causal_conv(
        b_cols,
        lax.dynamic_slice_in_dim(bc_served, b_low, DSTATE, 2),
        starts,
        req_tok,
        lax.dynamic_slice_in_dim(conv_bc, b_low, DSTATE, 1),
        lax.dynamic_slice_in_dim(conv_bc_bias, b_low, DSTATE, 0),
    ).astype(jnp.bfloat16)
    c_conv = causal_conv(
        c_cols,
        lax.dynamic_slice_in_dim(bc_served, c_low, DSTATE, 2),
        starts,
        req_tok,
        lax.dynamic_slice_in_dim(conv_bc, c_low, DSTATE, 1),
        lax.dynamic_slice_in_dim(conv_bc_bias, c_low, DSTATE, 0),
    ).astype(jnp.bfloat16)
    dt_dev = jax.nn.softplus(dt_cols + dt_bias[None, :])
    scores = jnp.dot(c_conv, b_conv.T, preferred_element_type=jnp.float32)
    x_heads = x_conv.reshape(tokens_here, HEAD_DEV, P_SIZE)
    y_heads, new_heads = jax.vmap(
        ssd_head, in_axes=(1, 1, 0, 0, 1, None, None, None, None, None, None), out_axes=(1, 1)
    )(
        x_heads,
        dt_dev,
        rate,
        dskip,
        h_served,
        scores,
        c_conv.astype(jnp.float32),
        b_conv.astype(jnp.float32),
        req_tok,
        starts,
        req_total,
    )
    return (y_heads.reshape(tokens_here, HEAD_DEV * P_SIZE).astype(jnp.bfloat16), new_heads)


def solution(mesh):
    in_specs = (
        P("group", "shard"),
        P("group", "shard"),
        P("shard", None),
        P(None, "shard"),
        P("shard"),
        P(),
        P(),
        P("shard"),
        P("shard"),
        P("shard"),
        P("group", "shard", None, None),
        P("group", None, "shard"),
        P("group", None, None),
        P(),
        P(),
        P(),
    )
    out_specs = (P("group", "shard"), P("group", "shard", None, None))
    return jax.shard_map(body, mesh=mesh, in_specs=in_specs, out_specs=out_specs, check_vma=False)
```

profile of v0, /device:TPU:6, one launch (start us, length us, event | category | flops | bytes accessed | tf_op | source)
XLA Modules:
  0.0 546.5 jit_solution(8637857617810126497)
XLA Ops:
  8.1 1.7 copy.104
  9.8 3.8 fusion.49
  13.7 0.7 all-gather.9.cloned.1.call-update
  14.5 0.7 all-gather.7.cloned.1.call-update
  16.6 19.7 %all_gather.18 = f32[64,3,256]{2,1,0:T(4,128)S(1)} all-gather(f32[4,3,256]{2,1,0:T(4,128)S(1)} %copy.111), channel_id=1, replica_groups=mesh['group'=16,'shard'=32] {'group'}, dimensions={0}, use_global_device_ids=true | all-gather | bytes 208896 | tf_op jit(solution)/shard_map/all_gather | solution.py:101
  37.3 2.5 gather_fusion.6
  39.8 1.2 iota_compare_fusion.6
  41.0 0.8 fusion.45
  41.8 0.6 fusion.47
  42.4 2.5 compare_select_fusion.1
  45.2 0.9 fusion.44
  46.1 0.7 fusion.48
  46.8 2.5 compare_and_fusion.3
  49.3 0.6 fusion.46
  50.1 0.9 fusion.21
  51.0 0.9 fusion.24
  51.9 5.1 all-gather.5.cloned.1.call-done
  57.0 2.2 gather_fusion
  59.3 3.3 gather_fusion.5
  62.6 3.4 gather_fusion.4
  66.0 20.3 %multiply_reduce_fusion.2 = (f32[512,256]{1,0:T(8,128)}, f32[512,256]{1,0:T(8,128)}, f32[512,256]{1,0:T(8,128)S(1)}, f32[512,256]{1,0:T(8,128)}, f32[512,256]{1,...) fusion(f32[512,3,256]{2,1,0:T(4,128)S(1)} %gather_fusion.6, ...), kind=kLoop, calls=%fused_computation.15 | loop fusion | flops 7077888 | bytes 9456128 | tf_op jit(solution)/shard_map/reduce_sum | solution.py:36
  86.5 1.3 copy.113
  88.0 2.1 copy.107
  90.2 2.1 copy.106
  92.2 1.0 copy.105
  93.7 1.3 copy.108
  94.9 404.1 %all-reduce.11.cloned.1.call-done = f32[512,2176]{0,1:T(8,128)} async-done(((f32[512,2176]{0,1:T(8,128)}), f32[512,2176]{0,1:T(8,128)}) %all-reduce.11.cloned.1.call-update) | async-done | bytes 4456464 | tf_op jit(solution)/shard_map/psum | solution.py:112
  499.0 0.8 broadcast_multiply_fusion
  499.8 1.2 reduce-window.6
  501.7 1.7 gather_fusion.2
  503.3 1.1 copy.116
  505.8 0.7 copy.122
  506.5 1.3 constant_dynamic-slice_fusion.2
  507.8 1.4 constant_dynamic-slice_fusion.1
  509.2 1.3 constant_dynamic-slice_fusion
  510.6 1.8 multiply_convert_fusion.12
  512.5 1.8 multiply_convert_fusion.11
  514.3 0.7 copy-done.10
  515.0 1.3 fusion.50
  516.4 6.9 %fusion.17 = f32[512,256]{0,1:T(8,128)S(1)} fusion(bf16[512,8192]{1,0:T(8,128)(2,1)} %all-gather.7.cloned.1.call-done, bf16[8192,256]{1,0:T(8,128)(2,1)} %all-gather.9.cloned.1.call-done), kind=kOutput, calls=%fused_computation.32 | convolution fusion | flops 2147745792 | bytes 13107200 | tf_op jit(solution)/shard_map/dot_general | solution.py:91
  523.4 0.8 multiply_convert_fusion.10
  524.1 0.9 convert_bitcast_fusion
  525.0 6.5 %gather_fusion.3 = f32[4,4,64,256]{3,2,1,0:T(8,128)S(1)} fusion(f32[64,4,64,256]{3,2,1,0:T(8,128)} %all-gather.11.cloned.1.call-done, s32[1024]{0:T(1024)S(1)} %pad_clamp_fusion.4), kind=kCustom, calls=%fused_computation.8 | custom fusion | bytes 2097168 | tf_op jit(solution)/shard_map/jit(_take)/gather | solution.py:104
  531.5 1.1 select_reduce_fusion
  532.7 2.5 fusion.16
  535.2 1.9 copy.125
  537.1 1.2 fusion.10
  538.3 1.0 copy.126
  (112 shorter events, 6.1 us)
Async XLA Ops:
  8.0 1.8 copy-start
  8.0 48.9 %all-gather.5.cloned.1.call-start = ((), (), s32[]{:S(2)}) async-start(), calls=%async_computation.1 | async-start | bytes 2228224 | tf_op jit(solution)/shard_map/all_gather | solution.py:102
  9.8 489.2 %all-reduce.11.cloned.1.call-start = ((), (), s32[]{:S(2)}) async-start(), calls=%async_computation | async-start | bytes 8912896 | tf_op jit(solution)/shard_map/psum | solution.py:112
  13.6 2.1 copy-start.14
  13.6 2.2 copy-start.26
  13.6 2.2 copy-start.21
  13.7 2.4 copy-start.27
  13.7 23.3 %copy-start.22 = (s32[16,4]{0,1:T(4,128)S(1)}, s32[16,4]{0,1:T(4,128)}, u32[]{:S(2)}) copy-start(s32[16,4]{0,1:T(4,128)} %param.37) | copy-start | bytes 772
  13.7 502.6 %all-gather.9.cloned.1.call-start = ((), (), s32[]{:S(2)}) async-start(), calls=%async_computation.3 | async-start | bytes 4456448 | tf_op jit(solution)/shard_map/all_gather | solution.py:146
  14.4 501.9 %all-gather.7.cloned.1.call-start = ((), (), s32[]{:S(2)}) async-start(), calls=%async_computation.2 | async-start | bytes 8650752 | tf_op jit(solution)/shard_map/all_gather | solution.py:92
  15.2 509.8 %all-gather.11.cloned.1.call-start = ((), (), s32[]{:S(2)}) async-start(), calls=%async_computation.4 | async-start | bytes 17825792 | tf_op jit(solution)/shard_map/all_gather | solution.py:100
  37.3 21.9 %copy-start.19 = (pred[4]{0:T(512)(128)(4,1)}, pred[4]{0:T(512)(128)(4,1)S(1)}, u32[]{:S(2)}) copy-start(pred[4]{0:T(512)(128)(4,1)S(1)} %compare_and_fusion.4) | copy-start | bytes 16
  37.3 12.0 %copy-start.18 = (f32[4,256]{1,0:T(4,128)S(1)}, f32[4,256]{1,0:T(4,128)}, u32[]{:S(2)}) copy-start(f32[4,256]{1,0:T(4,128)} %param.25) | copy-start | bytes 12292
  86.3 1.5 copy-start.8
  86.5 5.8 %copy-start.7 = (f32[512,256]{1,0:T(8,128)S(1)}, f32[512,256]{1,0:T(8,128)}, u32[]{:S(2)}) copy-start(f32[512,256]{1,0:T(8,128)} %get-tuple-element.31) | copy-start | bytes 1572868
  87.8 5.4 copy-start.6
  88.0 5.4 copy-start.5
  92.2 406.8 %copy-start.25 = (f32[4]{0:T(128)S(1)}, f32[4]{0:T(128)}, u32[]{:S(2)}) copy-start(f32[4]{0:T(128)} %param.30) | copy-start | bytes 52
  507.8 2.8 copy-start.2
  507.8 2.8 copy-start.3
  507.8 2.8 copy-start.4
  514.3 0.7 copy-start.10
  516.3 7.0 %copy-start.15 = (f32[1,256]{1,0:T(1,128)S(1)}, f32[1,256]{1,0:T(1,128)}, u32[]{:S(2)}) copy-start(f32[1,256]{1,0:T(1,128)} %get-tuple-element.65) | copy-start | bytes 3076
  516.3 7.0 %copy-start.16 = (f32[1,256]{1,0:T(1,128)S(1)}, f32[1,256]{1,0:T(1,128)}, u32[]{:S(2)}) copy-start(f32[1,256]{1,0:T(1,128)} %get-tuple-element.66) | copy-start | bytes 3076
  516.3 7.0 %copy-start.17 = (f32[1,256]{1,0:T(1,128)S(1)}, f32[1,256]{1,0:T(1,128)}, u32[]{:S(2)}) copy-start(f32[1,256]{1,0:T(1,128)} %get-tuple-element.67) | copy-start | bytes 3076
  516.3 7.0 %copy-start.24 = (f32[256]{0:T(256)S(1)}, f32[256]{0:T(256)}, u32[]{:S(2)}) copy-start(f32[256]{0:T(256)} %param.26) | copy-start | bytes 3076
  524.1 7.4 %copy-start.20 = (pred[4]{0:T(512)(128)(4,1)S(1)}, pred[4]{0:T(512)(128)(4,1)}, u32[]{:S(2)}) copy-start(pred[4]{0:T(512)(128)(4,1)} %copy-done.19) | copy-start | bytes 16
  525.0 7.6 %copy-start.9 = (f32[512,512]{1,0:T(8,128)S(1)}, f32[512,512]{1,0:T(8,128)}, u32[]{:S(2)}) copy-start(f32[512,512]{1,0:T(8,128)} %fusion.50) | copy-start | bytes 3145732
  525.0 7.6 %copy-start.13 = (pred[512,512]{1,0:T(8,128)(4,1)S(1)}, pred[512,512]{1,0:T(8,128)(4,1)}, u32[]{:S(2)}) copy-start(pred[512,512]{1,0:T(8,128)(4,1)} %fusion.21) | copy-start | bytes 786436
  525.0 7.6 %copy-start.28 = (f32[4]{0:T(128)S(1)}, f32[4]{0:T(128)}, u32[]{:S(2)}) copy-start(f32[4]{0:T(128)} %param.31) | copy-start | bytes 52
  532.7 4.4 copy-start.11
  532.7 4.4 copy-start.12
  532.7 4.4 copy-start.23
  532.7 4.4 copy-start.29
  535.2 4.2 copy-start.1
Sparse Core Ops, SparseCore 0:
  11.5 45.3 all-gather.4
  59.1 53.1 all-gather.8
  115.4 151.0 all-gather.6
  268.4 111.2 all-gather.10
Sparse Core Ops, SparseCore 1:
  13.8 485.2 all-reduce.10
where the time goes:
time: 547 us; the launch traced here: 546 us
  waiting for transfers between devices  411 us (75%)
  local copies, waits for them, and re-layouts  46.1 us (8%)
  other arithmetic  36.6 us (7%)
  blocking collectives  19.7 us (4%)
  matrix products  16.8 us (3%)
  between operations  15.9 us (3%)
    psum x1, waiting for transfers between devices, small_columns(): small_proj = lax.psum(partial_proj, 'shard')  404 us
    reduce_sum x1, other arithmetic, causal_conv(): from_tail = jnp.sum(tok_tail * select[:, :, None], axis=1)  20.3 us
    all_gather x1, blocking collectives, fetch_states(): lax.all_gather(x_tail, 'group', axis=0, tiled=True)  19.7 us
  transfers between devices with their start and end apart: 5, of which 2 were waited for; matrix products, arithmetic and copies ran while one was open for 15% of the time, Pallas kernels for 0%

commit v1 on v0

v1 whole, which is shorter than its diff:
```python
import functools

import jax
import jax.numpy as jnp
from jax import lax
from jax.experimental import pallas as pl
from jax.experimental.pallas import tpu as pltpu
from jax.sharding import PartitionSpec as P


TOK = 512
STATES = 256
CHAN = 256
HEAD_DEV = 4
P_SIZE = 64
REQ = 4
GROUPS = 16
GROUP = ("x", "ylo", "core")
SHARD = ("yhi", "z")
PAY = 272
SMALL = 72


bf16 = jnp.bfloat16
f32 = jnp.float32
NT = (((1,), (1,)), ((), ()))
HIGH = lax.Precision.HIGHEST


def iota(shape, dim):
    return lax.broadcasted_iota(jnp.int32, shape, dim)


def call(kernel, scalars, operands, outs, flops=0, moved=0):
    smem = pl.BlockSpec(memory_space=pltpu.SMEM)
    whole = pl.BlockSpec(memory_space=pltpu.VMEM)
    return pl.pallas_call(
        kernel,
        in_specs=[smem] * len(scalars) + [whole] * len(operands),
        out_specs=jax.tree.map(lambda _: whole, outs),
        out_shape=outs,
        compiler_params=pltpu.CompilerParams(vmem_limit_bytes=48 << 20),
        cost_estimate=pl.CostEstimate(flops=flops, bytes_accessed=moved, transcendentals=0),
    )(*scalars, *operands)


def array(dtype, *shape):
    return jax.ShapeDtypeStruct(shape, dtype)


def bounds(starts_ref):
    starts = [starts_ref[k] for k in range(REQ)]
    ends = [jnp.minimum(s, TOK) for s in starts[1:]] + [jnp.int32(TOK)]
    return starts, ends


def own_start(tok, starts):
    out = jnp.zeros_like(tok)
    for k in range(1, REQ):
        out = jnp.where(tok >= starts[k], starts[k], out)
    return out


def by_request(tok, starts, values):
    out = values[0]
    for k in range(1, REQ):
        out = jnp.where(tok >= starts[k], values[k], out)
    return out


def sigmoid_gate(v):
    return v * jax.nn.sigmoid(v)


def tail_rows(tails, taps, rows, width):
    place = iota((rows, width), 0)
    out = jnp.zeros((rows, width), f32)
    for k in range(REQ):
        for d in range(3):
            term = jnp.zeros((1, width), f32)
            for j in range(d + 1, 4):
                term = term + taps[3 - j] * tails[k][3 + d - j]
            out = jnp.where(place == d * REQ + k, term, out)
    return out


def first_tokens(shape, tok_dim, starts, ends):
    tok = iota(shape, tok_dim)
    place = iota(shape, 1 - tok_dim)
    out = jnp.zeros(shape, f32)
    for k in range(REQ):
        for d in range(3):
            hit = (place == d * REQ + k) & (tok == starts[k] + d) & (tok < ends[k])
            out = jnp.where(hit, 1.0, out)
    return out


def pack_kernel(slot_ref, state_ref, tail_ref, out_ref):
    @pl.loop(0, GROUPS)
    def _(i):
        slot = slot_ref[i]
        out_ref[i, :STATES, :] = state_ref[slot].astype(bf16)
        out_ref[i, STATES:, :] = tail_ref[slot].astype(bf16)


def arrange_kernel(z_ref, own, r1, r2, r3, l1, l2, l3, far_a, far_b, hz_ref):
    def put(block, step, low, high):
        place = pl.multiple_of(lax.rem(z_ref[0] + step + 8, 8) * CHAN, CHAN)
        hz_ref[low:high, pl.ds(place, CHAN)] = block[...]

    for step, block in ((0, own), (-1, r1), (-2, r2), (-3, r3), (1, l1), (2, l2), (3, l3)):
        put(block, step, 0, TOK)
    put(far_a, 4, 0, TOK // 2)
    put(far_b, 4, TOK // 2, TOK)


def small_kernel(core_ref, hz_ref, wo_ref, wx_ref, out_ref):
    rows = hz_ref[...]
    for ref, place in ((wo_ref, core_ref[0]), (wx_ref, 1 - core_ref[0])):
        cols = jnp.concatenate([ref[s] for s in range(8)], axis=1)
        out_ref[place] = lax.dot_general(cols, rows, NT, preferred_element_type=f32)


def conv_kernel(starts_ref, src_ref, part_ref, served_ref, taps_ref, bc_ref, dt_ref):
    starts, ends = bounds(starts_ref)
    signal = part_ref[0] + part_ref[1] + part_ref[2] + part_ref[3]
    dt_ref[...] = signal[64:]
    signal = signal[:64]
    taps = [taps_ref[i : i + 1, :] for i in range(4)]
    tails = []
    for k in range(REQ):
        rows = served_ref[src_ref[k], STATES:, :].astype(f32)
        tails.append([rows[3 + i : 4 + i, :128] for i in range(3)])
    table = jnp.concatenate(
        [
            tail_rows(tails, taps, 16, 128),
            taps_ref[...],
            jnp.zeros((104, 128), f32),
        ],
        axis=0,
    ).T
    onehot = first_tokens((128, TOK), 1, starts, ends)
    corr = jnp.dot(table, onehot, precision=HIGH, preferred_element_type=f32)[:64]
    tok = iota((64, TOK), 1)
    begin = own_start(tok, starts)
    summed = table[:64, 19:20] * signal + corr + table[:64, 20:21]
    for j in range(1, 4):
        moved = jnp.where(tok - j >= begin, pltpu.roll(signal, j, 1), 0.0)
        summed = summed + table[:64, 19 - j : 20 - j] * moved
    bc_ref[...] = sigmoid_gate(summed).astype(bf16)


def product(hz_ref, w_ref):
    return jnp.dot(hz_ref[...], w_ref[...], preferred_element_type=f32)


def far_kernel(index_ref, hz_ref, w_ref, low_ref, high_ref):
    total = product(hz_ref, w_ref).astype(bf16)
    low_ref[...] = total[: TOK // 2]
    high_ref[...] = total[TOK // 2 :]


def own_kernel(index_ref, hz_ref, w_ref, out_ref):
    out_ref[...] = product(hz_ref, w_ref)


def near_kernel(low, index_ref, hz_ref, w_ref, add_ref, out_ref):
    total = product(hz_ref, w_ref)
    out_ref[...] = total.astype(bf16)
    rows = slice(low, low + TOK // 2)
    out_ref[rows, :] = (total[rows] + add_ref[...].astype(f32)).astype(bf16)


def partial(kernel, index, operands, outs):
    whole = pl.BlockSpec(memory_space=pltpu.VMEM)
    block = pl.BlockSpec((None, 8 * CHAN, CHAN), lambda i, b: (b[0], 0, 0))
    return pl.pallas_call(
        kernel,
        grid_spec=pltpu.PrefetchScalarGridSpec(
            num_scalar_prefetch=1,
            grid=(1,),
            in_specs=[whole, block] + [whole] * (len(operands) - 2),
            out_specs=jax.tree.map(lambda _: whole, outs),
        ),
        out_shape=outs,
        compiler_params=pltpu.CompilerParams(vmem_limit_bytes=48 << 20),
        cost_estimate=pl.CostEstimate(
            flops=2 * 512 * 2048 * 256, bytes_accessed=3 << 20, transcendentals=0
        ),
    )(index, *operands)


def mixing_kernel(
    starts_ref, src_ref, rate_ref, bias_ref, bc_ref, dt_ref, served_ref, par_ref,
    mix_ref, carry_ref, cols_ref, decay_ref, b_ref, tail_ref,
):
    starts, ends = bounds(starts_ref)
    taps = [par_ref[i : i + 1, :] for i in range(4)]
    tails = []
    for k in range(REQ):
        rows = served_ref[src_ref[k], STATES:, :].astype(f32)
        tails.append([rows[i : i + 1, :] for i in range(3)])
    table = tail_rows(tails, taps, 128, CHAN)
    onehot = first_tokens((TOK, 128), 0, starts, ends)
    tail_ref[...] = jnp.dot(onehot, table, precision=HIGH, preferred_element_type=f32)
    b_rows = jnp.concatenate([bc_ref[s, 0:32, :] for s in range(8)], axis=0)
    c_rows = jnp.concatenate([bc_ref[s, 32:64, :] for s in range(8)], axis=0)
    b_ref[...] = b_rows
    c_cols = c_rows.astype(f32).T.astype(bf16)
    scores = jnp.dot(c_cols, b_rows, preferred_element_type=f32)

    row = iota((8, TOK), 0)
    tok = iota((8, TOK), 1)
    rate = jnp.zeros((8, TOK), f32)
    bias = jnp.zeros((8, TOK), f32)
    for h in range(HEAD_DEV):
        rate = jnp.where(row == h, rate_ref[h], rate)
        bias = jnp.where(row == h, bias_ref[h], bias)
    raw = dt_ref[0:8, :] + bias
    dt = jnp.maximum(raw, 0.0) + jnp.log1p(jnp.exp(-jnp.abs(raw)))
    decay = -rate * dt
    cum = decay
    step = 1
    while step < TOK:
        cum = cum + jnp.where(tok >= step, pltpu.roll(cum, step, 1), 0.0)
        step *= 2
    before = cum - decay
    at_start, at_end = [], []
    for k in range(REQ):
        first = jnp.minimum(starts[k], TOK - 1)
        at_start.append(jnp.sum(jnp.where(tok == first, before, 0.0), axis=1, keepdims=True))
        at_end.append(jnp.sum(jnp.where(tok == ends[k] - 1, cum, 0.0), axis=1, keepdims=True))
        decay_ref[k] = jnp.broadcast_to(jnp.exp(at_end[k] - at_start[k]), (8, 128))
    full_start = [jnp.broadcast_to(v, (8, TOK)) for v in at_start]
    full_end = [jnp.broadcast_to(v, (8, TOK)) for v in at_end]
    carried_decay = jnp.exp(cum - by_request(tok, starts, full_start))
    weight = jnp.exp(by_request(tok, starts, full_end) - cum) * dt
    cols = jnp.concatenate([cum, carried_decay, weight, jnp.zeros((104, TOK), f32)], axis=0).T
    cols_ref[...] = cols

    tok_c = iota((TOK, CHAN), 0)
    lane = iota((TOK, CHAN), 1)
    carry = jnp.zeros((TOK, CHAN), f32)
    for k in range(REQ):
        old = served_ref[src_ref[k], :CHAN, :]
        part = lax.dot_general(c_cols, old, NT, preferred_element_type=f32)
        carry = jnp.where((tok_c >= starts[k]) & (tok_c < ends[k]), part, carry)
    scale = jnp.zeros((TOK, CHAN), f32)
    for h in range(HEAD_DEV):
        scale = jnp.where(lane >= h * P_SIZE, cols[:, 8 + h : 9 + h], scale)
    carry_ref[...] = carry * scale

    for b in range(4):
        low, width = b * 128, (b + 1) * 128
        tok_t = iota((128, width), 0) + low
        tok_s = iota((128, width), 1)
        inside = (tok_s <= tok_t) & (tok_s >= own_start(tok_t, starts))
        block = scores[low : low + 128, :width]
        for h in range(HEAD_DEV):
            gap = cols[low : low + 128, h : h + 1] - cum[h : h + 1, :width]
            grown = jnp.exp(jnp.where(inside, gap, 0.0))
            value = jnp.where(inside, block * grown * dt[h : h + 1, :width], 0.0)
            mix_ref[h, low : low + 128, 0:width] = value.astype(bf16)


def output_kernel(
    starts_ref, src_ref, count_ref, x0, x1, x2, served_ref, par_ref,
    mix_ref, carry_ref, cols_ref, decay_ref, b_ref, tail_ref, y_ref, state_ref,
):
    starts, ends = bounds(starts_ref)
    count = count_ref[0]
    signal = x0[...] + x1[...].astype(f32) + x2[...].astype(f32)
    taps = [par_ref[i : i + 1, :] for i in range(4)]
    summed = tail_ref[...]
    tok = iota((TOK, CHAN), 0)
    lane = iota((TOK, CHAN), 1)
    begin = own_start(tok, starts)
    summed = summed + taps[3] * signal + par_ref[4:5, :]
    for j in range(1, 4):
        moved = jnp.where(tok - j >= begin, pltpu.roll(signal, j, 0), 0.0)
        summed = summed + taps[3 - j] * moved
    x_low = sigmoid_gate(summed).astype(bf16)
    x_wide = x_low.astype(f32)
    base = carry_ref[...] + par_ref[5:6, :] * x_wide
    for b in range(4):
        low, width = b * 128, (b + 1) * 128
        total = base[low : low + 128]
        for h in range(HEAD_DEV):
            mine = (lane[:width] >= h * P_SIZE) & (lane[:width] < (h + 1) * P_SIZE)
            x_head = jnp.where(mine, x_wide[:width], 0.0).astype(bf16)
            total = total + jnp.dot(
                mix_ref[h, low : low + 128, 0:width], x_head, preferred_element_type=f32
            )
        y_ref[low : low + 128, :] = total.astype(bf16)

    weight = jnp.zeros((TOK, CHAN), f32)
    for h in range(HEAD_DEV):
        weight = jnp.where(lane >= h * P_SIZE, cols_ref[:, 16 + h : 17 + h], weight)
    weighted = (x_wide * weight).T
    high = weighted.astype(bf16).astype(f32)
    rest = weighted - high
    tok_r = iota((CHAN, TOK), 1)
    b_rows = b_ref[...]
    for k in range(REQ):
        member = (tok_r >= starts[k]) & (tok_r < ends[k])
        gained = lax.dot_general(
            jnp.where(member, high, 0.0).astype(bf16), b_rows, NT, preferred_element_type=f32
        ) + lax.dot_general(
            jnp.where(member, rest, 0.0).astype(bf16), b_rows, NT, preferred_element_type=f32
        )
        for h in range(HEAD_DEV):
            lo, hi = h * P_SIZE, (h + 1) * P_SIZE
            old = served_ref[src_ref[k], lo:hi, :].astype(f32)
            new = decay_ref[k, h : h + 1, 0:1] * old + gained[lo:hi]
            state_ref[k, lo:hi, :] = jnp.where(k < count, new, 0.0)


def layer(
    hidden, w_x, w_small, conv_x, conv_x_bias, conv_bc, conv_bc_bias, rate, dt_bias, dskip,
    old_state, x_tail, bc_tail, req_count, req_source, req_start,
):
    group = lax.axis_index(GROUP)
    core = lax.axis_index("core")
    yhi = lax.axis_index("yhi")
    z = lax.axis_index("z")
    mine = lax.dynamic_index_in_dim(req_source, group, 0, keepdims=False)
    src = mine // REQ
    starts = lax.dynamic_index_in_dim(req_start, group, 0, keepdims=False)
    count = lax.dynamic_slice_in_dim(req_count, group, 1, 0)

    swap = [(a * 4 + b, b * 4 + a) for a in range(4) for b in range(4)]
    w_swapped = lax.ppermute(w_x, ("x", "yhi"), swap)
    w_all = lax.all_gather(w_swapped, GROUP, axis=0, tiled=False)

    up = [(i, (i + 1) % 8) for i in range(8)]
    down = [(i, (i - 1) % 8) for i in range(8)]
    blocks = [hidden]
    for ring in (up, down):
        block = hidden
        for _ in range(3):
            block = lax.ppermute(block, "z", ring)
            blocks.append(block)
    half = TOK // 2
    blocks.append(lax.ppermute(blocks[3][:half], "z", up))
    blocks.append(lax.ppermute(blocks[6][half:], "z", down))

    w_t = w_small.T
    w_b = w_t[:1024].reshape(4, 8, 32, 256)
    w_c = w_t[1024:2048].reshape(4, 8, 32, 256)
    w_d = jnp.pad(w_t[2048:].reshape(4, 8, 4, 256), ((0, 0), (0, 0), (0, SMALL - 68), (0, 0)))
    w_cols = jnp.concatenate([w_b, w_c, w_d], axis=2)
    w_cols = lax.dynamic_slice_in_dim(w_cols, core * 2, 2, 0)
    w_cols = w_cols.transpose(1, 0, 2, 3).reshape(8, 2 * SMALL, 256)
    w_cols = lax.all_to_all(w_cols, "z", 0, 0, tiled=True)
    w_other = lax.ppermute(w_cols, "core", [(0, 1), (1, 0)])

    owner, slot = req_source // REQ, req_source % REQ
    slots = jnp.sum(jnp.where(owner == group, slot, 0), axis=1).astype(jnp.int32)
    bc_mine = lax.dynamic_slice(
        bc_tail.reshape(REQ, 3, 2, 4, 8, 32), (0, 0, 0, yhi, z, 0), (REQ, 3, 2, 1, 1, 32)
    ).reshape(REQ, 3, 64)
    tails = jnp.concatenate(
        [x_tail, jnp.pad(bc_mine, ((0, 0), (0, 0), (0, 192))), jnp.zeros((REQ, 10, 256), f32)],
        axis=1,
    )
    packed = call(
        pack_kernel,
        (slots,),
        (old_state.reshape(REQ, 256, STATES), tails),
        array(bf16, GROUPS, PAY, 256),
        moved=7 << 20,
    )
    served = lax.all_to_all(packed, GROUP, 0, 0, tiled=True)

    hz = call(
        arrange_kernel,
        (z.astype(jnp.int32).reshape(1),),
        blocks,
        array(bf16, TOK, 8 * CHAN),
        moved=4 << 20,
    )
    part_small = call(
        small_kernel,
        (core.astype(jnp.int32).reshape(1),),
        (hz, w_cols, w_other),
        array(f32, 2, 2 * SMALL, TOK),
        flops=2 * 288 * 2048 * 512,
        moved=4 << 20,
    )
    part_small = lax.all_to_all(part_small.reshape(4, SMALL, TOK), "yhi", 0, 0, tiled=True)

    taps_bc = lax.dynamic_slice(
        conv_bc.reshape(4, 2, 4, 8, 32), (0, 0, yhi, z, 0), (4, 2, 1, 1, 32)
    ).reshape(4, 64)
    bias_bc = lax.dynamic_slice(
        conv_bc_bias.reshape(2, 4, 8, 32), (0, yhi, z, 0), (2, 1, 1, 32)
    ).reshape(1, 64)
    taps_bc = jnp.pad(jnp.concatenate([taps_bc, bias_bc], axis=0), ((0, 3), (0, 64)))
    bc_own, dt_raw = call(
        conv_kernel,
        (starts, src),
        (part_small, served, taps_bc),
        (array(bf16, 64, TOK), array(f32, SMALL - 64, TOK)),
        flops=2 * 6 * 128 * 128 * 512,
        moved=1 << 20,
    )
    bc_all = lax.all_to_all(
        jnp.broadcast_to(bc_own[None], (8, 64, TOK)), "z", 0, 0, tiled=True
    )

    w_view = w_all.reshape(4, 8 * CHAN, CHAN)
    index = [((yhi + r) % 4).astype(jnp.int32).reshape(1) for r in range(4)]
    ahead = [(i, (i + 1) % 4) for i in range(4)]
    back = [(i, (i - 1) % 4) for i in range(4)]
    low, high = partial(far_kernel, index[2], (hz, w_view), (array(bf16, half, CHAN),) * 2)
    low = lax.ppermute(low, "yhi", ahead)
    high = lax.ppermute(high, "yhi", back)
    x0 = partial(own_kernel, index[0], (hz, w_view), array(f32, TOK, CHAN))
    x1 = partial(
        functools.partial(near_kernel, 0),
        index[1], (hz, w_view, low), array(bf16, TOK, CHAN),
    )
    x1 = lax.ppermute(x1, "yhi", ahead)
    x2 = partial(
        functools.partial(near_kernel, half),
        index[3], (hz, w_view, high), array(bf16, TOK, CHAN),
    )
    x2 = lax.ppermute(x2, "yhi", back)

    params = jnp.concatenate(
        [conv_x, conv_x_bias[None], jnp.repeat(dskip, P_SIZE)[None], jnp.zeros((2, CHAN), f32)],
        axis=0,
    )
    made = call(
        mixing_kernel,
        (starts, src, rate, dt_bias),
        (bc_all, dt_raw, served, params),
        (
            array(bf16, HEAD_DEV, TOK, TOK),
            array(f32, TOK, CHAN),
            array(f32, TOK, 128),
            array(f32, REQ, 8, 128),
            array(bf16, STATES, TOK),
            array(f32, TOK, CHAN),
        ),
        flops=2 * 8 * 512 * 256 * 256,
        moved=12 << 20,
    )
    y, state = call(
        output_kernel,
        (starts, src, count),
        (x0, x1, x2, served, params, *made),
        (array(bf16, TOK, CHAN), array(f32, REQ, 256, STATES)),
        flops=2 * 20 * 512 * 256 * 256,
        moved=6 << 20,
    )
    return y, state.reshape(REQ, HEAD_DEV, P_SIZE, STATES)


def solution(mesh):
    fine = jax.sharding.Mesh(mesh.devices.reshape(4, 2, 2, 4, 8), ("x", "ylo", "core", "yhi", "z"))
    g, s = GROUP, SHARD
    in_specs = (
        P(g, s),
        P(g, s),
        P(s, None),
        P(None, s),
        P(s),
        P(),
        P(),
        P(s),
        P(s),
        P(s),
        P(g, s, None, None),
        P(g, None, s),
        P(g, None, None),
        P(),
        P(),
        P(),
    )
    out_specs = (P(g, s), P(g, s, None, None))
    return jax.shard_map(layer, mesh=fine, in_specs=in_specs, out_specs=out_specs, check_vma=False)
```

time: 547 us -> 224 us (0.41)
  the two profiles are of different devices: /device:TPU:6 before, /device:TPU:2 now
where the time goes in v1:
time: 224 us; the launch traced here: 222 us
  waiting for transfers between devices  87.5 us (39%)
  starting transfers between devices  77.9 us (35%)
  Pallas kernels  25 us (11%)
  local copies, waits for them, and re-layouts  17.3 us (8%)
  between operations  14.5 us (6%)
    all_to_all x1, waiting for transfers between devices, layer(): served = lax.all_to_all(packed, GROUP, 0, 0, tiled=True)  26.9 us
    ppermute x6, starting transfers between devices, layer(): block = lax.ppermute(block, 'z', ring)  21.5 us
    ppermute x1, waiting for transfers between devices, layer(): w_swapped = lax.ppermute(w_x, ('x', 'yhi'), swap)  18.7 us
    ppermute x6, waiting for transfers between devices, layer(): block = lax.ppermute(block, 'z', ring)  18.3 us
    pallas_call x6, Pallas kernels, call(): pl.pallas_call(kernel, in_specs=[smem] * len(scalars) + [whole] * len(ope...  15.9 us
    unnamed x58, local copies, waits for them, and re-layouts  13.5 us
    all_to_all x1, waiting for transfers between devices, layer(): lax.all_to_all(part_small.reshape(4, SMALL, TOK), 'yhi', 0, 0, tiled=True)  10.8 us
    all_to_all x1, starting transfers between devices, layer(): w_cols = lax.all_to_all(w_cols, 'z', 0, 0, tiled=True)  10.3 us
  transfers between devices with their start and end apart: 19, of which 10 were waited for; matrix products, arithmetic and copies ran while one was open for 3% of the time, Pallas kernels for 9%

profile of v1, /device:TPU:2, one launch (start us, length us, event | category | flops | bytes accessed | tf_op | source)
XLA Modules:
  0.0 222.4 jit_solution(15872497692511850670)
XLA Ops:
  7.2 4.5 %collective-permute-start.8 = (bf16[512,256]{1,0:T(8,128)(2,1)}, bf16[512,256]{1,0:T(8,128)(2,1)S(1)}, u32[]{:S(2)}, u32[]{:S(2)}) collective-permute-start(bf16[512,256]{1,0:T(8,128)(2,1)} %param.17), channel_id=1, source_target_pairs={{0,0},{8,128},{16,256},{24,384},{128,8},{136,136},{144,264},{152,3... | collective-permute-start | bytes 786440 | tf_op jit(solution)/shard_map/ppermute | solution.py:332
  11.7 18.7 %collective-permute-done.8 = bf16[512,256]{1,0:T(8,128)(2,1)S(1)} collective-permute-done((bf16[512,256]{1,0:T(8,128)(2,1)}, bf16[512,256]{1,0:T(8,128)(2,1)S(1)}, u32[]{:S(2)}, u32[]{:S(2)}) %collective-permute-start.8) | collective-permute-done | bytes 262176 | tf_op jit(solution)/shard_map/ppermute | solution.py:332
  31.1 1.7 copy.27
  33.0 0.9 copy.28
  33.9 10.3 %all-to-all-start.1 = ((bf16[8,144,256]{2,1,0:T(8,128)(2,1)}), bf16[8,144,256]{2,1,0:T(8,128)(2,1)S(1)}, u32[]{:S(2)}, u32[]{:S(2)}) async-start(bf16[8,144,256]{2,1,0:T(8,128)(2,1)} %bitcast.13), calls=%async_computation.1 | async-start | bytes 1179648 | tf_op jit(solution)/shard_map/all_to_all | solution.py:354
  44.2 3.9 %collective-permute-start = (bf16[512,256]{1,0:T(8,128)(2,1)S(1)}, bf16[512,256]{1,0:T(8,128)(2,1)S(1)}, u32[]{:S(2)}, u32[]{:S(2)}) collective-permute-start(bf16[512,256]{1,0:T(8,128)(2,1)S(1)} %copy-done.3), channel_id=1, source_target_pairs={{0,1},{1,2},{2,3},{3,4},{4,5},{5,6},{6,7},{7,0},{8,9},{9,10},{10,1... | collective-permute-start | bytes 786440 | tf_op jit(solution)/shard_map/ppermute | solution.py:341
  48.1 3.1 %collective-permute-start.3 = (bf16[512,256]{1,0:T(8,128)(2,1)S(1)}, bf16[512,256]{1,0:T(8,128)(2,1)S(1)}, u32[]{:S(2)}, u32[]{:S(2)}) collective-permute-start(bf16[512,256]{1,0:T(8,128)(2,1)S(1)} %copy-done.3), channel_id=1, source_target_pairs={{0,7},{1,0},{2,1},{3,2},{4,3},{5,4},{6,5},{7,6},{8,15},{9,8},{10,9... | collective-permute-start | bytes 786440 | tf_op jit(solution)/shard_map/ppermute | solution.py:341
  51.2 13.9 %collective-permute-done.r1 = bf16[512,256]{1,0:T(8,128)(2,1)S(1)} collective-permute-done((bf16[512,256]{1,0:T(8,128)(2,1)S(1)}, bf16[512,256]{1,0:T(8,128)(2,1)S(1)}, u32[]{:S(2)}, u32[]{:S(2)}) %collective-permute-start) | collective-permute-done | bytes 262176 | tf_op jit(solution)/shard_map/ppermute | solution.py:341
  65.2 1.9 collective-permute-start.1
  67.8 5.1 %collective-permute-start.4 = (bf16[512,256]{1,0:T(8,128)(2,1)S(1)}, bf16[512,256]{1,0:T(8,128)(2,1)S(1)}, u32[]{:S(2)}, u32[]{:S(2)}) collective-permute-start(bf16[512,256]{1,0:T(8,128)(2,1)S(1)} %collective-permute-done.3.l1), channel_id=1, source_target_pairs={{0,7},{1,0},{2,1},{3,2},{4,3},{5,4},{6,5},{7,6},{8,15},{9,8},{10,9... | collective-permute-start | bytes 786440 | tf_op jit(solution)/shard_map/ppermute | solution.py:341
  72.9 0.7 copy-done.6
  73.7 1.9 collective-permute-start.13
  75.6 1.9 collective-permute-start.2
  77.6 5.5 %collective-permute-start.5 = (bf16[512,256]{1,0:T(8,128)(2,1)S(1)}, bf16[512,256]{1,0:T(8,128)(2,1)S(1)}, u32[]{:S(2)}, u32[]{:S(2)}) collective-permute-start(bf16[512,256]{1,0:T(8,128)(2,1)S(1)} %collective-permute-done.4.l2), channel_id=1, source_target_pairs={{0,7},{1,0},{2,1},{3,2},{4,3},{5,4},{6,5},{7,6},{8,15},{9,8},{10,9... | collective-permute-start | bytes 786440 | tf_op jit(solution)/shard_map/ppermute | solution.py:341
  83.1 4.4 %collective-permute-done.2.r3 = bf16[512,256]{1,0:T(8,128)(2,1)S(1)} collective-permute-done((bf16[512,256]{1,0:T(8,128)(2,1)S(1)}, bf16[512,256]{1,0:T(8,128)(2,1)S(1)}, u32[]{:S(2)}, u32[]{:S(2)}) %collective-permute-start.2) | collective-permute-done | bytes 262176 | tf_op jit(solution)/shard_map/ppermute | solution.py:341
  87.4 1.9 collective-permute-start.6
  89.4 5.1 %collective-permute-start.7 = (bf16[256,256]{1,0:T(8,128)(2,1)S(1)}, bf16[256,256]{1,0:T(8,128)(2,1)S(1)}, u32[]{:S(2)}, u32[]{:S(2)}) collective-permute-start(bf16[256,256]{1,0:T(8,128)(2,1)S(1)} %slice.21), channel_id=1, source_target_pairs={{0,7},{1,0},{2,1},{3,2},{4,3},{5,4},{6,5},{7,6},{8,15},{9,8},{10,9... | collective-permute-start | bytes 393224 | tf_op jit(solution)/shard_map/ppermute | solution.py:345
  94.5 1.0 collective-permute-done.6.far_a
  96.3 0.8 collective-permute-done.7.far_b
  97.7 0.9 copy-done.5
  98.6 0.9 copy-done.7
  99.6 0.9 copy-done.9
  100.5 0.9 copy-done.11
  101.5 0.9 copy-done.13
  102.4 0.9 copy-done.15
  103.6 3.4 %shard_map.173 = f32[2,144,512]{2,1,0:T(8,128)} custom-call(s32[1]{0:T(128)} %bitcast.8.core_ref, bf16[512,2048]{1,0:T(8,128)(2,1)S(1)} %shard_map.167.hz_ref, bf16[8,144,256]{2,1,0:T(8,128)(2,1)S(1)} %all-to-all-done.1.wo_ref, bf16[8,144,256]{2,1,0:T(8,128)(2,1)} %collective-permute-done.13.wx_ref), custom_call_target="tpu_custom_call" | custom-call | flops 603979776 | bytes 4194304 | tf_op jit(solution)/shard_map/pallas_call | solution.py:37
  107.0 4.3 %all-to-all-start.2 = ((f32[4,72,512]{2,1,0:T(8,128)}), f32[4,72,512]{2,1,0:T(8,128)S(1)}, u32[]{:S(2)}, u32[]{:S(2)}) async-start(f32[4,72,512]{2,1,0:T(8,128)} %bitcast.14), calls=%async_computation.2 | async-start | bytes 1179648 | tf_op jit(solution)/shard_map/all_to_all | solution.py:390
  111.8 1.2 copy-done.2
  113.0 0.9 shard_map.172
  113.9 1.4 copy-done.1
  115.3 10.8 %all-to-all-done.2.part_ref = f32[4,72,512]{2,1,0:T(8,128)S(1)} async-done(((f32[4,72,512]{2,1,0:T(8,128)}), f32[4,72,512]{2,1,0:T(8,128)S(1)}, u32[]{:S(2)}, u32[]{:S(2)}) %all-to-all-start.2) | async-done | bytes 589856 | tf_op jit(solution)/shard_map/all_to_all | solution.py:390
  126.1 9.3 %all-to-all-start = ((bf16[16,272,256]{2,1,0:T(8,128)(2,1)}), bf16[16,272,256]{2,1,0:T(8,128)(2,1)}, u32[]{:S(2)}, u32[]{:S(2)}) async-start(bf16[16,272,256]{2,1,0:T(8,128)(2,1)} %copy-done.1), calls=%async_computation | async-start | bytes 4456448 | tf_op jit(solution)/shard_map/all_to_all | solution.py:373
  136.3 26.9 %all-to-all-done.served_ref = bf16[16,272,256]{2,1,0:T(8,128)(2,1)} async-done(((bf16[16,272,256]{2,1,0:T(8,128)(2,1)}), bf16[16,272,256]{2,1,0:T(8,128)(2,1)}, u32[]{:S(2)}, u32[]{:S(2)}) %all-to-all-start) | async-done | bytes 2228256 | tf_op jit(solution)/shard_map/all_to_all | solution.py:373
  163.2 2.1 shard_map.174
  165.3 0.8 broadcast_in_dim.24
  166.1 5.5 %all-to-all-start.3 = ((bf16[8,64,512]{2,1,0:T(8,128)(2,1)}), bf16[8,64,512]{2,1,0:T(8,128)(2,1)S(1)}, u32[]{:S(2)}, u32[]{:S(2)}) async-start(bf16[8,64,512]{2,1,0:T(8,128)(2,1)} %broadcast_in_dim.24), calls=%async_computation.3 | async-start | bytes 1048576 | tf_op jit(solution)/shard_map/all_to_all | solution.py:407
  171.7 2.5 %shard_map.169 = (bf16[256,256]{1,0:T(8,128)(2,1)}, bf16[256,256]{1,0:T(8,128)(2,1)S(1)}) custom-call(s32[1]{0:T(128)} %bitcast.4.index_ref, bf16[512,2048]{1,0:T(8,128)(2,1)S(1)} %shard_map.167.hz_ref, bf16[4,2048,256]{2,1,0:T(8,128)(2,1)} %bitcast.26), custom_call_target="tpu_custom_call" | custom-call | flops 536870912 | bytes 3145728 | tf_op jit(solution)/shard_map/pallas_call | solution.py:177
  174.2 3.1 %collective-permute-start.11 = (bf16[256,256]{1,0:T(8,128)(2,1)S(1)}, bf16[256,256]{1,0:T(8,128)(2,1)S(1)}, u32[]{:S(2)}, u32[]{:S(2)}) collective-permute-start(bf16[256,256]{1,0:T(8,128)(2,1)S(1)} %get-tuple-element.15), channel_id=1, source_target_pairs={{0,24},{8,0},{16,8},{24,16},{1,25},{9,1},{17,9},{25,17},{2,26},{10... | collective-permute-start | bytes 393224 | tf_op jit(solution)/shard_map/ppermute | solution.py:417
  177.4 3.6 %collective-permute-start.9 = (bf16[256,256]{1,0:T(8,128)(2,1)}, bf16[256,256]{1,0:T(8,128)(2,1)S(1)}, u32[]{:S(2)}, u32[]{:S(2)}) collective-permute-start(bf16[256,256]{1,0:T(8,128)(2,1)} %get-tuple-element.14), channel_id=1, source_target_pairs={{0,8},{8,16},{16,24},{24,0},{1,9},{9,17},{17,25},{25,1},{2,10},{10... | collective-permute-start | bytes 393224 | tf_op jit(solution)/shard_map/ppermute | solution.py:416
  181.9 2.6 %collective-permute-done.11.add_ref = bf16[256,256]{1,0:T(8,128)(2,1)S(1)} collective-permute-done((bf16[256,256]{1,0:T(8,128)(2,1)S(1)}, bf16[256,256]{1,0:T(8,128)(2,1)S(1)}, u32[]{:S(2)}, u32[]{:S(2)}) %collective-permute-start.11) | collective-permute-done | bytes 131104 | tf_op jit(solution)/shard_map/ppermute | solution.py:417
  184.5 1.9 shard_map.171
  186.4 4.4 %collective-permute-start.12 = (bf16[512,256]{1,0:T(8,128)(2,1)S(1)}, bf16[512,256]{1,0:T(8,128)(2,1)S(1)}, u32[]{:S(2)}, u32[]{:S(2)}) collective-permute-start(bf16[512,256]{1,0:T(8,128)(2,1)S(1)} %shard_map.171), channel_id=1, source_target_pairs={{0,24},{8,0},{16,8},{24,16},{1,25},{9,1},{17,9},{25,17},{2,26},{10... | collective-permute-start | bytes 786440 | tf_op jit(solution)/shard_map/ppermute | solution.py:428
  190.9 2.7 %shard_map.170 = bf16[512,256]{1,0:T(8,128)(2,1)} custom-call(s32[1]{0:T(128)} %bitcast.3.index_ref, bf16[512,2048]{1,0:T(8,128)(2,1)S(1)} %shard_map.167.hz_ref, bf16[4,2048,256]{2,1,0:T(8,128)(2,1)} %bitcast.28, bf16[256,256]{1,0:T(8,128)(2,1)S(1)} %collective-permute-done.9.add_ref), custom_call_target="tpu_custom_call" | custom-call | flops 536870912 | bytes 3145728 | tf_op jit(solution)/shard_map/pallas_call | solution.py:177
  193.5 2.4 %collective-permute-start.10 = (bf16[512,256]{1,0:T(8,128)(2,1)}, bf16[512,256]{1,0:T(8,128)(2,1)S(1)}, u32[]{:S(2)}, u32[]{:S(2)}) collective-permute-start(bf16[512,256]{1,0:T(8,128)(2,1)} %shard_map.170), channel_id=1, source_target_pairs={{0,8},{8,16},{16,24},{24,0},{1,9},{9,17},{17,25},{25,1},{2,10},{10... | collective-permute-start | bytes 786440 | tf_op jit(solution)/shard_map/ppermute | solution.py:423
  196.0 4.3 %shard_map.175 = (bf16[4,512,512]{2,1,0:T(8,128)(2,1)S(1)}, f32[512,256]{1,0:T(8,128)S(1)}, f32[512,128]{1,0:T(8,128)S(1)}, f32[4,8,128]{2,1,0:T(8,128)S(1)}, bf...) custom-call(s32[4]{0:T(128)S(1)} %dynamic-slice_reduce_fusion.1.starts_ref, s32[4]{0:T(128)S(1)} %and_select_fusion.src_ref, ...), custom_call_target="tpu_custom_call" | custom-call | flops 536870912 | bytes 12582912 | tf_op jit(solution)/shard_map/pallas_call | solution.py:37
  200.3 1.9 shard_map.168.x0
  202.7 7.9 %collective-permute-done.10.x1 = bf16[512,256]{1,0:T(8,128)(2,1)S(1)} collective-permute-done((bf16[512,256]{1,0:T(8,128)(2,1)}, bf16[512,256]{1,0:T(8,128)(2,1)S(1)}, u32[]{:S(2)}, u32[]{:S(2)}) %collective-permute-start.10) | collective-permute-done | bytes 262176 | tf_op jit(solution)/shard_map/ppermute | solution.py:423
  210.5 5.0 %shard_map.176 = (bf16[512,256]{1,0:T(8,128)(2,1)}, f32[4,256,256]{2,1,0:T(8,128)}) custom-call(s32[4]{0:T(128)S(1)} %dynamic-slice_reduce_fusion.1.starts_ref, s32[4]{0:T(128)S(1)} %and_select_fusion.src_ref, s32[1]{0:T(128)} %dynamic_slice.24.count_ref, f32[512,256]{1,0:T(8,128)S(1)} %shard_map.168.x0, bf16[512,256]{1,0:T(8,128)(2,1)S(1)} %collective-permute-done.10.x1, ...), custom_call_target="tpu_custom_call" | custom-call | flops 1342177280 | bytes 6291456 | tf_op jit(solution)/shard_map/pallas_call | solution.py:37
  (91 shorter events, 6.0 us)
Async XLA Ops:
  7.2 128.5 %copy-start = (s32[16,4]{0,1:T(4,128)S(1)}, s32[16,4]{0,1:T(4,128)}, u32[]{:S(2)}) copy-start(s32[16,4]{0,1:T(4,128)} %param.31) | copy-start | bytes 772
  7.2 164.5 %all-gather.3.cloned.1.call-start = ((), (), s32[]{:S(2)}) async-start(), calls=%async_computation.4 | async-start | bytes 4456448 | tf_op jit(solution)/shard_map/all_gather | solution.py:333
  7.2 23.2 %collective-permute-start.8 = (bf16[512,256]{1,0:T(8,128)(2,1)}, bf16[512,256]{1,0:T(8,128)(2,1)S(1)}, u32[]{:S(2)}, u32[]{:S(2)}) collective-permute-start(bf16[512,256]{1,0:T(8,128)(2,1)} %param.17), channel_id=1, source_target_pairs={{0,0},{8,128},{16,256},{24,384},{128,8},{136,136},{144,264},{152,3... | collective-permute-start | bytes 786440 | tf_op jit(solution)/shard_map/ppermute | solution.py:332
  30.4 0.7 copy-start.18
  33.0 11.2 %copy-start.3 = (bf16[512,256]{1,0:T(8,128)(2,1)S(1)}, bf16[512,256]{1,0:T(8,128)(2,1)}, u32[]{:S(2)}) copy-start(bf16[512,256]{1,0:T(8,128)(2,1)} %own.1) | copy-start | bytes 786436
  33.9 39.8 %all-to-all-start.1 = ((bf16[8,144,256]{2,1,0:T(8,128)(2,1)}), bf16[8,144,256]{2,1,0:T(8,128)(2,1)S(1)}, u32[]{:S(2)}, u32[]{:S(2)}) async-start(bf16[8,144,256]{2,1,0:T(8,128)(2,1)} %bitcast.13), calls=%async_computation.1 | async-start | bytes 1179648 | tf_op jit(solution)/shard_map/all_to_all | solution.py:354
  44.2 21.0 %collective-permute-start = (bf16[512,256]{1,0:T(8,128)(2,1)S(1)}, bf16[512,256]{1,0:T(8,128)(2,1)S(1)}, u32[]{:S(2)}, u32[]{:S(2)}) collective-permute-start(bf16[512,256]{1,0:T(8,128)(2,1)S(1)} %copy-done.3), channel_id=1, source_target_pairs={{0,1},{1,2},{2,3},{3,4},{4,5},{5,6},{6,7},{7,0},{8,9},{9,10},{10,1... | collective-permute-start | bytes 786440 | tf_op jit(solution)/shard_map/ppermute | solution.py:341
  48.1 19.7 %collective-permute-start.3 = (bf16[512,256]{1,0:T(8,128)(2,1)S(1)}, bf16[512,256]{1,0:T(8,128)(2,1)S(1)}, u32[]{:S(2)}, u32[]{:S(2)}) collective-permute-start(bf16[512,256]{1,0:T(8,128)(2,1)S(1)} %copy-done.3), channel_id=1, source_target_pairs={{0,7},{1,0},{2,1},{3,2},{4,3},{5,4},{6,5},{7,6},{8,15},{9,8},{10,9... | collective-permute-start | bytes 786440 | tf_op jit(solution)/shard_map/ppermute | solution.py:341
  65.2 10.4 %collective-permute-start.1 = (bf16[512,256]{1,0:T(8,128)(2,1)S(1)}, bf16[512,256]{1,0:T(8,128)(2,1)S(1)}, u32[]{:S(2)}, u32[]{:S(2)}) collective-permute-start(bf16[512,256]{1,0:T(8,128)(2,1)S(1)} %collective-permute-done.r1), channel_id=1, source_target_pairs={{0,1},{1,2},{2,3},{3,4},{4,5},{5,6},{6,7},{7,0},{8,9},{9,10},{10,1... | collective-permute-start | bytes 786440 | tf_op jit(solution)/shard_map/ppermute | solution.py:341
  67.1 0.7 copy-start.4
  67.8 9.7 %collective-permute-start.4 = (bf16[512,256]{1,0:T(8,128)(2,1)S(1)}, bf16[512,256]{1,0:T(8,128)(2,1)S(1)}, u32[]{:S(2)}, u32[]{:S(2)}) collective-permute-start(bf16[512,256]{1,0:T(8,128)(2,1)S(1)} %collective-permute-done.3.l1), channel_id=1, source_target_pairs={{0,7},{1,0},{2,1},{3,2},{4,3},{5,4},{6,5},{7,6},{8,15},{9,8},{10,9... | collective-permute-start | bytes 786440 | tf_op jit(solution)/shard_map/ppermute | solution.py:341
  72.9 0.7 copy-start.6
  73.7 29.9 %collective-permute-start.13 = (bf16[8,144,256]{2,1,0:T(8,128)(2,1)S(1)}, bf16[8,144,256]{2,1,0:T(8,128)(2,1)}, u32[]{:S(2)}, u32[]{:S(2)}) collective-permute-start(bf16[8,144,256]{2,1,0:T(8,128)(2,1)S(1)} %all-to-all-done.1.wo_ref), channel_id=1, source_target_pairs={{0,32},{32,0},{1,33},{33,1},{2,34},{34,2},{3,35},{35,3},{4,36},{36... | collective-permute-start | bytes 1769480 | tf_op jit(solution)/shard_map/ppermute | solution.py:355
  75.6 21.4 %copy-start.8 = (bf16[512,256]{1,0:T(8,128)(2,1)}, bf16[512,256]{1,0:T(8,128)(2,1)S(1)}, u32[]{:S(2)}) copy-start(bf16[512,256]{1,0:T(8,128)(2,1)S(1)} %collective-permute-done.1.r2) | copy-start | bytes 786436
  75.6 11.8 %collective-permute-start.2 = (bf16[512,256]{1,0:T(8,128)(2,1)S(1)}, bf16[512,256]{1,0:T(8,128)(2,1)S(1)}, u32[]{:S(2)}, u32[]{:S(2)}) collective-permute-start(bf16[512,256]{1,0:T(8,128)(2,1)S(1)} %collective-permute-done.1.r2), channel_id=1, source_target_pairs={{0,1},{1,2},{2,3},{3,4},{4,5},{5,6},{6,7},{7,0},{8,9},{9,10},{10,1... | collective-permute-start | bytes 786440 | tf_op jit(solution)/shard_map/ppermute | solution.py:341
  77.5 19.5 %copy-start.10 = (bf16[512,256]{1,0:T(8,128)(2,1)}, bf16[512,256]{1,0:T(8,128)(2,1)S(1)}, u32[]{:S(2)}) copy-start(bf16[512,256]{1,0:T(8,128)(2,1)S(1)} %collective-permute-done.4.l2) | copy-start | bytes 786436
  77.6 11.8 %collective-permute-start.5 = (bf16[512,256]{1,0:T(8,128)(2,1)S(1)}, bf16[512,256]{1,0:T(8,128)(2,1)S(1)}, u32[]{:S(2)}, u32[]{:S(2)}) collective-permute-start(bf16[512,256]{1,0:T(8,128)(2,1)S(1)} %collective-permute-done.4.l2), channel_id=1, source_target_pairs={{0,7},{1,0},{2,1},{3,2},{4,3},{5,4},{6,5},{7,6},{8,15},{9,8},{10,9... | collective-permute-start | bytes 786440 | tf_op jit(solution)/shard_map/ppermute | solution.py:341
  87.4 8.1 %collective-permute-start.6 = (bf16[256,256]{1,0:T(8,128)(2,1)S(1)}, bf16[256,256]{1,0:T(8,128)(2,1)S(1)}, u32[]{:S(2)}, u32[]{:S(2)}) collective-permute-start(bf16[256,256]{1,0:T(8,128)(2,1)S(1)} %slice.20), channel_id=1, source_target_pairs={{0,1},{1,2},{2,3},{3,4},{4,5},{5,6},{6,7},{7,0},{8,9},{9,10},{10,1... | collective-permute-start | bytes 393224 | tf_op jit(solution)/shard_map/ppermute | solution.py:344
  89.4 7.6 %collective-permute-start.7 = (bf16[256,256]{1,0:T(8,128)(2,1)S(1)}, bf16[256,256]{1,0:T(8,128)(2,1)S(1)}, u32[]{:S(2)}, u32[]{:S(2)}) collective-permute-start(bf16[256,256]{1,0:T(8,128)(2,1)S(1)} %slice.21), channel_id=1, source_target_pairs={{0,7},{1,0},{2,1},{3,2},{4,3},{5,4},{6,5},{7,6},{8,15},{9,8},{10,9... | collective-permute-start | bytes 393224 | tf_op jit(solution)/shard_map/ppermute | solution.py:345
  95.6 0.7 copy-start.12
  97.0 0.7 copy-start.14
  97.7 0.9 copy-start.5
  98.6 0.9 copy-start.7
  99.6 0.9 copy-start.9
  100.5 0.9 copy-start.11
  101.5 0.9 copy-start.13
  102.4 0.9 copy-start.15
  107.0 4.3 %copy-start.21 = (f32[4,3,256]{2,0,1:T(4,128)S(1)}, f32[4,3,256]{2,0,1:T(4,128)}, u32[]{:S(2)}) copy-start(f32[4,3,256]{2,0,1:T(4,128)} %param.27) | copy-start | bytes 36868
  107.0 4.3 %copy-start.19 = (f32[4,3,2048]{2,0,1:T(4,128)S(1)}, f32[4,3,2048]{2,0,1:T(4,128)}, u32[]{:S(2)}) copy-start(f32[4,3,2048]{2,0,1:T(4,128)} %param.28) | copy-start | bytes 294916
  107.0 4.7 %copy-start.23 = (s32[16,4]{0,1:T(4,128)S(1)}, s32[16,4]{0,1:T(4,128)}, u32[]{:S(2)}) copy-start(s32[16,4]{0,1:T(4,128)} %param.30) | copy-start | bytes 772
  107.0 19.1 %all-to-all-start.2 = ((f32[4,72,512]{2,1,0:T(8,128)}), f32[4,72,512]{2,1,0:T(8,128)S(1)}, u32[]{:S(2)}, u32[]{:S(2)}) async-start(f32[4,72,512]{2,1,0:T(8,128)} %bitcast.14), calls=%async_computation.2 | async-start | bytes 1179648 | tf_op jit(solution)/shard_map/all_to_all | solution.py:390
  111.8 1.2 copy-start.2
  113.9 1.4 copy-start.1
  115.3 20.5 %copy-start.22 = (f32[2048]{0:T(1024)S(1)}, f32[2048]{0:T(1024)}, u32[]{:S(2)}) copy-start(f32[2048]{0:T(1024)} %param.22) | copy-start | bytes 24580
  115.3 20.7 %copy-start.20 = (f32[4,2048]{1,0:T(4,128)S(1)}, f32[4,2048]{1,0:T(4,128)}, u32[]{:S(2)}) copy-start(f32[4,2048]{1,0:T(4,128)} %param.21) | copy-start | bytes 98308
  126.1 37.1 %all-to-all-start = ((bf16[16,272,256]{2,1,0:T(8,128)(2,1)}), bf16[16,272,256]{2,1,0:T(8,128)(2,1)}, u32[]{:S(2)}, u32[]{:S(2)}) async-start(bf16[16,272,256]{2,1,0:T(8,128)(2,1)} %copy-done.1), calls=%async_computation | async-start | bytes 4456448 | tf_op jit(solution)/shard_map/all_to_all | solution.py:373
  166.1 29.9 %all-to-all-start.3 = ((bf16[8,64,512]{2,1,0:T(8,128)(2,1)}), bf16[8,64,512]{2,1,0:T(8,128)(2,1)S(1)}, u32[]{:S(2)}, u32[]{:S(2)}) async-start(bf16[8,64,512]{2,1,0:T(8,128)(2,1)} %broadcast_in_dim.24), calls=%async_computation.3 | async-start | bytes 1048576 | tf_op jit(solution)/shard_map/all_to_all | solution.py:407
  171.7 9.3 %copy-start.27 = (s32[16]{0:T(128)S(1)}, s32[16]{0:T(128)}, u32[]{:S(2)}) copy-start(s32[16]{0:T(128)} %param.29) | copy-start | bytes 196
  171.7 10.1 %copy-start.26 = (f32[4]{0:T(128)S(1)}, f32[4]{0:T(128)}, u32[]{:S(2)}) copy-start(f32[4]{0:T(128)} %param.25) | copy-start | bytes 52
  174.2 10.3 %collective-permute-start.11 = (bf16[256,256]{1,0:T(8,128)(2,1)S(1)}, bf16[256,256]{1,0:T(8,128)(2,1)S(1)}, u32[]{:S(2)}, u32[]{:S(2)}) collective-permute-start(bf16[256,256]{1,0:T(8,128)(2,1)S(1)} %get-tuple-element.15), channel_id=1, source_target_pairs={{0,24},{8,0},{16,8},{24,16},{1,25},{9,1},{17,9},{25,17},{2,26},{10... | collective-permute-start | bytes 393224 | tf_op jit(solution)/shard_map/ppermute | solution.py:417
  177.4 13.4 %collective-permute-start.9 = (bf16[256,256]{1,0:T(8,128)(2,1)}, bf16[256,256]{1,0:T(8,128)(2,1)S(1)}, u32[]{:S(2)}, u32[]{:S(2)}) collective-permute-start(bf16[256,256]{1,0:T(8,128)(2,1)} %get-tuple-element.14), channel_id=1, source_target_pairs={{0,8},{8,16},{16,24},{24,0},{1,9},{9,17},{17,25},{25,1},{2,10},{10... | collective-permute-start | bytes 393224 | tf_op jit(solution)/shard_map/ppermute | solution.py:416
  186.4 16.2 %collective-permute-start.12 = (bf16[512,256]{1,0:T(8,128)(2,1)S(1)}, bf16[512,256]{1,0:T(8,128)(2,1)S(1)}, u32[]{:S(2)}, u32[]{:S(2)}) collective-permute-start(bf16[512,256]{1,0:T(8,128)(2,1)S(1)} %shard_map.171), channel_id=1, source_target_pairs={{0,24},{8,0},{16,8},{24,16},{1,25},{9,1},{17,9},{25,17},{2,26},{10... | collective-permute-start | bytes 786440 | tf_op jit(solution)/shard_map/ppermute | solution.py:428
  190.8 5.1 %copy-start.24 = (f32[4,256]{1,0:T(4,128)S(1)}, f32[4,256]{1,0:T(4,128)}, u32[]{:S(2)}) copy-start(f32[4,256]{1,0:T(4,128)} %param.19) | copy-start | bytes 12292
  190.8 5.1 %copy-start.25 = (f32[256]{0:T(256)S(1)}, f32[256]{0:T(256)}, u32[]{:S(2)}) copy-start(f32[256]{0:T(256)} %param.20) | copy-start | bytes 3076
  190.8 5.2 %copy-start.16 = (f32[4]{0:T(128)S(1)}, f32[4]{0:T(128)}, u32[]{:S(2)}) copy-start(f32[4]{0:T(128)} %rate_ref.1) | copy-start | bytes 52
  190.9 5.2 %copy-start.17 = (f32[4]{0:T(128)S(1)}, f32[4]{0:T(128)}, u32[]{:S(2)}) copy-start(f32[4]{0:T(128)} %bias_ref.1) | copy-start | bytes 52
  193.5 17.0 %collective-permute-start.10 = (bf16[512,256]{1,0:T(8,128)(2,1)}, bf16[512,256]{1,0:T(8,128)(2,1)S(1)}, u32[]{:S(2)}, u32[]{:S(2)}) collective-permute-start(bf16[512,256]{1,0:T(8,128)(2,1)} %shard_map.170), channel_id=1, source_target_pairs={{0,8},{8,16},{16,24},{24,0},{1,9},{9,17},{17,25},{25,1},{2,10},{10... | collective-permute-start | bytes 786440 | tf_op jit(solution)/shard_map/ppermute | solution.py:423
Sparse Core Ops, SparseCore 0:
  31.3 46.5 all-gather.2

commit v2 on v1

--- a/solution.py
+++ b/solution.py
@@ -17,8 +17,8 @@
 GROUPS = 16
 GROUP = ("x", "ylo", "core")
 SHARD = ("yhi", "z")
+SMALL = 72
 PAY = 272
-SMALL = 72
 
 
 bf16 = jnp.bfloat16
@@ -31,7 +31,7 @@
     return lax.broadcasted_iota(jnp.int32, shape, dim)
 
 
-def call(kernel, scalars, operands, outs, flops=0, moved=0):
+def call(kernel, scalars, operands, outs, flops=0, moved=0, scratch=(), room=8):
     smem = pl.BlockSpec(memory_space=pltpu.SMEM)
     whole = pl.BlockSpec(memory_space=pltpu.VMEM)
     return pl.pallas_call(
@@ -39,7 +39,8 @@
         in_specs=[smem] * len(scalars) + [whole] * len(operands),
         out_specs=jax.tree.map(lambda _: whole, outs),
         out_shape=outs,
-        compiler_params=pltpu.CompilerParams(vmem_limit_bytes=48 << 20),
+        scratch_shapes=scratch,
+        compiler_params=pltpu.CompilerParams(vmem_limit_bytes=room << 20),
         cost_estimate=pl.CostEstimate(flops=flops, bytes_accessed=moved, transcendentals=0),
     )(*scalars, *operands)
 
@@ -48,10 +49,29 @@
     return jax.ShapeDtypeStruct(shape, dtype)
 
 
+def group_index():
+    return lax.axis_index("x") * 4 + lax.axis_index("ylo") * 2 + lax.axis_index("core")
+
+
 def bounds(starts_ref):
-    starts = [starts_ref[k] for k in range(REQ)]
+    group = group_index()
+    starts = [starts_ref[k, group] for k in range(REQ)]
     ends = [jnp.minimum(s, TOK) for s in starts[1:]] + [jnp.int32(TOK)]
     return starts, ends
+
+
+def owners(src_ref):
+    group = group_index()
+    return [src_ref[k, group] >> 2 for k in range(REQ)]
+
+
+def bc_lanes(read):
+    yhi, z = lax.axis_index("yhi"), lax.axis_index("z")
+    block, offset = yhi * 2 + (z >> 2), (z & 3) * 32
+    b = pltpu.roll(read(block), (128 - offset) & 127, 1)
+    c = pltpu.roll(read(block + 8), (160 - offset) & 127, 1)
+    lane = iota(b.shape, 1)
+    return jnp.where(lane < 32, b, jnp.where(lane < 64, c, 0.0))
 
 
 def own_start(tok, starts):
@@ -95,47 +115,91 @@
     return out
 
 
-def pack_kernel(slot_ref, state_ref, tail_ref, out_ref):
+def slot_for(src_ref, target):
+    group = group_index()
+    slot = jnp.int32(0)
+    for k in range(REQ):
+        place = src_ref[k, target]
+        slot = jnp.where((place >> 2) == group, place & 3, slot)
+    return slot
+
+
+def pack_kernel(src_ref, state_ref, x_ref, bc_ref, out_ref, tmp_ref):
+    row = iota((16, CHAN), 0)
+    wide = [
+        bc_lanes(lambda block, i=i: bc_ref[i, :, pl.ds(pl.multiple_of(block * 128, 128), 128)])
+        for i in range(3)
+    ]
+    for slot in range(REQ):
+        value = jnp.zeros((16, CHAN), f32)
+        for i in range(3):
+            value = jnp.where(row == i, x_ref[i, slot : slot + 1, :], value)
+            line = jnp.concatenate([wide[i][slot : slot + 1], jnp.zeros((1, 128), f32)], axis=1)
+            value = jnp.where(row == 3 + i, line, value)
+        tmp_ref[slot] = value.astype(bf16)
+
     @pl.loop(0, GROUPS)
     def _(i):
-        slot = slot_ref[i]
+        slot = slot_for(src_ref, i)
         out_ref[i, :STATES, :] = state_ref[slot].astype(bf16)
-        out_ref[i, STATES:, :] = tail_ref[slot].astype(bf16)
-
-
-def arrange_kernel(z_ref, own, r1, r2, r3, l1, l2, l3, far_a, far_b, hz_ref):
-    def put(block, step, low, high):
-        place = pl.multiple_of(lax.rem(z_ref[0] + step + 8, 8) * CHAN, CHAN)
-        hz_ref[low:high, pl.ds(place, CHAN)] = block[...]
-
-    for step, block in ((0, own), (-1, r1), (-2, r2), (-3, r3), (1, l1), (2, l2), (3, l3)):
-        put(block, step, 0, TOK)
-    put(far_a, 4, 0, TOK // 2)
-    put(far_b, 4, TOK // 2, TOK)
-
-
-def small_kernel(core_ref, hz_ref, wo_ref, wx_ref, out_ref):
+        out_ref[i, STATES:, :] = tmp_ref[slot]
+
+
+def place_kernel(plan, count, *refs):
+    blocks, hz_ref, sems = refs[:count], refs[-2], refs[-1]
+    copies = []
+    for i, (step, low) in enumerate(plan):
+        block = blocks[count - len(plan) + i]
+        place = pl.multiple_of(((lax.axis_index("z") + step + 8) & 7) * CHAN, CHAN)
+        target = hz_ref.at[low : low + block.shape[0], pl.ds(place, CHAN)]
+        copies.append(pltpu.make_async_copy(block, target, sems.at[i]))
+        copies[-1].start()
+    for copy in copies:
+        copy.wait()
+
+
+def place_blocks(plan, operands):
+    anywhere = pl.BlockSpec(memory_space=pl.ANY)
+    return pl.pallas_call(
+        functools.partial(place_kernel, plan, len(operands)),
+        in_specs=[anywhere] * len(operands),
+        out_specs=anywhere,
+        out_shape=array(bf16, TOK, 8 * CHAN),
+        input_output_aliases={0: 0} if len(operands) > len(plan) else {},
+        scratch_shapes=[pltpu.SemaphoreType.DMA((len(plan),))],
+        compiler_params=pltpu.CompilerParams(vmem_limit_bytes=4 << 20),
+        cost_estimate=pl.CostEstimate(flops=0, bytes_accessed=1 << 20, transcendentals=0),
+        name="place_blocks",
+    )(*operands)
+
+
+def small_kernel(hz_ref, wo_ref, wx_ref, out_ref):
     rows = hz_ref[...]
-    for ref, place in ((wo_ref, core_ref[0]), (wx_ref, 1 - core_ref[0])):
+    core = lax.axis_index("core")
+    for ref, place in ((wo_ref, core), (wx_ref, 1 - core)):
         cols = jnp.concatenate([ref[s] for s in range(8)], axis=1)
         out_ref[place] = lax.dot_general(cols, rows, NT, preferred_element_type=f32)
 
 
-def conv_kernel(starts_ref, src_ref, part_ref, served_ref, taps_ref, bc_ref, dt_ref):
+def conv_kernel(starts_ref, src_ref, part_ref, served_ref, taps_ref, bias_ref, bc_ref, dt_ref):
     starts, ends = bounds(starts_ref)
+    src = owners(src_ref)
     signal = part_ref[0] + part_ref[1] + part_ref[2] + part_ref[3]
     dt_ref[...] = signal[64:]
     signal = signal[:64]
-    taps = [taps_ref[i : i + 1, :] for i in range(4)]
+    own_taps = bc_lanes(lambda block: taps_ref[:, pl.ds(pl.multiple_of(block * 128, 128), 128)])
+    own_bias = bc_lanes(lambda block: bias_ref[pl.ds(block, 1), :])
+    taps = [own_taps[i : i + 1] for i in range(4)]
     tails = []
     for k in range(REQ):
-        rows = served_ref[src_ref[k], STATES:, :].astype(f32)
+        rows = served_ref[src[k], STATES:, :].astype(f32)
         tails.append([rows[3 + i : 4 + i, :128] for i in range(3)])
     table = jnp.concatenate(
         [
             tail_rows(tails, taps, 16, 128),
-            taps_ref[...],
-            jnp.zeros((104, 128), f32),
+            own_taps,
+            own_bias,
+            jnp.zeros((107, 128), f32),
         ],
         axis=0,
     ).T
@@ -171,9 +235,10 @@
     out_ref[rows, :] = (total[rows] + add_ref[...].astype(f32)).astype(bf16)
 
 
-def partial(kernel, index, operands, outs):
+def partial(kernel, way, operands, outs):
     whole = pl.BlockSpec(memory_space=pltpu.VMEM)
-    block = pl.BlockSpec((None, 8 * CHAN, CHAN), lambda i, b: (b[0], 0, 0))
+    block = pl.BlockSpec((None, 8 * CHAN, CHAN), lambda i, b: ((b[0] + way) & 3, 0, 0))
+    index = lax.axis_index("yhi").astype(jnp.int32).reshape(1)
     return pl.pallas_call(
         kernel,
         grid_spec=pltpu.PrefetchScalarGridSpec(
@@ -191,14 +256,15 @@
 
 
 def mixing_kernel(
-    starts_ref, src_ref, rate_ref, bias_ref, bc_ref, dt_ref, served_ref, par_ref,
+    starts_ref, src_ref, rate_ref, bias_ref, bc_ref, dt_ref, served_ref, taps_ref,
     mix_ref, carry_ref, cols_ref, decay_ref, b_ref, tail_ref,
 ):
     starts, ends = bounds(starts_ref)
-    taps = [par_ref[i : i + 1, :] for i in range(4)]
+    src = owners(src_ref)
+    taps = [taps_ref[i : i + 1, :] for i in range(4)]
     tails = []
     for k in range(REQ):
-        rows = served_ref[src_ref[k], STATES:, :].astype(f32)
+        rows = served_ref[src[k], STATES:, :].astype(f32)
         tails.append([rows[i : i + 1, :] for i in range(3)])
     table = tail_rows(tails, taps, 128, CHAN)
     onehot = first_tokens((TOK, 128), 0, starts, ends)
@@ -242,7 +308,7 @@
     lane = iota((TOK, CHAN), 1)
     carry = jnp.zeros((TOK, CHAN), f32)
     for k in range(REQ):
-        old = served_ref[src_ref[k], :CHAN, :]
+        old = served_ref[src[k], :CHAN, :]
         part = lax.dot_general(c_cols, old, NT, preferred_element_type=f32)
         carry = jnp.where((tok_c >= starts[k]) & (tok_c < ends[k]), part, carry)
     scale = jnp.zeros((TOK, CHAN), f32)
@@ -264,24 +330,29 @@
 
 
 def output_kernel(
-    starts_ref, src_ref, count_ref, x0, x1, x2, served_ref, par_ref,
+    starts_ref, src_ref, count_ref, skip_ref, x0, x1, x2, served_ref, taps_ref, bias_ref,
     mix_ref, carry_ref, cols_ref, decay_ref, b_ref, tail_ref, y_ref, state_ref,
 ):
     starts, ends = bounds(starts_ref)
-    count = count_ref[0]
+    src = owners(src_ref)
+    count = count_ref[group_index()]
     signal = x0[...] + x1[...].astype(f32) + x2[...].astype(f32)
-    taps = [par_ref[i : i + 1, :] for i in range(4)]
+    taps = [taps_ref[i : i + 1, :] for i in range(4)]
+    bias = jnp.concatenate([bias_ref[0:1, :], bias_ref[1:2, :]], axis=1)
     summed = tail_ref[...]
     tok = iota((TOK, CHAN), 0)
     lane = iota((TOK, CHAN), 1)
     begin = own_start(tok, starts)
-    summed = summed + taps[3] * signal + par_ref[4:5, :]
+    summed = summed + taps[3] * signal + bias
     for j in range(1, 4):
         moved = jnp.where(tok - j >= begin, pltpu.roll(signal, j, 0), 0.0)
         summed = summed + taps[3 - j] * moved
     x_low = sigmoid_gate(summed).astype(bf16)
     x_wide = x_low.astype(f32)
-    base = carry_ref[...] + par_ref[5:6, :] * x_wide
+    skip = jnp.zeros((TOK, CHAN), f32)
+    for h in range(HEAD_DEV):
+        skip = jnp.where(lane >= h * P_SIZE, skip_ref[h], skip)
+    base = carry_ref[...] + skip * x_wide
     for b in range(4):
         low, width = b * 128, (b + 1) * 128
         total = base[low : low + 128]
@@ -310,7 +381,7 @@
         )
         for h in range(HEAD_DEV):
             lo, hi = h * P_SIZE, (h + 1) * P_SIZE
-            old = served_ref[src_ref[k], lo:hi, :].astype(f32)
+            old = served_ref[src[k], lo:hi, :].astype(f32)
             new = decay_ref[k, h : h + 1, 0:1] * old + gained[lo:hi]
             state_ref[k, lo:hi, :] = jnp.where(k < count, new, 0.0)
 
@@ -319,14 +390,8 @@
     hidden, w_x, w_small, conv_x, conv_x_bias, conv_bc, conv_bc_bias, rate, dt_bias, dskip,
     old_state, x_tail, bc_tail, req_count, req_source, req_start,
 ):
-    group = lax.axis_index(GROUP)
     core = lax.axis_index("core")
-    yhi = lax.axis_index("yhi")
-    z = lax.axis_index("z")
-    mine = lax.dynamic_index_in_dim(req_source, group, 0, keepdims=False)
-    src = mine // REQ
-    starts = lax.dynamic_index_in_dim(req_start, group, 0, keepdims=False)
-    count = lax.dynamic_slice_in_dim(req_count, group, 1, 0)
+    src, starts = req_source.T, req_start.T
 
     swap = [(a * 4 + b, b * 4 + a) for a in range(4) for b in range(4)]
     w_swapped = lax.ppermute(w_x, ("x", "yhi"), swap)
@@ -354,34 +419,27 @@
     w_cols = lax.all_to_all(w_cols, "z", 0, 0, tiled=True)
     w_other = lax.ppermute(w_cols, "core", [(0, 1), (1, 0)])
 
-    owner, slot = req_source // REQ, req_source % REQ
-    slots = jnp.sum(jnp.where(owner == group, slot, 0), axis=1).astype(jnp.int32)
-    bc_mine = lax.dynamic_slice(
-        bc_tail.reshape(REQ, 3, 2, 4, 8, 32), (0, 0, 0, yhi, z, 0), (REQ, 3, 2, 1, 1, 32)
-    ).reshape(REQ, 3, 64)
-    tails = jnp.concatenate(
-        [x_tail, jnp.pad(bc_mine, ((0, 0), (0, 0), (0, 192))), jnp.zeros((REQ, 10, 256), f32)],
-        axis=1,
-    )
-    packed = call(
+    served = call(
         pack_kernel,
-        (slots,),
-        (old_state.reshape(REQ, 256, STATES), tails),
-        array(bf16, GROUPS, PAY, 256),
+        (src,),
+        (
+            old_state.reshape(REQ, CHAN, STATES),
+            x_tail.transpose(1, 0, 2),
+            bc_tail.transpose(1, 0, 2),
+        ),
+        array(bf16, GROUPS, PAY, STATES),
         moved=7 << 20,
-    )
-    served = lax.all_to_all(packed, GROUP, 0, 0, tiled=True)
-
-    hz = call(
-        arrange_kernel,
-        (z.astype(jnp.int32).reshape(1),),
-        blocks,
-        array(bf16, TOK, 8 * CHAN),
-        moved=4 << 20,
-    )
+        scratch=[pltpu.VMEM((REQ, 16, CHAN), bf16)],
+    )
+    served = lax.all_to_all(served, GROUP, 0, 0, tiled=True)
+
+    hz = place_blocks(((0, 0), (-1, 0), (1, 0)), (hidden, blocks[1], blocks[4]))
+    for step in (2, 3):
+        hz = place_blocks(((-step, 0), (step, 0)), (hz, blocks[step], blocks[step + 3]))
+    hz = place_blocks(((4, 0), (4, half)), (hz, blocks[7], blocks[8]))
     part_small = call(
         small_kernel,
-        (core.astype(jnp.int32).reshape(1),),
+        (),
         (hz, w_cols, w_other),
         array(f32, 2, 2 * SMALL, TOK),
         flops=2 * 288 * 2048 * 512,
@@ -389,17 +447,10 @@
     )
     part_small = lax.all_to_all(part_small.reshape(4, SMALL, TOK), "yhi", 0, 0, tiled=True)
 
-    taps_bc = lax.dynamic_slice(
-        conv_bc.reshape(4, 2, 4, 8, 32), (0, 0, yhi, z, 0), (4, 2, 1, 1, 32)
-    ).reshape(4, 64)
-    bias_bc = lax.dynamic_slice(
-        conv_bc_bias.reshape(2, 4, 8, 32), (0, yhi, z, 0), (2, 1, 1, 32)
-    ).reshape(1, 64)
-    taps_bc = jnp.pad(jnp.concatenate([taps_bc, bias_bc], axis=0), ((0, 3), (0, 64)))
     bc_own, dt_raw = call(
         conv_kernel,
         (starts, src),
-        (part_small, served, taps_bc),
+        (part_small, served, conv_bc, conv_bc_bias.reshape(16, 128)),
         (array(bf16, 64, TOK), array(f32, SMALL - 64, TOK)),
         flops=2 * 6 * 128 * 128 * 512,
         moved=1 << 20,
@@ -409,32 +460,27 @@
     )
 
     w_view = w_all.reshape(4, 8 * CHAN, CHAN)
-    index = [((yhi + r) % 4).astype(jnp.int32).reshape(1) for r in range(4)]
     ahead = [(i, (i + 1) % 4) for i in range(4)]
     back = [(i, (i - 1) % 4) for i in range(4)]
-    low, high = partial(far_kernel, index[2], (hz, w_view), (array(bf16, half, CHAN),) * 2)
+    low, high = partial(far_kernel, 2, (hz, w_view), (array(bf16, half, CHAN),) * 2)
     low = lax.ppermute(low, "yhi", ahead)
     high = lax.ppermute(high, "yhi", back)
-    x0 = partial(own_kernel, index[0], (hz, w_view), array(f32, TOK, CHAN))
+    x0 = partial(own_kernel, 0, (hz, w_view), array(f32, TOK, CHAN))
     x1 = partial(
         functools.partial(near_kernel, 0),
-        index[1], (hz, w_view, low), array(bf16, TOK, CHAN),
+        1, (hz, w_view, low), array(bf16, TOK, CHAN),
     )
     x1 = lax.ppermute(x1, "yhi", ahead)
     x2 = partial(
         functools.partial(near_kernel, half),
-        index[3], (hz, w_view, high), array(bf16, TOK, CHAN),
+        3, (hz, w_view, high), array(bf16, TOK, CHAN),
     )
     x2 = lax.ppermute(x2, "yhi", back)
 
-    params = jnp.concatenate(
-        [conv_x, conv_x_bias[None], jnp.repeat(dskip, P_SIZE)[None], jnp.zeros((2, CHAN), f32)],
-        axis=0,
-    )
     made = call(
         mixing_kernel,
         (starts, src, rate, dt_bias),
-        (bc_all, dt_raw, served, params),
+        (bc_all, dt_raw, served, conv_x),
         (
             array(bf16, HEAD_DEV, TOK, TOK),
             array(f32, TOK, CHAN),
@@ -445,14 +491,16 @@
         ),
         flops=2 * 8 * 512 * 256 * 256,
         moved=12 << 20,
+        room=24,
     )
     y, state = call(
         output_kernel,
-        (starts, src, count),
-        (x0, x1, x2, served, params, *made),
+        (starts, src, req_count, dskip),
+        (x0, x1, x2, served, conv_x, conv_x_bias.reshape(2, 128), *made),
         (array(bf16, TOK, CHAN), array(f32, REQ, 256, STATES)),
         flops=2 * 20 * 512 * 256 * 256,
         moved=6 << 20,
+        room=24,
     )
     return y, state.reshape(REQ, HEAD_DEV, P_SIZE, STATES)
 

time: 224 us -> 209 us (0.933)
  the two profiles are of different devices: /device:TPU:2 before, /device:TPU:6 now
where the time goes in v2:
time: 209 us; the launch traced here: 205 us
  starting transfers between devices  74.6 us (36%)
  waiting for transfers between devices  54 us (26%)
  blocking collectives  31.3 us (15%)
  Pallas kernels  20.2 us (10%)
  between operations  14.5 us (7%)
  local copies, waits for them, and re-layouts  10.6 us (5%)
    all_to_all x1, blocking collectives, layer(): served = lax.all_to_all(served, GROUP, 0, 0, tiled=True)  31.3 us
    ppermute x6, starting transfers between devices, layer(): block = lax.ppermute(block, 'z', ring)  21.1 us
    ppermute x6, waiting for transfers between devices, layer(): block = lax.ppermute(block, 'z', ring)  19.6 us
    ppermute x1, waiting for transfers between devices, layer(): w_swapped = lax.ppermute(w_x, ('x', 'yhi'), swap)  17.1 us
    pallas_call x5, Pallas kernels, call(): pl.pallas_call(kernel, in_specs=[smem] * len(scalars) + [whole] * len(ope...  11.2 us
    all_to_all x1, waiting for transfers between devices, layer(): lax.all_to_all(part_small.reshape(4, SMALL, TOK), 'yhi', 0, 0, tiled=True)  11 us
    all_to_all x1, starting transfers between devices, layer(): w_cols = lax.all_to_all(w_cols, 'z', 0, 0, tiled=True)  10.3 us
    unnamed x47, local copies, waits for them, and re-layouts  8.79 us
  transfers between devices with their start and end apart: 18, of which 8 were waited for; matrix products, arithmetic and copies ran while one was open for 2% of the time, Pallas kernels for 8%

profile of v2, /device:TPU:6, one launch (start us, length us, event | category | flops | bytes accessed | tf_op | source)
XLA Modules:
  0.0 205.3 jit_solution(5543264476237200890)
XLA Ops:
  7.2 6.1 %collective-permute-start.8 = (bf16[512,256]{1,0:T(8,128)(2,1)}, bf16[512,256]{1,0:T(8,128)(2,1)S(1)}, u32[]{:S(2)}, u32[]{:S(2)}) collective-permute-start(bf16[512,256]{1,0:T(8,128)(2,1)} %param.17), channel_id=1, source_target_pairs={{0,0},{8,128},{16,256},{24,384},{128,8},{136,136},{144,264},{152,3... | collective-permute-start | bytes 786440 | tf_op jit(solution)/shard_map/ppermute | solution.py:397
  13.3 17.1 %collective-permute-done.8 = bf16[512,256]{1,0:T(8,128)(2,1)S(1)} collective-permute-done((bf16[512,256]{1,0:T(8,128)(2,1)}, bf16[512,256]{1,0:T(8,128)(2,1)S(1)}, u32[]{:S(2)}, u32[]{:S(2)}) %collective-permute-start.8) | collective-permute-done | bytes 262176 | tf_op jit(solution)/shard_map/ppermute | solution.py:397
  30.4 0.7 copy-done.22
  31.1 1.7 copy.24
  33.0 0.9 copy.25
  33.8 10.3 %all-to-all-start.1 = ((bf16[8,144,256]{2,1,0:T(8,128)(2,1)}), bf16[8,144,256]{2,1,0:T(8,128)(2,1)S(1)}, u32[]{:S(2)}, u32[]{:S(2)}) async-start(bf16[8,144,256]{2,1,0:T(8,128)(2,1)} %bitcast.12), calls=%async_computation.1 | async-start | bytes 1179648 | tf_op jit(solution)/shard_map/all_to_all | solution.py:419
  44.2 3.9 %collective-permute-start = (bf16[512,256]{1,0:T(8,128)(2,1)S(1)}, bf16[512,256]{1,0:T(8,128)(2,1)S(1)}, u32[]{:S(2)}, u32[]{:S(2)}) collective-permute-start(bf16[512,256]{1,0:T(8,128)(2,1)S(1)} %copy-done.5), channel_id=1, source_target_pairs={{0,1},{1,2},{2,3},{3,4},{4,5},{5,6},{6,7},{7,0},{8,9},{9,10},{10,1... | collective-permute-start | bytes 786440 | tf_op jit(solution)/shard_map/ppermute | solution.py:406
  48.1 3.1 %collective-permute-start.1 = (bf16[512,256]{1,0:T(8,128)(2,1)S(1)}, bf16[512,256]{1,0:T(8,128)(2,1)S(1)}, u32[]{:S(2)}, u32[]{:S(2)}) collective-permute-start(bf16[512,256]{1,0:T(8,128)(2,1)S(1)} %copy-done.5), channel_id=1, source_target_pairs={{0,7},{1,0},{2,1},{3,2},{4,3},{5,4},{6,5},{7,6},{8,15},{9,8},{10,9... | collective-permute-start | bytes 786440 | tf_op jit(solution)/shard_map/ppermute | solution.py:406
  51.2 14.8 %collective-permute-done.refs_1_ = bf16[512,256]{1,0:T(8,128)(2,1)S(1)} collective-permute-done((bf16[512,256]{1,0:T(8,128)(2,1)S(1)}, bf16[512,256]{1,0:T(8,128)(2,1)S(1)}, u32[]{:S(2)}, u32[]{:S(2)}) %collective-permute-start) | collective-permute-done | bytes 262176 | tf_op jit(solution)/shard_map/ppermute | solution.py:406
  66.0 1.9 collective-permute-start.2
  68.0 5.1 %collective-permute-start.3 = (bf16[512,256]{1,0:T(8,128)(2,1)S(1)}, bf16[512,256]{1,0:T(8,128)(2,1)S(1)}, u32[]{:S(2)}, u32[]{:S(2)}) collective-permute-start(bf16[512,256]{1,0:T(8,128)(2,1)S(1)} %collective-permute-done.1.refs_2_), channel_id=1, source_target_pairs={{0,7},{1,0},{2,1},{3,2},{4,3},{5,4},{6,5},{7,6},{8,15},{9,8},{10,9... | collective-permute-start | bytes 786440 | tf_op jit(solution)/shard_map/ppermute | solution.py:406
  73.1 1.9 collective-permute-start.13
  75.1 1.4 collective-permute-done.2.refs_1_
  76.5 1.9 collective-permute-start.4
  78.4 5.1 %collective-permute-start.5 = (bf16[512,256]{1,0:T(8,128)(2,1)S(1)}, bf16[512,256]{1,0:T(8,128)(2,1)S(1)}, u32[]{:S(2)}, u32[]{:S(2)}) collective-permute-start(bf16[512,256]{1,0:T(8,128)(2,1)S(1)} %collective-permute-done.3.refs_2_), channel_id=1, source_target_pairs={{0,7},{1,0},{2,1},{3,2},{4,3},{5,4},{6,5},{7,6},{8,15},{9,8},{10,9... | collective-permute-start | bytes 786440 | tf_op jit(solution)/shard_map/ppermute | solution.py:406
  83.5 3.4 %collective-permute-done.4.refs_1_ = bf16[512,256]{1,0:T(8,128)(2,1)S(1)} collective-permute-done((bf16[512,256]{1,0:T(8,128)(2,1)S(1)}, bf16[512,256]{1,0:T(8,128)(2,1)S(1)}, u32[]{:S(2)}, u32[]{:S(2)}) %collective-permute-start.4) | collective-permute-done | bytes 262176 | tf_op jit(solution)/shard_map/ppermute | solution.py:406
  86.9 1.9 collective-permute-start.6
  88.9 5.1 %collective-permute-start.7 = (bf16[256,256]{1,0:T(8,128)(2,1)S(1)}, bf16[256,256]{1,0:T(8,128)(2,1)S(1)}, u32[]{:S(2)}, u32[]{:S(2)}) collective-permute-start(bf16[256,256]{1,0:T(8,128)(2,1)S(1)} %slice.21), channel_id=1, source_target_pairs={{0,7},{1,0},{2,1},{3,2},{4,3},{5,4},{6,5},{7,6},{8,15},{9,8},{10,9... | collective-permute-start | bytes 393224 | tf_op jit(solution)/shard_map/ppermute | solution.py:410
  94.0 0.9 copy-done.7
  95.0 0.9 copy-done.9
  95.9 0.1 place_blocks.4.refs_0_
  96.1 0.1 place_blocks.5.refs_0_
  96.2 0.1 place_blocks.6.refs_0_
  96.3 0.2 collective-permute-done.7.refs_2_
  96.6 2.3 %shard_map.172 = f32[2,144,512]{2,1,0:T(8,128)} custom-call(bf16[512,2048]{1,0:T(8,128)(2,1)S(1)} %place_blocks.7.hz_ref, bf16[8,144,256]{2,1,0:T(8,128)(2,1)S(1)} %all-to-all-done.1.wo_ref, bf16[8,144,256]{2,1,0:T(8,128)(2,1)S(1)} %collective-permute-done.13.wx_ref), custom_call_target="tpu_custom_call" | custom-call | flops 603979776 | bytes 4194304 | tf_op jit(solution)/shard_map/pallas_call | solution.py:37
  98.9 7.2 %all-to-all-start.2 = ((f32[4,72,512]{2,1,0:T(8,128)}), f32[4,72,512]{2,1,0:T(8,128)S(1)}, u32[]{:S(2)}, u32[]{:S(2)}) async-start(f32[4,72,512]{2,1,0:T(8,128)} %bitcast.13), calls=%async_computation.2 | async-start | bytes 1179648 | tf_op jit(solution)/shard_map/all_to_all | solution.py:448
  106.2 1.2 copy-done.4
  107.4 1.2 shard_map.171
  108.6 1.4 copy-done.3
  109.9 11.0 %all-to-all-done.2.part_ref = f32[4,72,512]{2,1,0:T(8,128)S(1)} async-done(((f32[4,72,512]{2,1,0:T(8,128)}), f32[4,72,512]{2,1,0:T(8,128)S(1)}, u32[]{:S(2)}, u32[]{:S(2)}) %all-to-all-start.2) | async-done | bytes 589856 | tf_op jit(solution)/shard_map/all_to_all | solution.py:448
  120.9 31.3 %all_to_all.20.served_ref = bf16[16,272,256]{2,1,0:T(8,128)(2,1)S(1)} all-to-all(bf16[16,272,256]{2,1,0:T(8,128)(2,1)} %copy-done.3), channel_id=1, replica_groups=mesh['x'=4,'ylo'=2,'core'=2,'yhi'=4,'z'=8] {'x','ylo','core'}, dimensions={0} | all-to-all | bytes 4456448 | tf_op jit(solution)/shard_map/all_to_all | solution.py:434
  152.3 1.1 shard_map.173
  153.4 0.2 copy-done
  153.7 0.8 broadcast_in_dim.2
  154.5 4.8 %all-to-all-start.3 = ((bf16[8,64,512]{2,1,0:T(8,128)(2,1)}), bf16[8,64,512]{2,1,0:T(8,128)(2,1)S(1)}, u32[]{:S(2)}, u32[]{:S(2)}) async-start(bf16[8,64,512]{2,1,0:T(8,128)(2,1)} %broadcast_in_dim.2), calls=%async_computation.3 | async-start | bytes 1048576 | tf_op jit(solution)/shard_map/all_to_all | solution.py:458
  159.4 1.9 shard_map.168
  161.3 4.0 %collective-permute-start.9 = (bf16[256,256]{1,0:T(8,128)(2,1)S(1)}, bf16[256,256]{1,0:T(8,128)(2,1)S(1)}, u32[]{:S(2)}, u32[]{:S(2)}) collective-permute-start(bf16[256,256]{1,0:T(8,128)(2,1)S(1)} %get-tuple-element.14), channel_id=1, source_target_pairs={{0,8},{8,16},{16,24},{24,0},{1,9},{9,17},{17,25},{25,1},{2,10},{10... | collective-permute-start | bytes 393224 | tf_op jit(solution)/shard_map/ppermute | solution.py:466
  165.3 4.0 %collective-permute-start.11 = (bf16[256,256]{1,0:T(8,128)(2,1)S(1)}, bf16[256,256]{1,0:T(8,128)(2,1)S(1)}, u32[]{:S(2)}, u32[]{:S(2)}) collective-permute-start(bf16[256,256]{1,0:T(8,128)(2,1)S(1)} %get-tuple-element.15), channel_id=1, source_target_pairs={{0,24},{8,0},{16,8},{24,16},{1,25},{9,1},{17,9},{25,17},{2,26},{10... | collective-permute-start | bytes 393224 | tf_op jit(solution)/shard_map/ppermute | solution.py:467
  169.3 3.7 %collective-permute-done.9.add_ref = bf16[256,256]{1,0:T(8,128)(2,1)S(1)} collective-permute-done((bf16[256,256]{1,0:T(8,128)(2,1)S(1)}, bf16[256,256]{1,0:T(8,128)(2,1)S(1)}, u32[]{:S(2)}, u32[]{:S(2)}) %collective-permute-start.9) | collective-permute-done | bytes 131104 | tf_op jit(solution)/shard_map/ppermute | solution.py:466
  173.0 1.9 shard_map.169
  175.0 3.3 %collective-permute-start.10 = (bf16[512,256]{1,0:T(8,128)(2,1)S(1)}, bf16[512,256]{1,0:T(8,128)(2,1)S(1)}, u32[]{:S(2)}, u32[]{:S(2)}) collective-permute-start(bf16[512,256]{1,0:T(8,128)(2,1)S(1)} %shard_map.169), channel_id=1, source_target_pairs={{0,8},{8,16},{16,24},{24,0},{1,9},{9,17},{17,25},{25,1},{2,10},{10... | collective-permute-start | bytes 786440 | tf_op jit(solution)/shard_map/ppermute | solution.py:473
  178.3 2.6 %shard_map.170 = bf16[512,256]{1,0:T(8,128)(2,1)} custom-call(s32[1]{0:T(128)} %bitcast.2.index_ref, bf16[512,2048]{1,0:T(8,128)(2,1)S(1)} %place_blocks.7.hz_ref, bf16[4,2048,256]{2,1,0:T(8,128)(2,1)} %bitcast.31, bf16[256,256]{1,0:T(8,128)(2,1)S(1)} %collective-permute-done.11.add_ref), custom_call_target="tpu_custom_call" | custom-call | flops 536870912 | bytes 3145728 | tf_op jit(solution)/shard_map/pallas_call | solution.py:242
  180.9 4.8 %collective-permute-start.12 = (bf16[512,256]{1,0:T(8,128)(2,1)}, bf16[512,256]{1,0:T(8,128)(2,1)S(1)}, u32[]{:S(2)}, u32[]{:S(2)}) collective-permute-start(bf16[512,256]{1,0:T(8,128)(2,1)} %shard_map.170), channel_id=1, source_target_pairs={{0,24},{8,0},{16,8},{24,16},{1,25},{9,1},{17,9},{25,17},{2,26},{10... | collective-permute-start | bytes 786440 | tf_op jit(solution)/shard_map/ppermute | solution.py:478
  185.8 1.6 copy-done.1
  187.4 3.2 %shard_map.174 = (bf16[4,512,512]{2,1,0:T(8,128)(2,1)S(1)}, f32[512,256]{1,0:T(8,128)S(1)}, f32[512,128]{1,0:T(8,128)S(1)}, f32[4,8,128]{2,1,0:T(8,128)S(1)}, bf...) custom-call(s32[4,16]{1,0:T(4,128)S(1)} %bitcast.24, s32[4,16]{1,0:T(4,128)S(1)} %bitcast.21, f32[4]{0:T(128)S(1)} %copy-done.18, ...), custom_call_target="tpu_custom_call" | custom-call | flops 536870912 | bytes 12582912 | tf_op jit(solution)/shard_map/pallas_call | solution.py:37
  190.7 2.1 %shard_map.167.x0 = f32[512,256]{1,0:T(8,128)S(1)} custom-call(s32[1]{0:T(128)} %bitcast.2.index_ref, bf16[512,2048]{1,0:T(8,128)(2,1)S(1)} %place_blocks.7.hz_ref, bf16[4,2048,256]{2,1,0:T(8,128)(2,1)} %bitcast.32), custom_call_target="tpu_custom_call" | custom-call | flops 536870912 | bytes 3145728 | tf_op jit(solution)/shard_map/pallas_call | solution.py:242
  192.8 2.3 %collective-permute-done.12.x2 = bf16[512,256]{1,0:T(8,128)(2,1)S(1)} collective-permute-done((bf16[512,256]{1,0:T(8,128)(2,1)}, bf16[512,256]{1,0:T(8,128)(2,1)S(1)}, u32[]{:S(2)}, u32[]{:S(2)}) %collective-permute-start.12) | collective-permute-done | bytes 262176 | tf_op jit(solution)/shard_map/ppermute | solution.py:478
  195.1 3.3 %shard_map.175 = (bf16[512,256]{1,0:T(8,128)(2,1)}, f32[4,256,256]{2,1,0:T(8,128)}) custom-call(s32[4,16]{1,0:T(4,128)S(1)} %bitcast.25, s32[4,16]{1,0:T(4,128)S(1)} %bitcast.22, s32[16]{0:T(128)S(1)} %copy-done.20, f32[4]{0:T(128)S(1)} %copy-done.21, f32[512,256]{1,0:T(8,128)S(1)} %shard_map.167.x0, bf16[512,256]{1,0:T(8,128)(2,1)S(1)} %collective-permute-done.10.x1, ...), custom_call_target="tpu_custom_call" | custom-call | flops 1342177280 | bytes 6291456 | tf_op jit(solution)/shard_map/pallas_call | solution.py:37
  (58 shorter events, 0.4 us)
Async XLA Ops:
  7.2 152.2 %all-gather.3.cloned.1.call-start = ((), (), s32[]{:S(2)}) async-start(), calls=%async_computation.4 | async-start | bytes 4456448 | tf_op jit(solution)/shard_map/all_gather | solution.py:398
  7.2 23.2 %collective-permute-start.8 = (bf16[512,256]{1,0:T(8,128)(2,1)}, bf16[512,256]{1,0:T(8,128)(2,1)S(1)}, u32[]{:S(2)}, u32[]{:S(2)}) collective-permute-start(bf16[512,256]{1,0:T(8,128)(2,1)} %param.17), channel_id=1, source_target_pairs={{0,0},{8,128},{16,256},{24,384},{128,8},{136,136},{144,264},{152,3... | collective-permute-start | bytes 786440 | tf_op jit(solution)/shard_map/ppermute | solution.py:397
  30.4 0.7 copy-start.22
  33.0 11.2 %copy-start.5 = (bf16[512,256]{1,0:T(8,128)(2,1)S(1)}, bf16[512,256]{1,0:T(8,128)(2,1)}, u32[]{:S(2)}) copy-start(bf16[512,256]{1,0:T(8,128)(2,1)} %refs_0_.1) | copy-start | bytes 786436
  33.8 39.3 %all-to-all-start.1 = ((bf16[8,144,256]{2,1,0:T(8,128)(2,1)}), bf16[8,144,256]{2,1,0:T(8,128)(2,1)S(1)}, u32[]{:S(2)}, u32[]{:S(2)}) async-start(bf16[8,144,256]{2,1,0:T(8,128)(2,1)} %bitcast.12), calls=%async_computation.1 | async-start | bytes 1179648 | tf_op jit(solution)/shard_map/all_to_all | solution.py:419
  44.2 21.9 %collective-permute-start = (bf16[512,256]{1,0:T(8,128)(2,1)S(1)}, bf16[512,256]{1,0:T(8,128)(2,1)S(1)}, u32[]{:S(2)}, u32[]{:S(2)}) collective-permute-start(bf16[512,256]{1,0:T(8,128)(2,1)S(1)} %copy-done.5), channel_id=1, source_target_pairs={{0,1},{1,2},{2,3},{3,4},{4,5},{5,6},{6,7},{7,0},{8,9},{9,10},{10,1... | collective-permute-start | bytes 786440 | tf_op jit(solution)/shard_map/ppermute | solution.py:406
  48.1 19.9 %collective-permute-start.1 = (bf16[512,256]{1,0:T(8,128)(2,1)S(1)}, bf16[512,256]{1,0:T(8,128)(2,1)S(1)}, u32[]{:S(2)}, u32[]{:S(2)}) collective-permute-start(bf16[512,256]{1,0:T(8,128)(2,1)S(1)} %copy-done.5), channel_id=1, source_target_pairs={{0,7},{1,0},{2,1},{3,2},{4,3},{5,4},{6,5},{7,6},{8,15},{9,8},{10,9... | collective-permute-start | bytes 786440 | tf_op jit(solution)/shard_map/ppermute | solution.py:406
  66.0 22.8 %copy-start.6 = (bf16[512,256]{1,0:T(8,128)(2,1)}, bf16[512,256]{1,0:T(8,128)(2,1)S(1)}, u32[]{:S(2)}) copy-start(bf16[512,256]{1,0:T(8,128)(2,1)S(1)} %collective-permute-done.refs_1_) | copy-start | bytes 786436
  66.0 10.4 %collective-permute-start.2 = (bf16[512,256]{1,0:T(8,128)(2,1)S(1)}, bf16[512,256]{1,0:T(8,128)(2,1)S(1)}, u32[]{:S(2)}, u32[]{:S(2)}) collective-permute-start(bf16[512,256]{1,0:T(8,128)(2,1)S(1)} %collective-permute-done.refs_1_), channel_id=1, source_target_pairs={{0,1},{1,2},{2,3},{3,4},{4,5},{5,6},{6,7},{7,0},{8,9},{9,10},{10,1... | collective-permute-start | bytes 786440 | tf_op jit(solution)/shard_map/ppermute | solution.py:406
  68.0 20.9 %copy-start.8 = (bf16[512,256]{1,0:T(8,128)(2,1)}, bf16[512,256]{1,0:T(8,128)(2,1)S(1)}, u32[]{:S(2)}) copy-start(bf16[512,256]{1,0:T(8,128)(2,1)S(1)} %collective-permute-done.1.refs_2_) | copy-start | bytes 786436
  68.0 10.4 %collective-permute-start.3 = (bf16[512,256]{1,0:T(8,128)(2,1)S(1)}, bf16[512,256]{1,0:T(8,128)(2,1)S(1)}, u32[]{:S(2)}, u32[]{:S(2)}) collective-permute-start(bf16[512,256]{1,0:T(8,128)(2,1)S(1)} %collective-permute-done.1.refs_2_), channel_id=1, source_target_pairs={{0,7},{1,0},{2,1},{3,2},{4,3},{5,4},{6,5},{7,6},{8,15},{9,8},{10,9... | collective-permute-start | bytes 786440 | tf_op jit(solution)/shard_map/ppermute | solution.py:406
  73.1 23.5 %collective-permute-start.13 = (bf16[8,144,256]{2,1,0:T(8,128)(2,1)S(1)}, bf16[8,144,256]{2,1,0:T(8,128)(2,1)S(1)}, u32[]{:S(2)}, u32[]{:S(2)}) collective-permute-start(bf16[8,144,256]{2,1,0:T(8,128)(2,1)S(1)} %all-to-all-done.1.wo_ref), channel_id=1, source_target_pairs={{0,32},{32,0},{1,33},{33,1},{2,34},{34,2},{3,35},{35,3},{4,36},{36... | collective-permute-start | bytes 1769480 | tf_op jit(solution)/shard_map/ppermute | solution.py:420
  76.5 10.4 %collective-permute-start.4 = (bf16[512,256]{1,0:T(8,128)(2,1)S(1)}, bf16[512,256]{1,0:T(8,128)(2,1)S(1)}, u32[]{:S(2)}, u32[]{:S(2)}) collective-permute-start(bf16[512,256]{1,0:T(8,128)(2,1)S(1)} %collective-permute-done.2.refs_1_), channel_id=1, source_target_pairs={{0,1},{1,2},{2,3},{3,4},{4,5},{5,6},{6,7},{7,0},{8,9},{9,10},{10,1... | collective-permute-start | bytes 786440 | tf_op jit(solution)/shard_map/ppermute | solution.py:406
  78.4 10.4 %collective-permute-start.5 = (bf16[512,256]{1,0:T(8,128)(2,1)S(1)}, bf16[512,256]{1,0:T(8,128)(2,1)S(1)}, u32[]{:S(2)}, u32[]{:S(2)}) collective-permute-start(bf16[512,256]{1,0:T(8,128)(2,1)S(1)} %collective-permute-done.3.refs_2_), channel_id=1, source_target_pairs={{0,7},{1,0},{2,1},{3,2},{4,3},{5,4},{6,5},{7,6},{8,15},{9,8},{10,9... | collective-permute-start | bytes 786440 | tf_op jit(solution)/shard_map/ppermute | solution.py:406
  86.9 9.4 %collective-permute-start.6 = (bf16[256,256]{1,0:T(8,128)(2,1)S(1)}, bf16[256,256]{1,0:T(8,128)(2,1)S(1)}, u32[]{:S(2)}, u32[]{:S(2)}) collective-permute-start(bf16[256,256]{1,0:T(8,128)(2,1)S(1)} %slice.20), channel_id=1, source_target_pairs={{0,1},{1,2},{2,3},{3,4},{4,5},{5,6},{6,7},{7,0},{8,9},{9,10},{10,1... | collective-permute-start | bytes 393224 | tf_op jit(solution)/shard_map/ppermute | solution.py:409
  88.9 7.6 %collective-permute-start.7 = (bf16[256,256]{1,0:T(8,128)(2,1)S(1)}, bf16[256,256]{1,0:T(8,128)(2,1)S(1)}, u32[]{:S(2)}, u32[]{:S(2)}) collective-permute-start(bf16[256,256]{1,0:T(8,128)(2,1)S(1)} %slice.21), channel_id=1, source_target_pairs={{0,7},{1,0},{2,1},{3,2},{4,3},{5,4},{6,5},{7,6},{8,15},{9,8},{10,9... | collective-permute-start | bytes 393224 | tf_op jit(solution)/shard_map/ppermute | solution.py:410
  94.0 1.0 copy-start.7
  95.0 0.9 copy-start.9
  98.9 7.2 %copy-start.10 = (f32[4,3,2048]{2,0,1:T(4,128)S(1)}, f32[4,3,2048]{2,0,1:T(4,128)}, u32[]{:S(2)}) copy-start(f32[4,3,2048]{2,0,1:T(4,128)} %param.28) | copy-start | bytes 294916
  98.9 7.2 %copy-start.12 = (s32[16,4]{0,1:T(4,128)S(1)}, s32[16,4]{0,1:T(4,128)}, u32[]{:S(2)}) copy-start(s32[16,4]{0,1:T(4,128)} %param.30) | copy-start | bytes 772
  98.9 7.2 %copy-start.15 = (f32[4,3,256]{2,0,1:T(4,128)S(1)}, f32[4,3,256]{2,0,1:T(4,128)}, u32[]{:S(2)}) copy-start(f32[4,3,256]{2,0,1:T(4,128)} %param.27) | copy-start | bytes 36868
  98.9 22.0 %all-to-all-start.2 = ((f32[4,72,512]{2,1,0:T(8,128)}), f32[4,72,512]{2,1,0:T(8,128)S(1)}, u32[]{:S(2)}, u32[]{:S(2)}) async-start(f32[4,72,512]{2,1,0:T(8,128)} %bitcast.13), calls=%async_computation.2 | async-start | bytes 1179648 | tf_op jit(solution)/shard_map/all_to_all | solution.py:448
  106.1 1.2 copy-start.4
  108.5 1.4 copy-start.3
  109.9 42.3 %copy-start.11 = (f32[4,2048]{1,0:T(4,128)S(1)}, f32[4,2048]{1,0:T(4,128)}, u32[]{:S(2)}) copy-start(f32[4,2048]{1,0:T(4,128)} %taps_ref.3) | copy-start | bytes 98308
  109.9 42.3 %copy-start.13 = (s32[16,4]{0,1:T(4,128)S(1)}, s32[16,4]{0,1:T(4,128)}, u32[]{:S(2)}) copy-start(s32[16,4]{0,1:T(4,128)} %param.31) | copy-start | bytes 772
  109.9 42.3 %copy-start.16 = (f32[2048]{0:T(1024)S(1)}, f32[2048]{0:T(1024)}, u32[]{:S(2)}) copy-start(f32[2048]{0:T(1024)} %param.22) | copy-start | bytes 24580
  152.3 1.4 copy-start
  154.5 31.2 %all-to-all-start.3 = ((bf16[8,64,512]{2,1,0:T(8,128)(2,1)}), bf16[8,64,512]{2,1,0:T(8,128)(2,1)S(1)}, u32[]{:S(2)}, u32[]{:S(2)}) async-start(bf16[8,64,512]{2,1,0:T(8,128)(2,1)} %broadcast_in_dim.2), calls=%async_computation.3 | async-start | bytes 1048576 | tf_op jit(solution)/shard_map/all_to_all | solution.py:458
  161.3 11.7 %collective-permute-start.9 = (bf16[256,256]{1,0:T(8,128)(2,1)S(1)}, bf16[256,256]{1,0:T(8,128)(2,1)S(1)}, u32[]{:S(2)}, u32[]{:S(2)}) collective-permute-start(bf16[256,256]{1,0:T(8,128)(2,1)S(1)} %get-tuple-element.14), channel_id=1, source_target_pairs={{0,8},{8,16},{16,24},{24,0},{1,9},{9,17},{17,25},{25,1},{2,10},{10... | collective-permute-start | bytes 393224 | tf_op jit(solution)/shard_map/ppermute | solution.py:466
  165.3 13.0 %collective-permute-start.11 = (bf16[256,256]{1,0:T(8,128)(2,1)S(1)}, bf16[256,256]{1,0:T(8,128)(2,1)S(1)}, u32[]{:S(2)}, u32[]{:S(2)}) collective-permute-start(bf16[256,256]{1,0:T(8,128)(2,1)S(1)} %get-tuple-element.15), channel_id=1, source_target_pairs={{0,24},{8,0},{16,8},{24,16},{1,25},{9,1},{17,9},{25,17},{2,26},{10... | collective-permute-start | bytes 393224 | tf_op jit(solution)/shard_map/ppermute | solution.py:467
  174.9 10.8 %copy-start.14 = (f32[4,256]{1,0:T(4,128)S(1)}, f32[4,256]{1,0:T(4,128)}, u32[]{:S(2)}) copy-start(f32[4,256]{1,0:T(4,128)} %taps_ref.5) | copy-start | bytes 12292
  175.0 10.8 %copy-start.18 = (f32[4]{0:T(128)S(1)}, f32[4]{0:T(128)}, u32[]{:S(2)}) copy-start(f32[4]{0:T(128)} %rate_ref.1) | copy-start | bytes 52
  175.0 10.8 %copy-start.19 = (f32[4]{0:T(128)S(1)}, f32[4]{0:T(128)}, u32[]{:S(2)}) copy-start(f32[4]{0:T(128)} %bias_ref.1) | copy-start | bytes 52
  175.0 17.8 %collective-permute-start.10 = (bf16[512,256]{1,0:T(8,128)(2,1)S(1)}, bf16[512,256]{1,0:T(8,128)(2,1)S(1)}, u32[]{:S(2)}, u32[]{:S(2)}) collective-permute-start(bf16[512,256]{1,0:T(8,128)(2,1)S(1)} %shard_map.169), channel_id=1, source_target_pairs={{0,8},{8,16},{16,24},{24,0},{1,9},{9,17},{17,25},{25,1},{2,10},{10... | collective-permute-start | bytes 786440 | tf_op jit(solution)/shard_map/ppermute | solution.py:473
  180.9 14.1 %collective-permute-start.12 = (bf16[512,256]{1,0:T(8,128)(2,1)}, bf16[512,256]{1,0:T(8,128)(2,1)S(1)}, u32[]{:S(2)}, u32[]{:S(2)}) collective-permute-start(bf16[512,256]{1,0:T(8,128)(2,1)} %shard_map.170), channel_id=1, source_target_pairs={{0,24},{8,0},{16,8},{24,16},{1,25},{9,1},{17,9},{25,17},{2,26},{10... | collective-permute-start | bytes 786440 | tf_op jit(solution)/shard_map/ppermute | solution.py:478
  185.8 1.6 copy-start.1
  190.6 4.5 %copy-start.2 = (bf16[16,272,256]{2,1,0:T(8,128)(2,1)S(1)}, bf16[16,272,256]{2,1,0:T(8,128)(2,1)}, u32[]{:S(2)}) copy-start(bf16[16,272,256]{2,1,0:T(8,128)(2,1)} %copy-done) | copy-start | bytes 6684676
  190.6 4.4 %copy-start.17 = (f32[256]{0:T(256)S(1)}, f32[256]{0:T(256)}, u32[]{:S(2)}) copy-start(f32[256]{0:T(256)} %param.20) | copy-start | bytes 3076
  190.7 4.4 %copy-start.20 = (s32[16]{0:T(128)S(1)}, s32[16]{0:T(128)}, u32[]{:S(2)}) copy-start(s32[16]{0:T(128)} %count_ref.1) | copy-start | bytes 196
  190.7 4.4 %copy-start.21 = (f32[4]{0:T(128)S(1)}, f32[4]{0:T(128)}, u32[]{:S(2)}) copy-start(f32[4]{0:T(128)} %skip_ref.1) | copy-start | bytes 52
Sparse Core Ops, SparseCore 0:
  31.2 45.9 all-gather.2

commit v3 on v2

--- a/solution.py
+++ b/solution.py
@@ -14,11 +14,10 @@
 HEAD_DEV = 4
 P_SIZE = 64
 REQ = 4
-GROUPS = 16
 GROUP = ("x", "ylo", "core")
 SHARD = ("yhi", "z")
 SMALL = 72
-PAY = 272
+BLOCK = 576
 
 
 bf16 = jnp.bfloat16
@@ -60,11 +59,6 @@
     return starts, ends
 
 
-def owners(src_ref):
-    group = group_index()
-    return [src_ref[k, group] >> 2 for k in range(REQ)]
-
-
 def bc_lanes(read):
     yhi, z = lax.axis_index("yhi"), lax.axis_index("z")
     block, offset = yhi * 2 + (z >> 2), (z & 3) * 32
@@ -115,16 +109,8 @@
     return out
 
 
-def slot_for(src_ref, target):
-    group = group_index()
-    slot = jnp.int32(0)
-    for k in range(REQ):
-        place = src_ref[k, target]
-        slot = jnp.where((place >> 2) == group, place & 3, slot)
-    return slot
-
-
-def pack_kernel(src_ref, state_ref, x_ref, bc_ref, out_ref, tmp_ref):
+def panel_kernel(w_ref, x_ref, bc_ref, out_ref):
+    out_ref[:TOK, :] = w_ref[...]
     row = iota((16, CHAN), 0)
     wide = [
         bc_lanes(lambda block, i=i: bc_ref[i, :, pl.ds(pl.multiple_of(block * 128, 128), 128)])
@@ -136,13 +122,31 @@
             value = jnp.where(row == i, x_ref[i, slot : slot + 1, :], value)
             line = jnp.concatenate([wide[i][slot : slot + 1], jnp.zeros((1, 128), f32)], axis=1)
             value = jnp.where(row == 3 + i, line, value)
-        tmp_ref[slot] = value.astype(bf16)
-
-    @pl.loop(0, GROUPS)
-    def _(i):
-        slot = slot_for(src_ref, i)
-        out_ref[i, :STATES, :] = state_ref[slot].astype(bf16)
-        out_ref[i, STATES:, :] = tmp_ref[slot]
+        out_ref[TOK + slot * 16 : TOK + (slot + 1) * 16, :] = value.astype(bf16)
+
+
+def collect_kernel(mine_ref, b0, b1, b2, b3, out_ref):
+    for k, ref in enumerate((b0, b1, b2, b3)):
+        out_ref[k] = ref[...]
+
+
+def collect(mine, value, rows, index, room):
+    specs = [
+        pl.BlockSpec((None, rows, CHAN), functools.partial(lambda k, i, m: index(m[k]), k))
+        for k in range(REQ)
+    ]
+    return pl.pallas_call(
+        collect_kernel,
+        grid_spec=pltpu.PrefetchScalarGridSpec(
+            num_scalar_prefetch=1,
+            grid=(1,),
+            in_specs=specs,
+            out_specs=pl.BlockSpec(memory_space=pltpu.VMEM),
+        ),
+        out_shape=array(bf16, REQ, rows, CHAN),
+        compiler_params=pltpu.CompilerParams(vmem_limit_bytes=room << 20),
+        cost_estimate=pl.CostEstimate(flops=0, bytes_accessed=1 << 20, transcendentals=0),
+    )(mine, value, value, value, value)
 
 
 def place_kernel(plan, count, *refs):
@@ -181,9 +185,8 @@
         out_ref[place] = lax.dot_general(cols, rows, NT, preferred_element_type=f32)
 
 
-def conv_kernel(starts_ref, src_ref, part_ref, served_ref, taps_ref, bias_ref, bc_ref, dt_ref):
+def conv_kernel(starts_ref, part_ref, tails_ref, taps_ref, bias_ref, bc_ref, dt_ref):
     starts, ends = bounds(starts_ref)
-    src = owners(src_ref)
     signal = part_ref[0] + part_ref[1] + part_ref[2] + part_ref[3]
     dt_ref[...] = signal[64:]
     signal = signal[:64]
@@ -192,7 +195,7 @@
     taps = [own_taps[i : i + 1] for i in range(4)]
     tails = []
     for k in range(REQ):
-        rows = served_ref[src[k], STATES:, :].astype(f32)
+        rows = tails_ref[k].astype(f32)
         tails.append([rows[3 + i : 4 + i, :128] for i in range(3)])
     table = jnp.concatenate(
         [
@@ -215,7 +218,8 @@
 
 
 def product(hz_ref, w_ref):
-    return jnp.dot(hz_ref[...], w_ref[...], preferred_element_type=f32)
+    panel = jnp.concatenate([w_ref[i, :TOK, :] for i in range(4)], axis=0)
+    return jnp.dot(hz_ref[...], panel, preferred_element_type=f32)
 
 
 def far_kernel(index_ref, hz_ref, w_ref, low_ref, high_ref):
@@ -237,7 +241,7 @@
 
 def partial(kernel, way, operands, outs):
     whole = pl.BlockSpec(memory_space=pltpu.VMEM)
-    block = pl.BlockSpec((None, 8 * CHAN, CHAN), lambda i, b: ((b[0] + way) & 3, 0, 0))
+    block = pl.BlockSpec((None, 4, BLOCK, CHAN), lambda i, b: ((b[0] + way) & 3, 0, 0, 0))
     index = lax.axis_index("yhi").astype(jnp.int32).reshape(1)
     return pl.pallas_call(
         kernel,
@@ -256,15 +260,14 @@
 
 
 def mixing_kernel(
-    starts_ref, src_ref, rate_ref, bias_ref, bc_ref, dt_ref, served_ref, taps_ref,
-    mix_ref, carry_ref, cols_ref, decay_ref, b_ref, tail_ref,
+    starts_ref, rate_ref, bias_ref, bc_ref, dt_ref, tails_ref, taps_ref,
+    mix_ref, c_ref, cols_ref, decay_ref, b_ref, tail_ref,
 ):
     starts, ends = bounds(starts_ref)
-    src = owners(src_ref)
     taps = [taps_ref[i : i + 1, :] for i in range(4)]
     tails = []
     for k in range(REQ):
-        rows = served_ref[src[k], STATES:, :].astype(f32)
+        rows = tails_ref[k].astype(f32)
         tails.append([rows[i : i + 1, :] for i in range(3)])
     table = tail_rows(tails, taps, 128, CHAN)
     onehot = first_tokens((TOK, 128), 0, starts, ends)
@@ -273,6 +276,7 @@
     c_rows = jnp.concatenate([bc_ref[s, 32:64, :] for s in range(8)], axis=0)
     b_ref[...] = b_rows
     c_cols = c_rows.astype(f32).T.astype(bf16)
+    c_ref[...] = c_cols
     scores = jnp.dot(c_cols, b_rows, preferred_element_type=f32)
 
     row = iota((8, TOK), 0)
@@ -304,18 +308,6 @@
     cols = jnp.concatenate([cum, carried_decay, weight, jnp.zeros((104, TOK), f32)], axis=0).T
     cols_ref[...] = cols
 
-    tok_c = iota((TOK, CHAN), 0)
-    lane = iota((TOK, CHAN), 1)
-    carry = jnp.zeros((TOK, CHAN), f32)
-    for k in range(REQ):
-        old = served_ref[src[k], :CHAN, :]
-        part = lax.dot_general(c_cols, old, NT, preferred_element_type=f32)
-        carry = jnp.where((tok_c >= starts[k]) & (tok_c < ends[k]), part, carry)
-    scale = jnp.zeros((TOK, CHAN), f32)
-    for h in range(HEAD_DEV):
-        scale = jnp.where(lane >= h * P_SIZE, cols[:, 8 + h : 9 + h], scale)
-    carry_ref[...] = carry * scale
-
     for b in range(4):
         low, width = b * 128, (b + 1) * 128
         tok_t = iota((128, width), 0) + low
@@ -330,11 +322,10 @@
 
 
 def output_kernel(
-    starts_ref, src_ref, count_ref, skip_ref, x0, x1, x2, served_ref, taps_ref, bias_ref,
-    mix_ref, carry_ref, cols_ref, decay_ref, b_ref, tail_ref, y_ref, state_ref,
+    starts_ref, count_ref, skip_ref, x0, x1, x2, served_ref, taps_ref, bias_ref,
+    mix_ref, c_ref, cols_ref, decay_ref, b_ref, tail_ref, y_ref, state_ref,
 ):
     starts, ends = bounds(starts_ref)
-    src = owners(src_ref)
     count = count_ref[group_index()]
     signal = x0[...] + x1[...].astype(f32) + x2[...].astype(f32)
     taps = [taps_ref[i : i + 1, :] for i in range(4)]
@@ -352,7 +343,14 @@
     skip = jnp.zeros((TOK, CHAN), f32)
     for h in range(HEAD_DEV):
         skip = jnp.where(lane >= h * P_SIZE, skip_ref[h], skip)
-    base = carry_ref[...] + skip * x_wide
+    carry = jnp.zeros((TOK, CHAN), f32)
+    scale = jnp.zeros((TOK, CHAN), f32)
+    for k in range(REQ):
+        part = lax.dot_general(c_ref[...], served_ref[k], NT, preferred_element_type=f32)
+        carry = jnp.where((tok >= starts[k]) & (tok < ends[k]), part, carry)
+    for h in range(HEAD_DEV):
+        scale = jnp.where(lane >= h * P_SIZE, cols_ref[:, 8 + h : 9 + h], scale)
+    base = carry * scale + skip * x_wide
     for b in range(4):
         low, width = b * 128, (b + 1) * 128
         total = base[low : low + 128]
@@ -381,7 +379,7 @@
         )
         for h in range(HEAD_DEV):
             lo, hi = h * P_SIZE, (h + 1) * P_SIZE
-            old = served_ref[src[k], lo:hi, :].astype(f32)
+            old = served_ref[k, lo:hi, :].astype(f32)
             new = decay_ref[k, h : h + 1, 0:1] * old + gained[lo:hi]
             state_ref[k, lo:hi, :] = jnp.where(k < count, new, 0.0)
 
@@ -391,11 +389,20 @@
     old_state, x_tail, bc_tail, req_count, req_source, req_start,
 ):
     core = lax.axis_index("core")
-    src, starts = req_source.T, req_start.T
+    starts = req_start.T
+    mine = lax.dynamic_index_in_dim(req_source, lax.axis_index(GROUP), 0, keepdims=False)
 
     swap = [(a * 4 + b, b * 4 + a) for a in range(4) for b in range(4)]
     w_swapped = lax.ppermute(w_x, ("x", "yhi"), swap)
-    w_all = lax.all_gather(w_swapped, GROUP, axis=0, tiled=False)
+    panel = call(
+        panel_kernel,
+        (),
+        (w_swapped, x_tail.transpose(1, 0, 2), bc_tail.transpose(1, 0, 2)),
+        array(bf16, BLOCK, CHAN),
+        moved=1 << 20,
+    )
+    w_all = lax.all_gather(panel, GROUP, axis=0, tiled=False)
+    tails = collect(mine, w_all, 16, lambda m: (m >> 2, 32 + (m & 3), 0), 55)
 
     up = [(i, (i + 1) % 8) for i in range(8)]
     down = [(i, (i - 1) % 8) for i in range(8)]
@@ -419,19 +426,9 @@
     w_cols = lax.all_to_all(w_cols, "z", 0, 0, tiled=True)
     w_other = lax.ppermute(w_cols, "core", [(0, 1), (1, 0)])
 
-    served = call(
-        pack_kernel,
-        (src,),
-        (
-            old_state.reshape(REQ, CHAN, STATES),
-            x_tail.transpose(1, 0, 2),
-            bc_tail.transpose(1, 0, 2),
-        ),
-        array(bf16, GROUPS, PAY, STATES),
-        moved=7 << 20,
-        scratch=[pltpu.VMEM((REQ, 16, CHAN), bf16)],
-    )
-    served = lax.all_to_all(served, GROUP, 0, 0, tiled=True)
+    states = old_state.reshape(REQ, CHAN, STATES).astype(bf16)
+    states = lax.all_gather(states, GROUP, axis=0, tiled=True)
+    served = collect(mine, states, CHAN, lambda m: (m, 0, 0), 53)
 
     hz = place_blocks(((0, 0), (-1, 0), (1, 0)), (hidden, blocks[1], blocks[4]))
     for step in (2, 3):
@@ -449,8 +446,8 @@
 
     bc_own, dt_raw = call(
         conv_kernel,
-        (starts, src),
-        (part_small, served, conv_bc, conv_bc_bias.reshape(16, 128)),
+        (starts,),
+        (part_small, tails, conv_bc, conv_bc_bias.reshape(16, 128)),
         (array(bf16, 64, TOK), array(f32, SMALL - 64, TOK)),
         flops=2 * 6 * 128 * 128 * 512,
         moved=1 << 20,
@@ -459,7 +456,7 @@
         jnp.broadcast_to(bc_own[None], (8, 64, TOK)), "z", 0, 0, tiled=True
     )
 
-    w_view = w_all.reshape(4, 8 * CHAN, CHAN)
+    w_view = w_all.reshape(4, 4, BLOCK, CHAN)
     ahead = [(i, (i + 1) % 4) for i in range(4)]
     back = [(i, (i - 1) % 4) for i in range(4)]
     low, high = partial(far_kernel, 2, (hz, w_view), (array(bf16, half, CHAN),) * 2)
@@ -479,11 +476,11 @@
 
     made = call(
         mixing_kernel,
-        (starts, src, rate, dt_bias),
-        (bc_all, dt_raw, served, conv_x),
+        (starts, rate, dt_bias),
+        (bc_all, dt_raw, tails, conv_x),
         (
             array(bf16, HEAD_DEV, TOK, TOK),
-            array(f32, TOK, CHAN),
+            array(bf16, TOK, STATES),
             array(f32, TOK, 128),
             array(f32, REQ, 8, 128),
             array(bf16, STATES, TOK),
@@ -495,7 +492,7 @@
     )
     y, state = call(
         output_kernel,
-        (starts, src, req_count, dskip),
+        (starts, req_count, dskip),
         (x0, x1, x2, served, conv_x, conv_x_bias.reshape(2, 128), *made),
         (array(bf16, TOK, CHAN), array(f32, REQ, 256, STATES)),
         flops=2 * 20 * 512 * 256 * 256,

time: 209 us -> 191 us (0.914)
  blocking collectives: 31.3 us -> 0 us
  waiting for transfers between devices: 54 us -> 63.5 us
  Pallas kernels: 20.2 us -> 24.2 us
  starting transfers between devices: 74.6 us -> 71.4 us
  other arithmetic: 0.06 us -> 2.23 us
    all_to_all x1 -> x0, blocking collectives: 31.3 us -> none  [layer(): served = lax.all_to_all(served, GROUP, 0, 0, tiled=True)]
    all_to_all x1, waiting for transfers between devices: 11 us -> 20.5 us  [layer(): lax.all_to_all(part_small.reshape(4, SMALL, TOK), 'yhi', 0, 0, tiled=True)]
    pallas_call x0 -> x2, Pallas kernels: none -> 3.83 us  [collect(): pl.pallas_call(collect_kernel, grid_spec=pltpu.PrefetchScalarGridSpec(num...]
    ppermute x1, waiting for transfers between devices: 0.01 us -> 3.02 us  [layer(): x1 = lax.ppermute(x1, 'yhi', ahead)]
    ppermute x1, waiting for transfers between devices: 3.74 us -> 1.14 us  [layer(): low = lax.ppermute(low, 'yhi', ahead)]
    ppermute x1, waiting for transfers between devices: 2.3 us -> 0.01 us  [layer(): x2 = lax.ppermute(x2, 'yhi', back)]
    convert_element_type x0 -> x1, other arithmetic: none -> 2.17 us  [layer(): states = old_state.reshape(REQ, CHAN, STATES).astype(bf16)]
    unnamed x47 -> x59, local copies, waits for them, and re-layouts: 8.79 us -> 8.97 us
  transfers between devices with their start and end apart: 18 -> 19, of which waited for: 8 -> 9; matrix products, arithmetic and copies ran while one was open for 2% -> 3% of each run, Pallas kernels for 8% -> 10%
where the time goes in v3:
time: 191 us; the launch traced here: 187 us
  starting transfers between devices  71.4 us (37%)
  waiting for transfers between devices  63.5 us (33%)
  Pallas kernels  24.2 us (13%)
  between operations  14.5 us (8%)
  local copies, waits for them, and re-layouts  11.5 us (6%)
  other arithmetic  2.23 us (1%)
    ppermute x6, starting transfers between devices, layer(): block = lax.ppermute(block, 'z', ring)  21.1 us
    all_to_all x1, waiting for transfers between devices, layer(): lax.all_to_all(part_small.reshape(4, SMALL, TOK), 'yhi', 0, 0, tiled=True)  20.5 us
    ppermute x6, waiting for transfers between devices, layer(): block = lax.ppermute(block, 'z', ring)  19.6 us
    ppermute x1, waiting for transfers between devices, layer(): w_swapped = lax.ppermute(w_x, ('x', 'yhi'), swap)  17.1 us
    pallas_call x5, Pallas kernels, call(): pl.pallas_call(kernel, in_specs=[smem] * len(scalars) + [whole] * len(ope...  11.3 us
    all_to_all x1, starting transfers between devices, layer(): w_cols = lax.all_to_all(w_cols, 'z', 0, 0, tiled=True)  10.3 us
    unnamed x59, local copies, waits for them, and re-layouts  8.97 us
    pallas_call x4, Pallas kernels, partial(): pl.pallas_call(kernel, grid_spec=pltpu.PrefetchScalarGridSpec(num_scalar_...  8.71 us
  transfers between devices with their start and end apart: 19, of which 9 were waited for; matrix products, arithmetic and copies ran while one was open for 3% of the time, Pallas kernels for 10%

profile of v3, /device:TPU:6, one launch (start us, length us, event | category | flops | bytes accessed | tf_op | source)
XLA Modules:
  0.0 187.4 jit_solution(94464708601157999)
XLA Ops:
  7.2 6.1 %collective-permute-start.8 = (bf16[512,256]{1,0:T(8,128)(2,1)}, bf16[512,256]{1,0:T(8,128)(2,1)S(1)}, u32[]{:S(2)}, u32[]{:S(2)}) collective-permute-start(bf16[512,256]{1,0:T(8,128)(2,1)} %param.17), channel_id=1, source_target_pairs={{0,0},{8,128},{16,256},{24,384},{128,8},{136,136},{144,264},{152,3... | collective-permute-start | bytes 786440 | tf_op jit(solution)/shard_map/ppermute | solution.py:396
  13.3 17.1 %collective-permute-done.8.w_ref = bf16[512,256]{1,0:T(8,128)(2,1)S(1)} collective-permute-done((bf16[512,256]{1,0:T(8,128)(2,1)}, bf16[512,256]{1,0:T(8,128)(2,1)S(1)}, u32[]{:S(2)}, u32[]{:S(2)}) %collective-permute-start.8) | collective-permute-done | bytes 262176 | tf_op jit(solution)/shard_map/ppermute | solution.py:396
  30.4 0.9 copy-done.16
  31.3 0.7 copy-done.18
  32.0 0.8 shard_map.167
  32.9 2.2 %convert_element_type.8 = bf16[4,4,64,256]{3,2,1,0:T(8,128)(2,1)} convert(f32[4,4,64,256]{3,2,1,0:T(8,128)} %param.26) | non-fusion elementwise | flops 262144 | bytes 1572864 | tf_op jit(solution)/shard_map/convert_element_type | solution.py:429
  36.0 0.9 copy.27
  36.9 10.3 %all-to-all-start = ((bf16[8,144,256]{2,1,0:T(8,128)(2,1)}), bf16[8,144,256]{2,1,0:T(8,128)(2,1)S(1)}, u32[]{:S(2)}, u32[]{:S(2)}) async-start(bf16[8,144,256]{2,1,0:T(8,128)(2,1)} %bitcast.11), calls=%async_computation | async-start | bytes 1179648 | tf_op jit(solution)/shard_map/all_to_all | solution.py:426
  47.2 3.9 %collective-permute-start = (bf16[512,256]{1,0:T(8,128)(2,1)S(1)}, bf16[512,256]{1,0:T(8,128)(2,1)S(1)}, u32[]{:S(2)}, u32[]{:S(2)}) collective-permute-start(bf16[512,256]{1,0:T(8,128)(2,1)S(1)} %copy-done.9), channel_id=1, source_target_pairs={{0,1},{1,2},{2,3},{3,4},{4,5},{5,6},{6,7},{7,0},{8,9},{9,10},{10,1... | collective-permute-start | bytes 786440 | tf_op jit(solution)/shard_map/ppermute | solution.py:413
  51.1 3.1 %collective-permute-start.1 = (bf16[512,256]{1,0:T(8,128)(2,1)S(1)}, bf16[512,256]{1,0:T(8,128)(2,1)S(1)}, u32[]{:S(2)}, u32[]{:S(2)}) collective-permute-start(bf16[512,256]{1,0:T(8,128)(2,1)S(1)} %copy-done.9), channel_id=1, source_target_pairs={{0,7},{1,0},{2,1},{3,2},{4,3},{5,4},{6,5},{7,6},{8,15},{9,8},{10,9... | collective-permute-start | bytes 786440 | tf_op jit(solution)/shard_map/ppermute | solution.py:413
  54.2 14.8 %collective-permute-done.refs_1_ = bf16[512,256]{1,0:T(8,128)(2,1)S(1)} collective-permute-done((bf16[512,256]{1,0:T(8,128)(2,1)S(1)}, bf16[512,256]{1,0:T(8,128)(2,1)S(1)}, u32[]{:S(2)}, u32[]{:S(2)}) %collective-permute-start) | collective-permute-done | bytes 262176 | tf_op jit(solution)/shard_map/ppermute | solution.py:413
  69.1 1.9 %collective-permute-start.2 = (bf16[512,256]{1,0:T(8,128)(2,1)S(1)}, bf16[512,256]{1,0:T(8,128)(2,1)S(1)}, u32[]{:S(2)}, u32[]{:S(2)}) collective-permute-start(bf16[512,256]{1,0:T(8,128)(2,1)S(1)} %collective-permute-done.refs_1_), channel_id=1, source_target_pairs={{0,1},{1,2},{2,3},{3,4},{4,5},{5,6},{6,7},{7,0},{8,9},{9,10},{10,1... | collective-permute-start | bytes 786440 | tf_op jit(solution)/shard_map/ppermute | solution.py:413
  71.0 5.1 %collective-permute-start.3 = (bf16[512,256]{1,0:T(8,128)(2,1)S(1)}, bf16[512,256]{1,0:T(8,128)(2,1)S(1)}, u32[]{:S(2)}, u32[]{:S(2)}) collective-permute-start(bf16[512,256]{1,0:T(8,128)(2,1)S(1)} %collective-permute-done.1.refs_2_), channel_id=1, source_target_pairs={{0,7},{1,0},{2,1},{3,2},{4,3},{5,4},{6,5},{7,6},{8,15},{9,8},{10,9... | collective-permute-start | bytes 786440 | tf_op jit(solution)/shard_map/ppermute | solution.py:413
  76.2 1.9 %collective-permute-start.13 = (bf16[8,144,256]{2,1,0:T(8,128)(2,1)S(1)}, bf16[8,144,256]{2,1,0:T(8,128)(2,1)S(1)}, u32[]{:S(2)}, u32[]{:S(2)}) collective-permute-start(bf16[8,144,256]{2,1,0:T(8,128)(2,1)S(1)} %all-to-all-done.wo_ref), channel_id=1, source_target_pairs={{0,32},{32,0},{1,33},{33,1},{2,34},{34,2},{3,35},{35,3},{4,36},{36... | collective-permute-start | bytes 1769480 | tf_op jit(solution)/shard_map/ppermute | solution.py:427
  78.1 1.4 collective-permute-done.2.refs_1_
  79.5 1.9 %collective-permute-start.4 = (bf16[512,256]{1,0:T(8,128)(2,1)S(1)}, bf16[512,256]{1,0:T(8,128)(2,1)S(1)}, u32[]{:S(2)}, u32[]{:S(2)}) collective-permute-start(bf16[512,256]{1,0:T(8,128)(2,1)S(1)} %collective-permute-done.2.refs_1_), channel_id=1, source_target_pairs={{0,1},{1,2},{2,3},{3,4},{4,5},{5,6},{6,7},{7,0},{8,9},{9,10},{10,1... | collective-permute-start | bytes 786440 | tf_op jit(solution)/shard_map/ppermute | solution.py:413
  81.4 5.1 %collective-permute-start.5 = (bf16[512,256]{1,0:T(8,128)(2,1)S(1)}, bf16[512,256]{1,0:T(8,128)(2,1)S(1)}, u32[]{:S(2)}, u32[]{:S(2)}) collective-permute-start(bf16[512,256]{1,0:T(8,128)(2,1)S(1)} %collective-permute-done.3.refs_2_), channel_id=1, source_target_pairs={{0,7},{1,0},{2,1},{3,2},{4,3},{5,4},{6,5},{7,6},{8,15},{9,8},{10,9... | collective-permute-start | bytes 786440 | tf_op jit(solution)/shard_map/ppermute | solution.py:413
  86.6 3.4 %collective-permute-done.4.refs_1_ = bf16[512,256]{1,0:T(8,128)(2,1)S(1)} collective-permute-done((bf16[512,256]{1,0:T(8,128)(2,1)S(1)}, bf16[512,256]{1,0:T(8,128)(2,1)S(1)}, u32[]{:S(2)}, u32[]{:S(2)}) %collective-permute-start.4) | collective-permute-done | bytes 262176 | tf_op jit(solution)/shard_map/ppermute | solution.py:413
  89.9 1.9 %collective-permute-start.6 = (bf16[256,256]{1,0:T(8,128)(2,1)S(1)}, bf16[256,256]{1,0:T(8,128)(2,1)S(1)}, u32[]{:S(2)}, u32[]{:S(2)}) collective-permute-start(bf16[256,256]{1,0:T(8,128)(2,1)S(1)} %slice.20), channel_id=1, source_target_pairs={{0,1},{1,2},{2,3},{3,4},{4,5},{5,6},{6,7},{7,0},{8,9},{9,10},{10,1... | collective-permute-start | bytes 393224 | tf_op jit(solution)/shard_map/ppermute | solution.py:416
  91.9 5.1 %collective-permute-start.7 = (bf16[256,256]{1,0:T(8,128)(2,1)S(1)}, bf16[256,256]{1,0:T(8,128)(2,1)S(1)}, u32[]{:S(2)}, u32[]{:S(2)}) collective-permute-start(bf16[256,256]{1,0:T(8,128)(2,1)S(1)} %slice.21), channel_id=1, source_target_pairs={{0,7},{1,0},{2,1},{3,2},{4,3},{5,4},{6,5},{7,6},{8,15},{9,8},{10,9... | collective-permute-start | bytes 393224 | tf_op jit(solution)/shard_map/ppermute | solution.py:417
  97.0 1.0 copy-done.11
  98.0 0.9 copy-done.13
  99.6 2.3 %shard_map.173 = f32[2,144,512]{2,1,0:T(8,128)} custom-call(bf16[512,2048]{1,0:T(8,128)(2,1)S(1)} %place_blocks.7.hz_ref, bf16[8,144,256]{2,1,0:T(8,128)(2,1)S(1)} %all-to-all-done.wo_ref, bf16[8,144,256]{2,1,0:T(8,128)(2,1)S(1)} %collective-permute-done.13.wx_ref), custom_call_target="tpu_custom_call" | custom-call | flops 603979776 | bytes 4194304 | tf_op jit(solution)/shard_map/pallas_call | solution.py:36
  101.9 7.1 %all-to-all-start.1 = ((f32[4,72,512]{2,1,0:T(8,128)}), f32[4,72,512]{2,1,0:T(8,128)S(1)}, u32[]{:S(2)}, u32[]{:S(2)}) async-start(f32[4,72,512]{2,1,0:T(8,128)} %bitcast.12), calls=%async_computation.1 | async-start | bytes 1179648 | tf_op jit(solution)/shard_map/all_to_all | solution.py:445
  109.0 0.8 dynamic-slice_reduce_fusion.mine_ref
  109.8 2.2 %shard_map.174.tails_ref = bf16[4,16,256]{2,1,0:T(8,128)(2,1)} custom-call(s32[4]{0:T(128)} %dynamic-slice_reduce_fusion.mine_ref, bf16[16,576,256]{2,1,0:T(8,128)(2,1)} %bitcast.24, bf16[16,576,256]{2,1,0:T(8,128)(2,1)} %bitcast.25, bf16[16,576,256]{2,1,0:T(8,128)(2,1)} %bitcast.26, bf16[16,576,256]{2,1,0:T(8,128)(2,1)} %bitcast.27), custom_call_target="tpu_custom_call" | custom-call | bytes 1048576 | tf_op jit(solution)/shard_map/pallas_call | solution.py:138
  112.0 20.5 %all-to-all-done.1.part_ref = f32[4,72,512]{2,1,0:T(8,128)S(1)} async-done(((f32[4,72,512]{2,1,0:T(8,128)}), f32[4,72,512]{2,1,0:T(8,128)S(1)}, u32[]{:S(2)}, u32[]{:S(2)}) %all-to-all-start.1) | async-done | bytes 589856 | tf_op jit(solution)/shard_map/all_to_all | solution.py:445
  132.5 0.7 copy-done.14
  133.3 1.1 shard_map.175
  134.4 0.8 broadcast_in_dim.2
  135.2 5.2 %all-to-all-start.2 = ((bf16[8,64,512]{2,1,0:T(8,128)(2,1)}), bf16[8,64,512]{2,1,0:T(8,128)(2,1)S(1)}, u32[]{:S(2)}, u32[]{:S(2)}) async-start(bf16[8,64,512]{2,1,0:T(8,128)(2,1)} %broadcast_in_dim.2), calls=%async_computation.2 | async-start | bytes 1048576 | tf_op jit(solution)/shard_map/all_to_all | solution.py:455
  140.4 2.0 %shard_map.169 = (bf16[256,256]{1,0:T(8,128)(2,1)S(1)}, bf16[256,256]{1,0:T(8,128)(2,1)S(1)}) custom-call(s32[1]{0:T(128)} %bitcast.1.index_ref, bf16[512,2048]{1,0:T(8,128)(2,1)S(1)} %place_blocks.7.hz_ref, bf16[4,4,576,256]{3,2,1,0:T(8,128)(2,1)} %bitcast.28), custom_call_target="tpu_custom_call" | custom-call | flops 536870912 | bytes 3145728 | tf_op jit(solution)/shard_map/pallas_call | solution.py:246
  142.5 2.1 %collective-permute-start.11 = (bf16[256,256]{1,0:T(8,128)(2,1)S(1)}, bf16[256,256]{1,0:T(8,128)(2,1)S(1)}, u32[]{:S(2)}, u32[]{:S(2)}) collective-permute-start(bf16[256,256]{1,0:T(8,128)(2,1)S(1)} %get-tuple-element.15), channel_id=1, source_target_pairs={{0,24},{8,0},{16,8},{24,16},{1,25},{9,1},{17,9},{25,17},{2,26},{10... | collective-permute-start | bytes 393224 | tf_op jit(solution)/shard_map/ppermute | solution.py:464
  144.6 4.6 %collective-permute-start.9 = (bf16[256,256]{1,0:T(8,128)(2,1)S(1)}, bf16[256,256]{1,0:T(8,128)(2,1)S(1)}, u32[]{:S(2)}, u32[]{:S(2)}) collective-permute-start(bf16[256,256]{1,0:T(8,128)(2,1)S(1)} %get-tuple-element.14), channel_id=1, source_target_pairs={{0,8},{8,16},{16,24},{24,0},{1,9},{9,17},{17,25},{25,1},{2,10},{10... | collective-permute-start | bytes 393224 | tf_op jit(solution)/shard_map/ppermute | solution.py:463
  149.2 1.9 %collective-permute-done.11.add_ref = bf16[256,256]{1,0:T(8,128)(2,1)S(1)} collective-permute-done((bf16[256,256]{1,0:T(8,128)(2,1)S(1)}, bf16[256,256]{1,0:T(8,128)(2,1)S(1)}, u32[]{:S(2)}, u32[]{:S(2)}) %collective-permute-start.11) | collective-permute-done | bytes 131104 | tf_op jit(solution)/shard_map/ppermute | solution.py:464
  151.1 2.0 %shard_map.171 = bf16[512,256]{1,0:T(8,128)(2,1)S(1)} custom-call(s32[1]{0:T(128)} %bitcast.1.index_ref, bf16[512,2048]{1,0:T(8,128)(2,1)S(1)} %place_blocks.7.hz_ref, bf16[4,4,576,256]{3,2,1,0:T(8,128)(2,1)} %bitcast.29, bf16[256,256]{1,0:T(8,128)(2,1)S(1)} %collective-permute-done.11.add_ref), custom_call_target="tpu_custom_call" | custom-call | flops 536870912 | bytes 3145728 | tf_op jit(solution)/shard_map/pallas_call | solution.py:246
  153.1 3.5 %collective-permute-start.12 = (bf16[512,256]{1,0:T(8,128)(2,1)S(1)}, bf16[512,256]{1,0:T(8,128)(2,1)}, u32[]{:S(2)}, u32[]{:S(2)}) collective-permute-start(bf16[512,256]{1,0:T(8,128)(2,1)S(1)} %shard_map.171), channel_id=1, source_target_pairs={{0,24},{8,0},{16,8},{24,16},{1,25},{9,1},{17,9},{25,17},{2,26},{10... | collective-permute-start | bytes 786440 | tf_op jit(solution)/shard_map/ppermute | solution.py:475
  156.6 1.1 collective-permute-done.9.add_ref
  157.8 2.7 %shard_map.170 = bf16[512,256]{1,0:T(8,128)(2,1)} custom-call(s32[1]{0:T(128)} %bitcast.1.index_ref, bf16[512,2048]{1,0:T(8,128)(2,1)S(1)} %place_blocks.7.hz_ref, bf16[4,4,576,256]{3,2,1,0:T(8,128)(2,1)} %bitcast.30, bf16[256,256]{1,0:T(8,128)(2,1)S(1)} %collective-permute-done.9.add_ref), custom_call_target="tpu_custom_call" | custom-call | flops 536870912 | bytes 3145728 | tf_op jit(solution)/shard_map/pallas_call | solution.py:246
  160.5 2.3 %collective-permute-start.10 = (bf16[512,256]{1,0:T(8,128)(2,1)}, bf16[512,256]{1,0:T(8,128)(2,1)}, u32[]{:S(2)}, u32[]{:S(2)}) collective-permute-start(bf16[512,256]{1,0:T(8,128)(2,1)} %shard_map.170), channel_id=1, source_target_pairs={{0,8},{8,16},{16,24},{24,0},{1,9},{9,17},{17,25},{25,1},{2,10},{10... | collective-permute-start | bytes 786440 | tf_op jit(solution)/shard_map/ppermute | solution.py:470
  162.8 2.0 %shard_map.168.x0 = f32[512,256]{1,0:T(8,128)S(1)} custom-call(s32[1]{0:T(128)} %bitcast.1.index_ref, bf16[512,2048]{1,0:T(8,128)(2,1)S(1)} %place_blocks.7.hz_ref, bf16[4,4,576,256]{3,2,1,0:T(8,128)(2,1)} %bitcast.31), custom_call_target="tpu_custom_call" | custom-call | flops 536870912 | bytes 3145728 | tf_op jit(solution)/shard_map/pallas_call | solution.py:246
  164.8 0.8 copy-done.1
  165.6 1.0 copy-done.2
  166.7 2.7 %shard_map.176 = (bf16[4,512,512]{2,1,0:T(8,128)(2,1)S(1)}, bf16[512,256]{1,0:T(8,128)(2,1)S(1)}, f32[512,128]{1,0:T(8,128)S(1)}, f32[4,8,128]{2,1,0:T(8,128)S(1...) custom-call(s32[4,16]{1,0:T(4,128)S(1)} %bitcast.20, f32[4]{0:T(128)S(1)} %copy-done.26, f32[4]{0:T(128)S(1)} %copy-done.27, ...), custom_call_target="tpu_custom_call" | custom-call | flops 536870912 | bytes 12582912 | tf_op jit(solution)/shard_map/pallas_call | solution.py:36
  170.1 0.7 copy-done.5
  171.5 1.7 shard_map.172.served_ref
  173.2 3.0 %collective-permute-done.10.x1 = bf16[512,256]{1,0:T(8,128)(2,1)} collective-permute-done((bf16[512,256]{1,0:T(8,128)(2,1)}, bf16[512,256]{1,0:T(8,128)(2,1)}, u32[]{:S(2)}, u32[]{:S(2)}) %collective-permute-start.10) | collective-permute-done | bytes 262176 | tf_op jit(solution)/shard_map/ppermute | solution.py:470
  176.3 4.3 %shard_map.177 = (bf16[512,256]{1,0:T(8,128)(2,1)}, f32[4,256,256]{2,1,0:T(8,128)}) custom-call(s32[4,16]{1,0:T(4,128)S(1)} %bitcast.21, s32[16]{0:T(128)S(1)} %copy-done.24, f32[4]{0:T(128)S(1)} %copy-done.25, f32[512,256]{1,0:T(8,128)S(1)} %shard_map.168.x0, bf16[512,256]{1,0:T(8,128)(2,1)} %collective-permute-done.10.x1, ...), custom_call_target="tpu_custom_call" | custom-call | flops 1342177280 | bytes 6291456 | tf_op jit(solution)/shard_map/pallas_call | solution.py:36
  (76 shorter events, 3.1 us)
Async XLA Ops:
  7.2 101.9 %copy-start = (s32[16,4]{0,1:T(4,128)S(1)}, s32[16,4]{0,1:T(4,128)}, u32[]{:S(2)}) copy-start(s32[16,4]{0,1:T(4,128)} %param.30) | copy-start | bytes 772
  7.2 102.6 %all-gather.6.cloned.1.call-start = ((), (), s32[]{:S(2)}) async-start(), calls=%async_computation.4 | async-start | bytes 5013504 | tf_op jit(solution)/shard_map/all_gather | solution.py:404
  7.2 23.2 %collective-permute-start.8 = (bf16[512,256]{1,0:T(8,128)(2,1)}, bf16[512,256]{1,0:T(8,128)(2,1)S(1)}, u32[]{:S(2)}, u32[]{:S(2)}) collective-permute-start(bf16[512,256]{1,0:T(8,128)(2,1)} %param.17), channel_id=1, source_target_pairs={{0,0},{8,128},{16,256},{24,384},{128,8},{136,136},{144,264},{152,3... | collective-permute-start | bytes 786440 | tf_op jit(solution)/shard_map/ppermute | solution.py:396
  30.4 0.9 copy-start.16
  31.3 0.7 copy-start.18
  32.8 2.3 %copy-start.28 = (bf16[256,2176]{1,0:T(8,128)(2,1)S(1)}, bf16[256,2176]{1,0:T(8,128)(2,1)}, u32[]{:S(2)}) copy-start(bf16[256,2176]{1,0:T(8,128)(2,1)} %param.18) | copy-start | bytes 3342340
  32.8 138.6 %all-gather.4.cloned.1.call-start = ((), (), s32[]{:S(2)}) async-start(), calls=%async_computation.3 | async-start | bytes 8912896 | tf_op jit(solution)/shard_map/all_gather | solution.py:430
  36.0 11.2 %copy-start.9 = (bf16[512,256]{1,0:T(8,128)(2,1)S(1)}, bf16[512,256]{1,0:T(8,128)(2,1)}, u32[]{:S(2)}) copy-start(bf16[512,256]{1,0:T(8,128)(2,1)} %refs_0_.1) | copy-start | bytes 786436
  36.9 39.3 %all-to-all-start = ((bf16[8,144,256]{2,1,0:T(8,128)(2,1)}), bf16[8,144,256]{2,1,0:T(8,128)(2,1)S(1)}, u32[]{:S(2)}, u32[]{:S(2)}) async-start(bf16[8,144,256]{2,1,0:T(8,128)(2,1)} %bitcast.11), calls=%async_computation | async-start | bytes 1179648 | tf_op jit(solution)/shard_map/all_to_all | solution.py:426
  47.2 21.9 %collective-permute-start = (bf16[512,256]{1,0:T(8,128)(2,1)S(1)}, bf16[512,256]{1,0:T(8,128)(2,1)S(1)}, u32[]{:S(2)}, u32[]{:S(2)}) collective-permute-start(bf16[512,256]{1,0:T(8,128)(2,1)S(1)} %copy-done.9), channel_id=1, source_target_pairs={{0,1},{1,2},{2,3},{3,4},{4,5},{5,6},{6,7},{7,0},{8,9},{9,10},{10,1... | collective-permute-start | bytes 786440 | tf_op jit(solution)/shard_map/ppermute | solution.py:413
  51.1 19.9 %collective-permute-start.1 = (bf16[512,256]{1,0:T(8,128)(2,1)S(1)}, bf16[512,256]{1,0:T(8,128)(2,1)S(1)}, u32[]{:S(2)}, u32[]{:S(2)}) collective-permute-start(bf16[512,256]{1,0:T(8,128)(2,1)S(1)} %copy-done.9), channel_id=1, source_target_pairs={{0,7},{1,0},{2,1},{3,2},{4,3},{5,4},{6,5},{7,6},{8,15},{9,8},{10,9... | collective-permute-start | bytes 786440 | tf_op jit(solution)/shard_map/ppermute | solution.py:413
  69.1 22.8 %copy-start.10 = (bf16[512,256]{1,0:T(8,128)(2,1)}, bf16[512,256]{1,0:T(8,128)(2,1)S(1)}, u32[]{:S(2)}) copy-start(bf16[512,256]{1,0:T(8,128)(2,1)S(1)} %collective-permute-done.refs_1_) | copy-start | bytes 786436
  69.1 10.4 %collective-permute-start.2 = (bf16[512,256]{1,0:T(8,128)(2,1)S(1)}, bf16[512,256]{1,0:T(8,128)(2,1)S(1)}, u32[]{:S(2)}, u32[]{:S(2)}) collective-permute-start(bf16[512,256]{1,0:T(8,128)(2,1)S(1)} %collective-permute-done.refs_1_), channel_id=1, source_target_pairs={{0,1},{1,2},{2,3},{3,4},{4,5},{5,6},{6,7},{7,0},{8,9},{9,10},{10,1... | collective-permute-start | bytes 786440 | tf_op jit(solution)/shard_map/ppermute | solution.py:413
  71.0 20.9 %copy-start.12 = (bf16[512,256]{1,0:T(8,128)(2,1)}, bf16[512,256]{1,0:T(8,128)(2,1)S(1)}, u32[]{:S(2)}) copy-start(bf16[512,256]{1,0:T(8,128)(2,1)S(1)} %collective-permute-done.1.refs_2_) | copy-start | bytes 786436
  71.0 10.4 %collective-permute-start.3 = (bf16[512,256]{1,0:T(8,128)(2,1)S(1)}, bf16[512,256]{1,0:T(8,128)(2,1)S(1)}, u32[]{:S(2)}, u32[]{:S(2)}) collective-permute-start(bf16[512,256]{1,0:T(8,128)(2,1)S(1)} %collective-permute-done.1.refs_2_), channel_id=1, source_target_pairs={{0,7},{1,0},{2,1},{3,2},{4,3},{5,4},{6,5},{7,6},{8,15},{9,8},{10,9... | collective-permute-start | bytes 786440 | tf_op jit(solution)/shard_map/ppermute | solution.py:413
  76.2 23.5 %collective-permute-start.13 = (bf16[8,144,256]{2,1,0:T(8,128)(2,1)S(1)}, bf16[8,144,256]{2,1,0:T(8,128)(2,1)S(1)}, u32[]{:S(2)}, u32[]{:S(2)}) collective-permute-start(bf16[8,144,256]{2,1,0:T(8,128)(2,1)S(1)} %all-to-all-done.wo_ref), channel_id=1, source_target_pairs={{0,32},{32,0},{1,33},{33,1},{2,34},{34,2},{3,35},{35,3},{4,36},{36... | collective-permute-start | bytes 1769480 | tf_op jit(solution)/shard_map/ppermute | solution.py:427
  79.5 10.4 %collective-permute-start.4 = (bf16[512,256]{1,0:T(8,128)(2,1)S(1)}, bf16[512,256]{1,0:T(8,128)(2,1)S(1)}, u32[]{:S(2)}, u32[]{:S(2)}) collective-permute-start(bf16[512,256]{1,0:T(8,128)(2,1)S(1)} %collective-permute-done.2.refs_1_), channel_id=1, source_target_pairs={{0,1},{1,2},{2,3},{3,4},{4,5},{5,6},{6,7},{7,0},{8,9},{9,10},{10,1... | collective-permute-start | bytes 786440 | tf_op jit(solution)/shard_map/ppermute | solution.py:413
  81.4 10.4 %collective-permute-start.5 = (bf16[512,256]{1,0:T(8,128)(2,1)S(1)}, bf16[512,256]{1,0:T(8,128)(2,1)S(1)}, u32[]{:S(2)}, u32[]{:S(2)}) collective-permute-start(bf16[512,256]{1,0:T(8,128)(2,1)S(1)} %collective-permute-done.3.refs_2_), channel_id=1, source_target_pairs={{0,7},{1,0},{2,1},{3,2},{4,3},{5,4},{6,5},{7,6},{8,15},{9,8},{10,9... | collective-permute-start | bytes 786440 | tf_op jit(solution)/shard_map/ppermute | solution.py:413
  89.9 9.4 %collective-permute-start.6 = (bf16[256,256]{1,0:T(8,128)(2,1)S(1)}, bf16[256,256]{1,0:T(8,128)(2,1)S(1)}, u32[]{:S(2)}, u32[]{:S(2)}) collective-permute-start(bf16[256,256]{1,0:T(8,128)(2,1)S(1)} %slice.20), channel_id=1, source_target_pairs={{0,1},{1,2},{2,3},{3,4},{4,5},{5,6},{6,7},{7,0},{8,9},{9,10},{10,1... | collective-permute-start | bytes 393224 | tf_op jit(solution)/shard_map/ppermute | solution.py:416
  91.9 7.6 %collective-permute-start.7 = (bf16[256,256]{1,0:T(8,128)(2,1)S(1)}, bf16[256,256]{1,0:T(8,128)(2,1)S(1)}, u32[]{:S(2)}, u32[]{:S(2)}) collective-permute-start(bf16[256,256]{1,0:T(8,128)(2,1)S(1)} %slice.21), channel_id=1, source_target_pairs={{0,7},{1,0},{2,1},{3,2},{4,3},{5,4},{6,5},{7,6},{8,15},{9,8},{10,9... | collective-permute-start | bytes 393224 | tf_op jit(solution)/shard_map/ppermute | solution.py:417
  97.0 1.0 copy-start.11
  98.0 0.9 copy-start.13
  101.9 30.6 %all-to-all-start.1 = ((f32[4,72,512]{2,1,0:T(8,128)}), f32[4,72,512]{2,1,0:T(8,128)S(1)}, u32[]{:S(2)}, u32[]{:S(2)}) async-start(f32[4,72,512]{2,1,0:T(8,128)} %bitcast.12), calls=%async_computation.1 | async-start | bytes 1179648 | tf_op jit(solution)/shard_map/all_to_all | solution.py:445
  109.8 22.7 %copy-start.17 = (f32[4,2048]{1,0:T(4,128)S(1)}, f32[4,2048]{1,0:T(4,128)}, u32[]{:S(2)}) copy-start(f32[4,2048]{1,0:T(4,128)} %taps_ref.3) | copy-start | bytes 98308
  109.8 22.7 %copy-start.19 = (s32[16,4]{0,1:T(4,128)S(1)}, s32[16,4]{0,1:T(4,128)}, u32[]{:S(2)}) copy-start(s32[16,4]{0,1:T(4,128)} %param.31) | copy-start | bytes 772
  109.8 22.7 %copy-start.20 = (f32[2048]{0:T(1024)S(1)}, f32[2048]{0:T(1024)}, u32[]{:S(2)}) copy-start(f32[2048]{0:T(1024)} %param.22) | copy-start | bytes 24580
  132.5 0.8 copy-start.14
  135.2 29.6 %all-to-all-start.2 = ((bf16[8,64,512]{2,1,0:T(8,128)(2,1)}), bf16[8,64,512]{2,1,0:T(8,128)(2,1)S(1)}, u32[]{:S(2)}, u32[]{:S(2)}) async-start(bf16[8,64,512]{2,1,0:T(8,128)(2,1)} %broadcast_in_dim.2), calls=%async_computation.2 | async-start | bytes 1048576 | tf_op jit(solution)/shard_map/all_to_all | solution.py:455
  142.5 8.7 %collective-permute-start.11 = (bf16[256,256]{1,0:T(8,128)(2,1)S(1)}, bf16[256,256]{1,0:T(8,128)(2,1)S(1)}, u32[]{:S(2)}, u32[]{:S(2)}) collective-permute-start(bf16[256,256]{1,0:T(8,128)(2,1)S(1)} %get-tuple-element.15), channel_id=1, source_target_pairs={{0,24},{8,0},{16,8},{24,16},{1,25},{9,1},{17,9},{25,17},{2,26},{10... | collective-permute-start | bytes 393224 | tf_op jit(solution)/shard_map/ppermute | solution.py:464
  144.6 13.1 %collective-permute-start.9 = (bf16[256,256]{1,0:T(8,128)(2,1)S(1)}, bf16[256,256]{1,0:T(8,128)(2,1)S(1)}, u32[]{:S(2)}, u32[]{:S(2)}) collective-permute-start(bf16[256,256]{1,0:T(8,128)(2,1)S(1)} %get-tuple-element.14), channel_id=1, source_target_pairs={{0,8},{8,16},{16,24},{24,0},{1,9},{9,17},{17,25},{25,1},{2,10},{10... | collective-permute-start | bytes 393224 | tf_op jit(solution)/shard_map/ppermute | solution.py:463
  153.1 20.1 %collective-permute-start.12 = (bf16[512,256]{1,0:T(8,128)(2,1)S(1)}, bf16[512,256]{1,0:T(8,128)(2,1)}, u32[]{:S(2)}, u32[]{:S(2)}) collective-permute-start(bf16[512,256]{1,0:T(8,128)(2,1)S(1)} %shard_map.171), channel_id=1, source_target_pairs={{0,24},{8,0},{16,8},{24,16},{1,25},{9,1},{17,9},{25,17},{2,26},{10... | collective-permute-start | bytes 786440 | tf_op jit(solution)/shard_map/ppermute | solution.py:475
  160.5 5.1 %copy-start.15 = (bf16[4,16,256]{2,1,0:T(8,128)(2,1)S(1)}, bf16[4,16,256]{2,1,0:T(8,128)(2,1)}, u32[]{:S(2)}) copy-start(bf16[4,16,256]{2,1,0:T(8,128)(2,1)} %shard_map.174.tails_ref) | copy-start | bytes 98308
  160.5 5.1 %copy-start.22 = (f32[4,256]{1,0:T(4,128)S(1)}, f32[4,256]{1,0:T(4,128)}, u32[]{:S(2)}) copy-start(f32[4,256]{1,0:T(4,128)} %taps_ref.5) | copy-start | bytes 12292
  160.5 5.1 %copy-start.26 = (f32[4]{0:T(128)S(1)}, f32[4]{0:T(128)}, u32[]{:S(2)}) copy-start(f32[4]{0:T(128)} %rate_ref.1) | copy-start | bytes 52
  160.5 5.1 %copy-start.27 = (f32[4]{0:T(128)S(1)}, f32[4]{0:T(128)}, u32[]{:S(2)}) copy-start(f32[4]{0:T(128)} %bias_ref.1) | copy-start | bytes 52
  160.5 15.8 %collective-permute-start.10 = (bf16[512,256]{1,0:T(8,128)(2,1)}, bf16[512,256]{1,0:T(8,128)(2,1)}, u32[]{:S(2)}, u32[]{:S(2)}) collective-permute-start(bf16[512,256]{1,0:T(8,128)(2,1)} %shard_map.170), channel_id=1, source_target_pairs={{0,8},{8,16},{16,24},{24,0},{1,9},{9,17},{17,25},{25,1},{2,10},{10... | collective-permute-start | bytes 786440 | tf_op jit(solution)/shard_map/ppermute | solution.py:470
  164.8 6.7 %copy-start.21 = (s32[4]{0:T(128)S(1)}, s32[4]{0:T(128)}, u32[]{:S(2)}) copy-start(s32[4]{0:T(128)} %dynamic-slice_reduce_fusion.mine_ref) | copy-start | bytes 52
  164.8 0.8 copy-start.1
  165.6 1.0 copy-start.2
  169.4 0.7 copy-start.3
  170.1 0.7 copy-start.5
  170.8 0.7 copy-start.7
  171.5 4.8 %copy-start.23 = (f32[256]{0:T(256)S(1)}, f32[256]{0:T(256)}, u32[]{:S(2)}) copy-start(f32[256]{0:T(256)} %param.20) | copy-start | bytes 3076
  171.5 4.8 %copy-start.24 = (s32[16]{0:T(128)S(1)}, s32[16]{0:T(128)}, u32[]{:S(2)}) copy-start(s32[16]{0:T(128)} %count_ref.1) | copy-start | bytes 196
  171.5 4.8 %copy-start.25 = (f32[4]{0:T(128)S(1)}, f32[4]{0:T(128)}, u32[]{:S(2)}) copy-start(f32[4]{0:T(128)} %skip_ref.1) | copy-start | bytes 52
  171.5 4.7 %copy-start.4 = (bf16[512,256]{1,0:T(8,128)(2,1)S(1)}, bf16[512,256]{1,0:T(8,128)(2,1)}, u32[]{:S(2)}) copy-start(bf16[512,256]{1,0:T(8,128)(2,1)} %copy-done.3) | copy-start | bytes 786436
  171.5 4.7 %copy-start.6 = (f32[512,128]{1,0:T(8,128)S(1)}, f32[512,128]{1,0:T(8,128)}, u32[]{:S(2)}) copy-start(f32[512,128]{1,0:T(8,128)} %copy-done.5) | copy-start | bytes 786436
  171.5 4.7 %copy-start.8 = (bf16[256,512]{1,0:T(8,128)(2,1)S(1)}, bf16[256,512]{1,0:T(8,128)(2,1)}, u32[]{:S(2)}) copy-start(bf16[256,512]{1,0:T(8,128)(2,1)} %copy-done.7) | copy-start | bytes 786436
Sparse Core Ops, SparseCore 0:
  33.0 46.4 all-gather.5
  81.6 80.8 all-gather.3

commit v4 on v3

--- a/solution.py
+++ b/solution.py
@@ -14,10 +14,12 @@
 HEAD_DEV = 4
 P_SIZE = 64
 REQ = 4
+GROUPS = 16
 GROUP = ("x", "ylo", "core")
 SHARD = ("yhi", "z")
 SMALL = 72
 BLOCK = 576
+SPLIT = 192
 
 
 bf16 = jnp.bfloat16
@@ -107,6 +109,21 @@
             hit = (place == d * REQ + k) & (tok == starts[k] + d) & (tok < ends[k])
             out = jnp.where(hit, 1.0, out)
     return out
+
+
+def slot_for(src_ref, target):
+    group = group_index()
+    slot = jnp.int32(0)
+    for k in range(REQ):
+        place = src_ref[k, target]
+        slot = jnp.where((place >> 2) == group, place & 3, slot)
+    return slot
+
+
+def pack_kernel(src_ref, state_ref, out_ref):
+    @pl.loop(0, GROUPS)
+    def _(i):
+        out_ref[i] = state_ref[slot_for(src_ref, i), :SPLIT, :].astype(bf16)
 
 
 def panel_kernel(w_ref, x_ref, bc_ref, out_ref):
@@ -214,7 +231,9 @@
     for j in range(1, 4):
         moved = jnp.where(tok - j >= begin, pltpu.roll(signal, j, 1), 0.0)
         summed = summed + table[:64, 19 - j : 20 - j] * moved
-    bc_ref[...] = sigmoid_gate(summed).astype(bf16)
+    mine = sigmoid_gate(summed).astype(bf16)
+    for i in range(8):
+        bc_ref[i] = mine
 
 
 def product(hz_ref, w_ref):
@@ -322,7 +341,7 @@
 
 
 def output_kernel(
-    starts_ref, count_ref, skip_ref, x0, x1, x2, served_ref, taps_ref, bias_ref,
+    starts_ref, src_ref, count_ref, skip_ref, x0, x1, x2, early_ref, served_ref, taps_ref, bias_ref,
     mix_ref, c_ref, cols_ref, decay_ref, b_ref, tail_ref, y_ref, state_ref,
 ):
     starts, ends = bounds(starts_ref)
@@ -346,7 +365,10 @@
     carry = jnp.zeros((TOK, CHAN), f32)
     scale = jnp.zeros((TOK, CHAN), f32)
     for k in range(REQ):
-        part = lax.dot_general(c_ref[...], served_ref[k], NT, preferred_element_type=f32)
+        old = (early_ref[src_ref[k, group_index()] >> 2], served_ref[k])
+        part = jnp.concatenate(
+            [lax.dot_general(c_ref[...], v, NT, preferred_element_type=f32) for v in old], axis=1
+        )
         carry = jnp.where((tok >= starts[k]) & (tok < ends[k]), part, carry)
     for h in range(HEAD_DEV):
         scale = jnp.where(lane >= h * P_SIZE, cols_ref[:, 8 + h : 9 + h], scale)
@@ -379,7 +401,10 @@
         )
         for h in range(HEAD_DEV):
             lo, hi = h * P_SIZE, (h + 1) * P_SIZE
-            old = served_ref[k, lo:hi, :].astype(f32)
+            if hi <= SPLIT:
+                old = early_ref[src_ref[k, group_index()] >> 2, lo:hi, :].astype(f32)
+            else:
+                old = served_ref[k, lo - SPLIT : hi - SPLIT, :].astype(f32)
             new = decay_ref[k, h : h + 1, 0:1] * old + gained[lo:hi]
             state_ref[k, lo:hi, :] = jnp.where(k < count, new, 0.0)
 
@@ -389,7 +414,7 @@
     old_state, x_tail, bc_tail, req_count, req_source, req_start,
 ):
     core = lax.axis_index("core")
-    starts = req_start.T
+    src, starts = req_source.T, req_start.T
     mine = lax.dynamic_index_in_dim(req_source, lax.axis_index(GROUP), 0, keepdims=False)
 
     swap = [(a * 4 + b, b * 4 + a) for a in range(4) for b in range(4)]
@@ -426,9 +451,11 @@
     w_cols = lax.all_to_all(w_cols, "z", 0, 0, tiled=True)
     w_other = lax.ppermute(w_cols, "core", [(0, 1), (1, 0)])
 
-    states = old_state.reshape(REQ, CHAN, STATES).astype(bf16)
-    states = lax.all_gather(states, GROUP, axis=0, tiled=True)
-    served = collect(mine, states, CHAN, lambda m: (m, 0, 0), 53)
+    states = old_state.reshape(REQ, CHAN, STATES)
+    early = call(pack_kernel, (src,), (states,), array(bf16, GROUPS, SPLIT, STATES), moved=4 << 20)
+    early = lax.all_to_all(early, GROUP, 0, 0, tiled=True)
+    states = lax.all_gather(states[:, SPLIT:].astype(bf16), GROUP, axis=0, tiled=True)
+    served = collect(mine, states, CHAN - SPLIT, lambda m: (m, 0, 0), 55)
 
     hz = place_blocks(((0, 0), (-1, 0), (1, 0)), (hidden, blocks[1], blocks[4]))
     for step in (2, 3):
@@ -448,13 +475,11 @@
         conv_kernel,
         (starts,),
         (part_small, tails, conv_bc, conv_bc_bias.reshape(16, 128)),
-        (array(bf16, 64, TOK), array(f32, SMALL - 64, TOK)),
+        (array(bf16, 8, 64, TOK), array(f32, SMALL - 64, TOK)),
         flops=2 * 6 * 128 * 128 * 512,
         moved=1 << 20,
     )
-    bc_all = lax.all_to_all(
-        jnp.broadcast_to(bc_own[None], (8, 64, TOK)), "z", 0, 0, tiled=True
-    )
+    bc_all = lax.all_to_all(bc_own, "z", 0, 0, tiled=True)
 
     w_view = w_all.reshape(4, 4, BLOCK, CHAN)
     ahead = [(i, (i + 1) % 4) for i in range(4)]
@@ -492,8 +517,8 @@
     )
     y, state = call(
         output_kernel,
-        (starts, req_count, dskip),
-        (x0, x1, x2, served, conv_x, conv_x_bias.reshape(2, 128), *made),
+        (starts, src, req_count, dskip),
+        (x0, x1, x2, early, served, conv_x, conv_x_bias.reshape(2, 128), *made),
         (array(bf16, TOK, CHAN), array(f32, REQ, 256, STATES)),
         flops=2 * 20 * 512 * 256 * 256,
         moved=6 << 20,

time: 191 us -> 224 us (1.17)
  waiting for transfers between devices: 63.5 us -> 81.7 us
  local copies, waits for them, and re-layouts: 11.5 us -> 19.4 us
  starting transfers between devices: 71.4 us -> 79.2 us
  Pallas kernels: 24.2 us -> 26.8 us
    ppermute x1, waiting for transfers between devices: 1.14 us -> 21 us  [layer(): low = lax.ppermute(low, 'yhi', ahead)]
    all_to_all x1 -> x2, waiting for transfers between devices: 0.01 us -> 13.6 us  [the longest x1 13.6 us: layer(): bc_all = lax.all_to_all(bc_own, 'z', 0, 0, tiled=True)]
    all_to_all x1, waiting for transfers between devices: 20.5 us -> 10.2 us  [layer(): lax.all_to_all(part_small.reshape(4, SMALL, TOK), 'yhi', 0, 0, tiled=True)]
    unnamed x59 -> x67, local copies, waits for them, and re-layouts: 8.97 us -> 16.1 us
    all_to_all x1 -> x2, starting transfers between devices: 5.19 us -> 9.51 us  [the longest x1 4.98 us: layer(): bc_all = lax.all_to_all(bc_own, 'z', 0, 0, tiled=True)]
    ppermute x1, waiting for transfers between devices: 3.02 us -> 0.01 us  [layer(): x1 = lax.ppermute(x1, 'yhi', ahead)]
    pallas_call x5 -> x6, Pallas kernels: 11.3 us -> 13.4 us  [call(): pl.pallas_call(kernel, in_specs=[smem] * len(scalars) + [whole] * len(ope...]
  transfers between devices with their start and end apart: 19 -> 20, of which waited for: 9 -> 8; matrix products, arithmetic and copies ran while one was open for 3% -> 2% of each run, Pallas kernels for 10% -> 9%
where the time goes in v4:
time: 224 us; the launch traced here: 222 us
  waiting for transfers between devices  81.7 us (36%)
  starting transfers between devices  79.2 us (35%)
  Pallas kernels  26.8 us (12%)
  local copies, waits for them, and re-layouts  19.4 us (9%)
  between operations  14.6 us (7%)
    ppermute x6, starting transfers between devices, layer(): block = lax.ppermute(block, 'z', ring)  21.1 us
    ppermute x1, waiting for transfers between devices, layer(): low = lax.ppermute(low, 'yhi', ahead)  21 us
    ppermute x6, waiting for transfers between devices, layer(): block = lax.ppermute(block, 'z', ring)  19.6 us
    ppermute x1, waiting for transfers between devices, layer(): w_swapped = lax.ppermute(w_x, ('x', 'yhi'), swap)  17.1 us
    unnamed x67, local copies, waits for them, and re-layouts  16.1 us
    all_to_all x1, waiting for transfers between devices, layer(): bc_all = lax.all_to_all(bc_own, 'z', 0, 0, tiled=True)  13.6 us
    pallas_call x6, Pallas kernels, call(): pl.pallas_call(kernel, in_specs=[smem] * len(scalars) + [whole] * len(ope...  13.4 us
    all_to_all x1, starting transfers between devices, layer(): w_cols = lax.all_to_all(w_cols, 'z', 0, 0, tiled=True)  10.3 us
  transfers between devices with their start and end apart: 20, of which 8 were waited for; matrix products, arithmetic and copies ran while one was open for 2% of the time, Pallas kernels for 9%

profile of v4, /device:TPU:6, one launch (start us, length us, event | category | flops | bytes accessed | tf_op | source)
XLA Modules:
  0.0 221.7 jit_solution(18188115448917687073)
XLA Ops:
  7.2 6.1 %collective-permute-start.8 = (bf16[512,256]{1,0:T(8,128)(2,1)}, bf16[512,256]{1,0:T(8,128)(2,1)S(1)}, u32[]{:S(2)}, u32[]{:S(2)}) collective-permute-start(bf16[512,256]{1,0:T(8,128)(2,1)} %param.17), channel_id=1, source_target_pairs={{0,0},{8,128},{16,256},{24,384},{128,8},{136,136},{144,264},{152,3... | collective-permute-start | bytes 786440 | tf_op jit(solution)/shard_map/ppermute | solution.py:421
  13.3 17.1 %collective-permute-done.8.w_ref = bf16[512,256]{1,0:T(8,128)(2,1)S(1)} collective-permute-done((bf16[512,256]{1,0:T(8,128)(2,1)}, bf16[512,256]{1,0:T(8,128)(2,1)S(1)}, u32[]{:S(2)}, u32[]{:S(2)}) %collective-permute-start.8) | collective-permute-done | bytes 262176 | tf_op jit(solution)/shard_map/ppermute | solution.py:421
  30.4 0.9 copy-done.17
  32.0 0.8 shard_map.167
  32.8 1.7 copy.26
  34.7 0.9 copy.27
  35.5 10.3 %all-to-all-start.1 = ((bf16[8,144,256]{2,1,0:T(8,128)(2,1)}), bf16[8,144,256]{2,1,0:T(8,128)(2,1)S(1)}, u32[]{:S(2)}, u32[]{:S(2)}) async-start(bf16[8,144,256]{2,1,0:T(8,128)(2,1)} %bitcast.12), calls=%async_computation.1 | async-start | bytes 1179648 | tf_op jit(solution)/shard_map/all_to_all | solution.py:451
  45.8 3.9 %collective-permute-start = (bf16[512,256]{1,0:T(8,128)(2,1)S(1)}, bf16[512,256]{1,0:T(8,128)(2,1)S(1)}, u32[]{:S(2)}, u32[]{:S(2)}) collective-permute-start(bf16[512,256]{1,0:T(8,128)(2,1)S(1)} %copy-done.10), channel_id=1, source_target_pairs={{0,1},{1,2},{2,3},{3,4},{4,5},{5,6},{6,7},{7,0},{8,9},{9,10},{10,1... | collective-permute-start | bytes 786440 | tf_op jit(solution)/shard_map/ppermute | solution.py:438
  49.8 3.1 %collective-permute-start.1 = (bf16[512,256]{1,0:T(8,128)(2,1)S(1)}, bf16[512,256]{1,0:T(8,128)(2,1)S(1)}, u32[]{:S(2)}, u32[]{:S(2)}) collective-permute-start(bf16[512,256]{1,0:T(8,128)(2,1)S(1)} %copy-done.10), channel_id=1, source_target_pairs={{0,7},{1,0},{2,1},{3,2},{4,3},{5,4},{6,5},{7,6},{8,15},{9,8},{10,9... | collective-permute-start | bytes 786440 | tf_op jit(solution)/shard_map/ppermute | solution.py:438
  52.9 14.8 %collective-permute-done.refs_1_ = bf16[512,256]{1,0:T(8,128)(2,1)S(1)} collective-permute-done((bf16[512,256]{1,0:T(8,128)(2,1)S(1)}, bf16[512,256]{1,0:T(8,128)(2,1)S(1)}, u32[]{:S(2)}, u32[]{:S(2)}) %collective-permute-start) | collective-permute-done | bytes 262176 | tf_op jit(solution)/shard_map/ppermute | solution.py:438
  67.7 1.9 collective-permute-start.2
  69.7 5.1 %collective-permute-start.3 = (bf16[512,256]{1,0:T(8,128)(2,1)S(1)}, bf16[512,256]{1,0:T(8,128)(2,1)S(1)}, u32[]{:S(2)}, u32[]{:S(2)}) collective-permute-start(bf16[512,256]{1,0:T(8,128)(2,1)S(1)} %collective-permute-done.1.refs_2_), channel_id=1, source_target_pairs={{0,7},{1,0},{2,1},{3,2},{4,3},{5,4},{6,5},{7,6},{8,15},{9,8},{10,9... | collective-permute-start | bytes 786440 | tf_op jit(solution)/shard_map/ppermute | solution.py:438
  74.8 1.9 collective-permute-start.13
  76.8 1.4 collective-permute-done.2.refs_1_
  78.2 1.9 collective-permute-start.4
  80.1 5.1 %collective-permute-start.5 = (bf16[512,256]{1,0:T(8,128)(2,1)S(1)}, bf16[512,256]{1,0:T(8,128)(2,1)S(1)}, u32[]{:S(2)}, u32[]{:S(2)}) collective-permute-start(bf16[512,256]{1,0:T(8,128)(2,1)S(1)} %collective-permute-done.3.refs_2_), channel_id=1, source_target_pairs={{0,7},{1,0},{2,1},{3,2},{4,3},{5,4},{6,5},{7,6},{8,15},{9,8},{10,9... | collective-permute-start | bytes 786440 | tf_op jit(solution)/shard_map/ppermute | solution.py:438
  85.2 3.4 %collective-permute-done.4.refs_1_ = bf16[512,256]{1,0:T(8,128)(2,1)S(1)} collective-permute-done((bf16[512,256]{1,0:T(8,128)(2,1)S(1)}, bf16[512,256]{1,0:T(8,128)(2,1)S(1)}, u32[]{:S(2)}, u32[]{:S(2)}) %collective-permute-start.4) | collective-permute-done | bytes 262176 | tf_op jit(solution)/shard_map/ppermute | solution.py:438
  88.6 1.9 collective-permute-start.6
  90.6 5.1 %collective-permute-start.7 = (bf16[256,256]{1,0:T(8,128)(2,1)S(1)}, bf16[256,256]{1,0:T(8,128)(2,1)S(1)}, u32[]{:S(2)}, u32[]{:S(2)}) collective-permute-start(bf16[256,256]{1,0:T(8,128)(2,1)S(1)} %slice.26), channel_id=1, source_target_pairs={{0,7},{1,0},{2,1},{3,2},{4,3},{5,4},{6,5},{7,6},{8,15},{9,8},{10,9... | collective-permute-start | bytes 393224 | tf_op jit(solution)/shard_map/ppermute | solution.py:442
  95.7 0.9 copy-done.12
  96.7 0.9 copy-done.14
  98.3 2.3 %shard_map.174 = f32[2,144,512]{2,1,0:T(8,128)} custom-call(bf16[512,2048]{1,0:T(8,128)(2,1)S(1)} %place_blocks.7.hz_ref, bf16[8,144,256]{2,1,0:T(8,128)(2,1)S(1)} %all-to-all-done.1.wo_ref, bf16[8,144,256]{2,1,0:T(8,128)(2,1)S(1)} %collective-permute-done.13.wx_ref), custom_call_target="tpu_custom_call" | custom-call | flops 603979776 | bytes 4194304 | tf_op jit(solution)/shard_map/pallas_call | solution.py:38
  100.6 7.2 %all-to-all-start.2 = ((f32[4,72,512]{2,1,0:T(8,128)}), f32[4,72,512]{2,1,0:T(8,128)S(1)}, u32[]{:S(2)}, u32[]{:S(2)}) async-start(f32[4,72,512]{2,1,0:T(8,128)} %bitcast.13), calls=%async_computation.2 | async-start | bytes 1179648 | tf_op jit(solution)/shard_map/all_to_all | solution.py:472
  107.8 1.6 slice.32
  110.3 2.1 shard_map.175.tails_ref
  112.4 10.2 %all-to-all-done.2.part_ref = f32[4,72,512]{2,1,0:T(8,128)S(1)} async-done(((f32[4,72,512]{2,1,0:T(8,128)}), f32[4,72,512]{2,1,0:T(8,128)S(1)}, u32[]{:S(2)}, u32[]{:S(2)}) %all-to-all-start.2) | async-done | bytes 589856 | tf_op jit(solution)/shard_map/all_to_all | solution.py:472
  123.4 1.1 shard_map.176
  124.5 0.8 copy-done.3
  125.9 5.0 %all-to-all-start.3 = ((bf16[8,64,512]{2,1,0:T(8,128)(2,1)}), bf16[8,64,512]{2,1,0:T(8,128)(2,1)}, u32[]{:S(2)}, u32[]{:S(2)}) async-start(bf16[8,64,512]{2,1,0:T(8,128)(2,1)} %copy-done.3), calls=%async_computation.3 | async-start | bytes 1048576 | tf_op jit(solution)/shard_map/all_to_all | solution.py:482
  130.9 1.1 shard_map.172
  132.0 1.2 copy-done
  133.1 13.6 %all-to-all-done.3.bc_ref = bf16[8,64,512]{2,1,0:T(8,128)(2,1)} async-done(((bf16[8,64,512]{2,1,0:T(8,128)(2,1)}), bf16[8,64,512]{2,1,0:T(8,128)(2,1)}, u32[]{:S(2)}, u32[]{:S(2)}) %all-to-all-start.3) | async-done | bytes 524320 | tf_op jit(solution)/shard_map/all_to_all | solution.py:482
  146.7 4.5 %all-to-all-start = ((bf16[16,192,256]{2,1,0:T(8,128)(2,1)}), bf16[16,192,256]{2,1,0:T(8,128)(2,1)}, u32[]{:S(2)}, u32[]{:S(2)}) async-start(bf16[16,192,256]{2,1,0:T(8,128)(2,1)} %copy-done), calls=%async_computation | async-start | bytes 3145728 | tf_op jit(solution)/shard_map/all_to_all | solution.py:456
  151.3 2.0 shard_map.169
  153.3 5.3 %collective-permute-start.9 = (bf16[256,256]{1,0:T(8,128)(2,1)S(1)}, bf16[256,256]{1,0:T(8,128)(2,1)S(1)}, u32[]{:S(2)}, u32[]{:S(2)}) collective-permute-start(bf16[256,256]{1,0:T(8,128)(2,1)S(1)} %get-tuple-element.14), channel_id=1, source_target_pairs={{0,8},{8,16},{16,24},{24,0},{1,9},{9,17},{17,25},{25,1},{2,10},{10... | collective-permute-start | bytes 393224 | tf_op jit(solution)/shard_map/ppermute | solution.py:488
  158.6 2.6 %collective-permute-start.11 = (bf16[256,256]{1,0:T(8,128)(2,1)S(1)}, bf16[256,256]{1,0:T(8,128)(2,1)S(1)}, u32[]{:S(2)}, u32[]{:S(2)}) collective-permute-start(bf16[256,256]{1,0:T(8,128)(2,1)S(1)} %get-tuple-element.15), channel_id=1, source_target_pairs={{0,24},{8,0},{16,8},{24,16},{1,25},{9,1},{17,9},{25,17},{2,26},{10... | collective-permute-start | bytes 393224 | tf_op jit(solution)/shard_map/ppermute | solution.py:489
  161.2 21.0 %collective-permute-done.9.add_ref = bf16[256,256]{1,0:T(8,128)(2,1)S(1)} collective-permute-done((bf16[256,256]{1,0:T(8,128)(2,1)S(1)}, bf16[256,256]{1,0:T(8,128)(2,1)S(1)}, u32[]{:S(2)}, u32[]{:S(2)}) %collective-permute-start.9) | collective-permute-done | bytes 131104 | tf_op jit(solution)/shard_map/ppermute | solution.py:488
  182.2 2.0 shard_map.170
  184.2 3.4 %collective-permute-start.10 = (bf16[512,256]{1,0:T(8,128)(2,1)S(1)}, bf16[512,256]{1,0:T(8,128)(2,1)}, u32[]{:S(2)}, u32[]{:S(2)}) collective-permute-start(bf16[512,256]{1,0:T(8,128)(2,1)S(1)} %shard_map.170), channel_id=1, source_target_pairs={{0,8},{8,16},{16,24},{24,0},{1,9},{9,17},{17,25},{25,1},{2,10},{10... | collective-permute-start | bytes 786440 | tf_op jit(solution)/shard_map/ppermute | solution.py:495
  187.6 2.7 %shard_map.171 = bf16[512,256]{1,0:T(8,128)(2,1)} custom-call(s32[1]{0:T(128)} %bitcast.2.index_ref, bf16[512,2048]{1,0:T(8,128)(2,1)S(1)} %place_blocks.7.hz_ref, bf16[4,4,576,256]{3,2,1,0:T(8,128)(2,1)} %bitcast.35, bf16[256,256]{1,0:T(8,128)(2,1)S(1)} %collective-permute-done.11.add_ref), custom_call_target="tpu_custom_call" | custom-call | flops 536870912 | bytes 3145728 | tf_op jit(solution)/shard_map/pallas_call | solution.py:265
  190.2 4.6 %collective-permute-start.12 = (bf16[512,256]{1,0:T(8,128)(2,1)}, bf16[512,256]{1,0:T(8,128)(2,1)}, u32[]{:S(2)}, u32[]{:S(2)}) collective-permute-start(bf16[512,256]{1,0:T(8,128)(2,1)} %shard_map.171), channel_id=1, source_target_pairs={{0,24},{8,0},{16,8},{24,16},{1,25},{9,1},{17,9},{25,17},{2,26},{10... | collective-permute-start | bytes 786440 | tf_op jit(solution)/shard_map/ppermute | solution.py:500
  194.9 2.1 shard_map.173.served_ref
  197.0 2.0 shard_map.168.x0
  199.1 3.2 %shard_map.177 = (bf16[4,512,512]{2,1,0:T(8,128)(2,1)S(1)}, bf16[512,256]{1,0:T(8,128)(2,1)S(1)}, f32[512,128]{1,0:T(8,128)S(1)}, f32[4,8,128]{2,1,0:T(8,128)S(1...) custom-call(s32[4,16]{1,0:T(4,128)S(1)} %bitcast.25, f32[4]{0:T(128)S(1)} %copy-done.31, f32[4]{0:T(128)S(1)} %copy-done.32, ...), custom_call_target="tpu_custom_call" | custom-call | flops 536870912 | bytes 12582912 | tf_op jit(solution)/shard_map/pallas_call | solution.py:38
  205.1 0.9 copy-done.5
  206.0 0.9 copy-done.7
  207.0 0.9 copy-done.9
  210.0 4.9 %shard_map.178 = (bf16[512,256]{1,0:T(8,128)(2,1)}, f32[4,256,256]{2,1,0:T(8,128)}) custom-call(s32[4,16]{1,0:T(4,128)S(1)} %bitcast.26, s32[4,16]{1,0:T(4,128)S(1)} %bitcast.22, s32[16]{0:T(128)S(1)} %copy-done.27, f32[4]{0:T(128)S(1)} %copy-done.28, f32[512,256]{1,0:T(8,128)S(1)} %shard_map.168.x0, bf16[512,256]{1,0:T(8,128)(2,1)} %collective-permute-done.10.x1, ...), custom_call_target="tpu_custom_call" | custom-call | flops 1342177280 | bytes 6291456 | tf_op jit(solution)/shard_map/pallas_call | solution.py:38
  (86 shorter events, 8.6 us)
Async XLA Ops:
  7.2 103.1 %all-gather.6.cloned.1.call-start = ((), (), s32[]{:S(2)}) async-start(), calls=%async_computation.5 | async-start | bytes 5013504 | tf_op jit(solution)/shard_map/all_gather | solution.py:429
  7.2 23.2 %collective-permute-start.8 = (bf16[512,256]{1,0:T(8,128)(2,1)}, bf16[512,256]{1,0:T(8,128)(2,1)S(1)}, u32[]{:S(2)}, u32[]{:S(2)}) collective-permute-start(bf16[512,256]{1,0:T(8,128)(2,1)} %param.17), channel_id=1, source_target_pairs={{0,0},{8,128},{16,256},{24,384},{128,8},{136,136},{144,264},{152,3... | collective-permute-start | bytes 786440 | tf_op jit(solution)/shard_map/ppermute | solution.py:421
  30.4 0.9 copy-start.17
  31.3 0.7 copy-start.22
  34.7 11.2 %copy-start.10 = (bf16[512,256]{1,0:T(8,128)(2,1)S(1)}, bf16[512,256]{1,0:T(8,128)(2,1)}, u32[]{:S(2)}) copy-start(bf16[512,256]{1,0:T(8,128)(2,1)} %refs_0_.1) | copy-start | bytes 786436
  35.5 39.3 %all-to-all-start.1 = ((bf16[8,144,256]{2,1,0:T(8,128)(2,1)}), bf16[8,144,256]{2,1,0:T(8,128)(2,1)S(1)}, u32[]{:S(2)}, u32[]{:S(2)}) async-start(bf16[8,144,256]{2,1,0:T(8,128)(2,1)} %bitcast.12), calls=%async_computation.1 | async-start | bytes 1179648 | tf_op jit(solution)/shard_map/all_to_all | solution.py:451
  45.8 21.9 %collective-permute-start = (bf16[512,256]{1,0:T(8,128)(2,1)S(1)}, bf16[512,256]{1,0:T(8,128)(2,1)S(1)}, u32[]{:S(2)}, u32[]{:S(2)}) collective-permute-start(bf16[512,256]{1,0:T(8,128)(2,1)S(1)} %copy-done.10), channel_id=1, source_target_pairs={{0,1},{1,2},{2,3},{3,4},{4,5},{5,6},{6,7},{7,0},{8,9},{9,10},{10,1... | collective-permute-start | bytes 786440 | tf_op jit(solution)/shard_map/ppermute | solution.py:438
  49.8 19.9 %collective-permute-start.1 = (bf16[512,256]{1,0:T(8,128)(2,1)S(1)}, bf16[512,256]{1,0:T(8,128)(2,1)S(1)}, u32[]{:S(2)}, u32[]{:S(2)}) collective-permute-start(bf16[512,256]{1,0:T(8,128)(2,1)S(1)} %copy-done.10), channel_id=1, source_target_pairs={{0,7},{1,0},{2,1},{3,2},{4,3},{5,4},{6,5},{7,6},{8,15},{9,8},{10,9... | collective-permute-start | bytes 786440 | tf_op jit(solution)/shard_map/ppermute | solution.py:438
  67.7 22.8 %copy-start.11 = (bf16[512,256]{1,0:T(8,128)(2,1)}, bf16[512,256]{1,0:T(8,128)(2,1)S(1)}, u32[]{:S(2)}) copy-start(bf16[512,256]{1,0:T(8,128)(2,1)S(1)} %collective-permute-done.refs_1_) | copy-start | bytes 786436
  67.7 10.4 %collective-permute-start.2 = (bf16[512,256]{1,0:T(8,128)(2,1)S(1)}, bf16[512,256]{1,0:T(8,128)(2,1)S(1)}, u32[]{:S(2)}, u32[]{:S(2)}) collective-permute-start(bf16[512,256]{1,0:T(8,128)(2,1)S(1)} %collective-permute-done.refs_1_), channel_id=1, source_target_pairs={{0,1},{1,2},{2,3},{3,4},{4,5},{5,6},{6,7},{7,0},{8,9},{9,10},{10,1... | collective-permute-start | bytes 786440 | tf_op jit(solution)/shard_map/ppermute | solution.py:438
  69.7 20.9 %copy-start.13 = (bf16[512,256]{1,0:T(8,128)(2,1)}, bf16[512,256]{1,0:T(8,128)(2,1)S(1)}, u32[]{:S(2)}) copy-start(bf16[512,256]{1,0:T(8,128)(2,1)S(1)} %collective-permute-done.1.refs_2_) | copy-start | bytes 786436
  69.7 10.4 %collective-permute-start.3 = (bf16[512,256]{1,0:T(8,128)(2,1)S(1)}, bf16[512,256]{1,0:T(8,128)(2,1)S(1)}, u32[]{:S(2)}, u32[]{:S(2)}) collective-permute-start(bf16[512,256]{1,0:T(8,128)(2,1)S(1)} %collective-permute-done.1.refs_2_), channel_id=1, source_target_pairs={{0,7},{1,0},{2,1},{3,2},{4,3},{5,4},{6,5},{7,6},{8,15},{9,8},{10,9... | collective-permute-start | bytes 786440 | tf_op jit(solution)/shard_map/ppermute | solution.py:438
  74.8 23.5 %collective-permute-start.13 = (bf16[8,144,256]{2,1,0:T(8,128)(2,1)S(1)}, bf16[8,144,256]{2,1,0:T(8,128)(2,1)S(1)}, u32[]{:S(2)}, u32[]{:S(2)}) collective-permute-start(bf16[8,144,256]{2,1,0:T(8,128)(2,1)S(1)} %all-to-all-done.1.wo_ref), channel_id=1, source_target_pairs={{0,32},{32,0},{1,33},{33,1},{2,34},{34,2},{3,35},{35,3},{4,36},{36... | collective-permute-start | bytes 1769480 | tf_op jit(solution)/shard_map/ppermute | solution.py:452
  78.2 10.4 %collective-permute-start.4 = (bf16[512,256]{1,0:T(8,128)(2,1)S(1)}, bf16[512,256]{1,0:T(8,128)(2,1)S(1)}, u32[]{:S(2)}, u32[]{:S(2)}) collective-permute-start(bf16[512,256]{1,0:T(8,128)(2,1)S(1)} %collective-permute-done.2.refs_1_), channel_id=1, source_target_pairs={{0,1},{1,2},{2,3},{3,4},{4,5},{5,6},{6,7},{7,0},{8,9},{9,10},{10,1... | collective-permute-start | bytes 786440 | tf_op jit(solution)/shard_map/ppermute | solution.py:438
  80.1 10.4 %collective-permute-start.5 = (bf16[512,256]{1,0:T(8,128)(2,1)S(1)}, bf16[512,256]{1,0:T(8,128)(2,1)S(1)}, u32[]{:S(2)}, u32[]{:S(2)}) collective-permute-start(bf16[512,256]{1,0:T(8,128)(2,1)S(1)} %collective-permute-done.3.refs_2_), channel_id=1, source_target_pairs={{0,7},{1,0},{2,1},{3,2},{4,3},{5,4},{6,5},{7,6},{8,15},{9,8},{10,9... | collective-permute-start | bytes 786440 | tf_op jit(solution)/shard_map/ppermute | solution.py:438
  88.6 9.4 %collective-permute-start.6 = (bf16[256,256]{1,0:T(8,128)(2,1)S(1)}, bf16[256,256]{1,0:T(8,128)(2,1)S(1)}, u32[]{:S(2)}, u32[]{:S(2)}) collective-permute-start(bf16[256,256]{1,0:T(8,128)(2,1)S(1)} %slice.25), channel_id=1, source_target_pairs={{0,1},{1,2},{2,3},{3,4},{4,5},{5,6},{6,7},{7,0},{8,9},{9,10},{10,1... | collective-permute-start | bytes 393224 | tf_op jit(solution)/shard_map/ppermute | solution.py:441
  90.6 7.6 %collective-permute-start.7 = (bf16[256,256]{1,0:T(8,128)(2,1)S(1)}, bf16[256,256]{1,0:T(8,128)(2,1)S(1)}, u32[]{:S(2)}, u32[]{:S(2)}) collective-permute-start(bf16[256,256]{1,0:T(8,128)(2,1)S(1)} %slice.26), channel_id=1, source_target_pairs={{0,7},{1,0},{2,1},{3,2},{4,3},{5,4},{6,5},{7,6},{8,15},{9,8},{10,9... | collective-permute-start | bytes 393224 | tf_op jit(solution)/shard_map/ppermute | solution.py:442
  95.7 1.0 copy-start.12
  96.7 0.9 copy-start.14
  100.6 8.9 %copy-start.19 = (s32[16,4]{0,1:T(4,128)S(1)}, s32[16,4]{0,1:T(4,128)}, u32[]{:S(2)}) copy-start(s32[16,4]{0,1:T(4,128)} %param.30) | copy-start | bytes 772
  100.6 22.0 %all-to-all-start.2 = ((f32[4,72,512]{2,1,0:T(8,128)}), f32[4,72,512]{2,1,0:T(8,128)S(1)}, u32[]{:S(2)}, u32[]{:S(2)}) async-start(f32[4,72,512]{2,1,0:T(8,128)} %bitcast.13), calls=%async_computation.2 | async-start | bytes 1179648 | tf_op jit(solution)/shard_map/all_to_all | solution.py:472
  107.8 87.0 %all-gather.4.cloned.1.call-start = ((), (), s32[]{:S(2)}) async-start(), calls=%async_computation.4 | async-start | bytes 2228224 | tf_op jit(solution)/shard_map/all_gather | solution.py:457
  110.3 12.4 %copy-start.18 = (f32[4,2048]{1,0:T(4,128)S(1)}, f32[4,2048]{1,0:T(4,128)}, u32[]{:S(2)}) copy-start(f32[4,2048]{1,0:T(4,128)} %taps_ref.3) | copy-start | bytes 98308
  110.3 12.4 %copy-start.23 = (s32[16,4]{0,1:T(4,128)S(1)}, s32[16,4]{0,1:T(4,128)}, u32[]{:S(2)}) copy-start(s32[16,4]{0,1:T(4,128)} %param.31) | copy-start | bytes 772
  110.3 12.4 %copy-start.24 = (f32[2048]{0:T(1024)S(1)}, f32[2048]{0:T(1024)}, u32[]{:S(2)}) copy-start(f32[2048]{0:T(1024)} %param.22) | copy-start | bytes 24580
  122.6 0.8 copy-start.15
  124.5 0.8 copy-start.3
  125.9 5.0 %copy-start.1 = (f32[4,4,64,256]{3,2,1,0:T(8,128)S(1)}, f32[4,4,64,256]{3,2,1,0:T(8,128)}, u32[]{:S(2)}) copy-start(f32[4,4,64,256]{3,2,1,0:T(8,128)} %param.26) | copy-start | bytes 3145732
  125.9 20.8 %all-to-all-start.3 = ((bf16[8,64,512]{2,1,0:T(8,128)(2,1)}), bf16[8,64,512]{2,1,0:T(8,128)(2,1)}, u32[]{:S(2)}, u32[]{:S(2)}) async-start(bf16[8,64,512]{2,1,0:T(8,128)(2,1)} %copy-done.3), calls=%async_computation.3 | async-start | bytes 1048576 | tf_op jit(solution)/shard_map/all_to_all | solution.py:482
  132.0 1.2 copy-start
  146.7 58.3 %all-to-all-start = ((bf16[16,192,256]{2,1,0:T(8,128)(2,1)}), bf16[16,192,256]{2,1,0:T(8,128)(2,1)}, u32[]{:S(2)}, u32[]{:S(2)}) async-start(bf16[16,192,256]{2,1,0:T(8,128)(2,1)} %copy-done), calls=%async_computation | async-start | bytes 3145728 | tf_op jit(solution)/shard_map/all_to_all | solution.py:456
  153.3 28.9 %collective-permute-start.9 = (bf16[256,256]{1,0:T(8,128)(2,1)S(1)}, bf16[256,256]{1,0:T(8,128)(2,1)S(1)}, u32[]{:S(2)}, u32[]{:S(2)}) collective-permute-start(bf16[256,256]{1,0:T(8,128)(2,1)S(1)} %get-tuple-element.14), channel_id=1, source_target_pairs={{0,8},{8,16},{16,24},{24,0},{1,9},{9,17},{17,25},{25,1},{2,10},{10... | collective-permute-start | bytes 393224 | tf_op jit(solution)/shard_map/ppermute | solution.py:488
  158.6 29.0 %collective-permute-start.11 = (bf16[256,256]{1,0:T(8,128)(2,1)S(1)}, bf16[256,256]{1,0:T(8,128)(2,1)S(1)}, u32[]{:S(2)}, u32[]{:S(2)}) collective-permute-start(bf16[256,256]{1,0:T(8,128)(2,1)S(1)} %get-tuple-element.15), channel_id=1, source_target_pairs={{0,24},{8,0},{16,8},{24,16},{1,25},{9,1},{17,9},{25,17},{2,26},{10... | collective-permute-start | bytes 393224 | tf_op jit(solution)/shard_map/ppermute | solution.py:489
  184.2 20.9 %collective-permute-start.10 = (bf16[512,256]{1,0:T(8,128)(2,1)S(1)}, bf16[512,256]{1,0:T(8,128)(2,1)}, u32[]{:S(2)}, u32[]{:S(2)}) collective-permute-start(bf16[512,256]{1,0:T(8,128)(2,1)S(1)} %shard_map.170), channel_id=1, source_target_pairs={{0,8},{8,16},{16,24},{24,0},{1,9},{9,17},{17,25},{25,1},{2,10},{10... | collective-permute-start | bytes 786440 | tf_op jit(solution)/shard_map/ppermute | solution.py:495
  190.2 14.8 %collective-permute-start.12 = (bf16[512,256]{1,0:T(8,128)(2,1)}, bf16[512,256]{1,0:T(8,128)(2,1)}, u32[]{:S(2)}, u32[]{:S(2)}) collective-permute-start(bf16[512,256]{1,0:T(8,128)(2,1)} %shard_map.171), channel_id=1, source_target_pairs={{0,24},{8,0},{16,8},{24,16},{1,25},{9,1},{17,9},{25,17},{2,26},{10... | collective-permute-start | bytes 786440 | tf_op jit(solution)/shard_map/ppermute | solution.py:500
  197.0 2.1 copy-start.16
  197.0 2.1 copy-start.25
  197.0 2.1 copy-start.30
  197.0 2.1 copy-start.31
  197.0 2.1 copy-start.32
  199.1 6.0 %copy-start.2 = (bf16[4,64,256]{2,1,0:T(8,128)(2,1)S(1)}, bf16[4,64,256]{2,1,0:T(8,128)(2,1)}, u32[]{:S(2)}) copy-start(bf16[4,64,256]{2,1,0:T(8,128)(2,1)} %shard_map.173.served_ref) | copy-start | bytes 393220
  199.1 6.0 %copy-start.26 = (f32[256]{0:T(256)S(1)}, f32[256]{0:T(256)}, u32[]{:S(2)}) copy-start(f32[256]{0:T(256)} %param.20) | copy-start | bytes 3076
  202.3 0.7 copy-start.4
  203.0 0.7 copy-start.6
  205.1 1.0 copy-start.5
  206.0 0.9 copy-start.7
  207.0 0.9 copy-start.9
  207.9 0.7 copy-start.21
  (5 other events, 3.2 us)
Sparse Core Ops, SparseCore 0:
  32.9 46.3 all-gather.5
  110.8 37.7 all-gather.3
